TPU v7x, 32 devices: a whole 2x2x4 slice. The times are simulated.
32 devices in a mesh: fsdp: 8 (over y, x, core), grp: 4 (over z).
Axes of the slice: x: 2, y: 2, z: 4, core: 2. Of those that a mesh axis runs over, the one named last changes fastest.
Arguments:
- tokens: bfloat16 [12288, 1536], P(('fsdp', 'grp')), may hold values from -6 to 6
- block_order: int32 [8, 4], P('fsdp'), may hold values from 0 to 3, each once within a row
- cont_lengths: int32 [8, 2, 4], P('fsdp'), may hold values from 1 to 192, 384 in all within a row
- gain_attn: float32 [1536], replicated, may hold values from 0.5 to 1.5
- w_qkv: bfloat16 [1536, 4608], P(('fsdp', 'grp')), may hold values from -0.15625 to 0.15625
- w_forget: bfloat16 [1536, 24], P(('fsdp', 'grp')), may hold values from -0.15625 to 0.15625
- b_forget: float32 [24], replicated, may hold values from 3 to 9
- w_out: bfloat16 [1536, 1536], P(('fsdp', 'grp')), may hold values from -0.625 to 0.625
- gain_ffn: float32 [1536], replicated, may hold values from 0.5 to 1.5
- w_gate_up: bfloat16 [1536, 8192], P(('fsdp', 'grp')), may hold values from -0.15625 to 0.15625
- w_down: bfloat16 [4096, 1536], P(('fsdp', 'grp')), may hold values from -0.09375 to 0.09375
- grad_out: bfloat16 [12288, 1536], P(('fsdp', 'grp')), may hold values from -6 to 6
Outputs:
- out: bfloat16 [12288, 1536], P(('fsdp', 'grp'))
- grad_tokens: bfloat16 [12288, 1536], P(('fsdp', 'grp'))
- grad_gain_attn: float32 [1536], replicated
- grad_w_qkv: float32 [1536, 4608], P(('fsdp', 'grp'))
- grad_w_forget: float32 [1536, 24], P(('fsdp', 'grp'))
- grad_b_forget: float32 [24], replicated
- grad_w_out: float32 [1536, 1536], P(('fsdp', 'grp'))
- grad_gain_ffn: float32 [1536], replicated
- grad_w_gate_up: float32 [1536, 8192], P(('fsdp', 'grp'))
- grad_w_down: float32 [4096, 1536], P(('fsdp', 'grp'))
Inputs may be any that keep to these rules, and one draw needn't show every extreme that they name: Each row of block_order is a permutation of 0 to 3. `cont_lengths`: each row of 4 lengths sums to 384, and its largest entry is 192.
All inputs are finite; a program needn't handle non-finite values.
Results may differ from a plain program's by a relative error of at most 0.015.
The roundings to bfloat16 on the way count: a program that leaves them out, or rounds other values in their place, can miss the bound.
Values may be sent and summed in bfloat16 or wider, within the bound.
A program may use at most 320 MiB of HBM per device.

v0:
```python
import jax
import jax.numpy as jnp
from jax import lax
from jax.sharding import PartitionSpec as P

EPSILON = 1e-05


def norm_rows(features):
    row_scale = lax.rsqrt(jnp.mean(features * features, axis=-1, keepdims=True) + EPSILON)
    return (features * row_scale, row_scale)


def norm_back(grad_normed, normed, row_scale):
    average_addend = jnp.mean(grad_normed * normed, axis=-1, keepdims=True)
    return row_scale * (grad_normed - normed * average_addend)


def contract_rows(first_op, second_op):
    return lax.dot_general(
        first_op, second_op, (((0,), (0,)), ((), ())), preferred_element_type=jnp.float32
    )


def contract_cols(first_op, second_op):
    return lax.dot_general(
        first_op, second_op, (((1,), (1,)), ((), ())), preferred_element_type=jnp.float32
    )


def on_device(
    tokens,
    block_order,
    cont_lengths,
    gain_attn,
    w_qkv,
    w_forget,
    b_forget,
    w_out,
    gain_ffn,
    w_gate_up,
    w_down,
    grad_out,
):
    tok_rows, model_width = tokens.shape
    head_count = w_forget.shape[1]
    head_size = model_width // head_count
    heads_each = 2
    group_count = head_count // heads_each
    score_scale = head_size ** (-0.5)
    block_count = lax.axis_size("grp")
    my_index = lax.axis_index("grp")
    slots = block_order[0]
    my_block = jnp.sum(
        jnp.arange(block_count, dtype=jnp.int32) * (slots == my_index).astype(jnp.int32)
    )
    is_prompt = my_block < 2
    cont_slot = jnp.maximum(my_block - 2, 0)
    lengths = lax.dynamic_index_in_dim(cont_lengths[0], cont_slot, 0, keepdims=False)
    seg_ends = jnp.cumsum(lengths)
    positions = jnp.arange(tok_rows, dtype=jnp.int32)
    segment = jnp.sum((positions[:, None] >= seg_ends[None, :]).astype(jnp.int32), axis=1)
    within = jnp.logical_and(
        segment[:, None] == segment[None, :], positions[None, :] <= positions[:, None]
    )
    summing = within.T.astype(jnp.float32)
    own_mask = jnp.logical_and(within, jnp.logical_not(is_prompt))
    prompt_pos = jnp.minimum(my_block, 1) * tok_rows + positions
    key_pos = jnp.arange(2 * tok_rows, dtype=jnp.int32)
    prompt_mask = jnp.logical_or(
        key_pos[None, :] <= prompt_pos[:, None], jnp.logical_not(is_prompt)
    )
    allowed = jnp.concatenate([prompt_mask, own_mask], axis=1)
    qkv_full, forget_full, out_full = (
        lax.all_gather(w_qkv, ("fsdp", "grp"), axis=0, tiled=True),
        lax.all_gather(w_forget, ("fsdp", "grp"), axis=0, tiled=True),
        lax.all_gather(w_out, ("fsdp", "grp"), axis=0, tiled=True),
    )
    inputs = tokens.astype(jnp.float32)
    normed_one, scale_one = norm_rows(inputs)
    acts = (normed_one * gain_attn).astype(jnp.bfloat16)
    mixed = jnp.dot(acts, qkv_full, preferred_element_type=jnp.float32)
    logits = jnp.dot(acts, forget_full, preferred_element_type=jnp.float32) + b_forget
    log_keep = jax.nn.log_sigmoid(logits)
    queries = mixed[:, :model_width].astype(jnp.bfloat16)
    keys = mixed[:, model_width : 2 * model_width].astype(jnp.bfloat16)
    values = mixed[:, 2 * model_width :].astype(jnp.bfloat16)
    keys_all, values_all = (
        lax.all_gather(keys, "grp", axis=0, tiled=True),
        lax.all_gather(values, "grp", axis=0, tiled=True),
    )
    logs_all = lax.all_gather(log_keep.T, "grp", axis=1, tiled=True)

    def decay_fn(logs_whole):
        first_block = lax.dynamic_slice_in_dim(logs_whole, slots[0] * tok_rows, tok_rows, 1)
        second_block = lax.dynamic_slice_in_dim(logs_whole, slots[1] * tok_rows, tok_rows, 1)
        prompt_cum = jnp.cumsum(jnp.concatenate([first_block, second_block], axis=1), axis=1)
        mine = lax.dynamic_slice_in_dim(logs_whole, my_index * tok_rows, tok_rows, 1)
        local_cum = jnp.dot(mine, summing, precision=lax.Precision.HIGHEST)
        as_prompt = lax.dynamic_slice_in_dim(
            prompt_cum, jnp.minimum(my_block, 1) * tok_rows, tok_rows, 1
        )
        as_cont = prompt_cum[:, -1:] + local_cum
        return (jnp.where(is_prompt, as_prompt, as_cont), prompt_cum, local_cum)

    (query_cum, prompt_cum, local_cum), decay_back = jax.vjp(decay_fn, logs_all)

    def prompt_rows(whole):
        return jnp.concatenate(
            [
                lax.dynamic_slice_in_dim(whole, slots[0] * tok_rows, tok_rows, 0),
                lax.dynamic_slice_in_dim(whole, slots[1] * tok_rows, tok_rows, 0),
            ],
            axis=0,
        )

    key_set = jnp.concatenate([prompt_rows(keys_all), keys], axis=0)
    value_set = jnp.concatenate([prompt_rows(values_all), values], axis=0)
    key_cum = jnp.concatenate([prompt_cum, local_cum], axis=1)

    def split_heads(matrix):
        return matrix.reshape(matrix.shape[0], group_count, heads_each, head_size).transpose(
            1, 0, 2, 3
        )

    def divided_running_total(cumul):
        return cumul.reshape(group_count, heads_each, cumul.shape[1])

    def combine_head_outputs(stacked):
        return stacked.transpose(1, 0, 2, 3).reshape(stacked.shape[1], model_width)

    def scores_of(query_part, key_part, query_decay, key_decay):
        raw_scores = (
            jnp.einsum("qhd,khd->hqk", query_part, key_part, preferred_element_type=jnp.float32)
            * score_scale
        )
        scores = raw_scores + query_decay[:, :, None] - key_decay[:, None, :]
        return jnp.where(allowed[None], scores, -jnp.inf)

    def attend_block(pieces):
        query_part, key_part, value_part, query_decay, key_decay = pieces
        scores = scores_of(query_part, key_part, query_decay, key_decay)
        row_top = jnp.max(scores, axis=-1, keepdims=True)
        shifted = jnp.exp(scores - row_top)
        row_total = jnp.sum(shifted, axis=-1, keepdims=True)
        weights = (shifted / row_total).astype(jnp.bfloat16)
        mixed_part = jnp.einsum(
            "hqk,khd->qhd", weights, value_part, preferred_element_type=jnp.float32
        )
        return (mixed_part, (row_top + jnp.log(row_total))[..., 0])

    head_inputs = (
        split_heads(queries),
        split_heads(key_set),
        split_heads(value_set),
        divided_running_total(query_cum),
        divided_running_total(key_cum),
    )
    head_out, log_totals = lax.map(attend_block, head_inputs)
    attn_o = combine_head_outputs(head_out).astype(jnp.bfloat16)
    attn_branch = jnp.dot(attn_o, out_full, preferred_element_type=jnp.float32)
    resid = inputs + attn_branch
    normed_two, scale_two = norm_rows(resid)
    acts_two = (normed_two * gain_ffn).astype(jnp.bfloat16)
    gate_up_full, down_full = (
        lax.all_gather(w_gate_up, ("fsdp", "grp"), axis=0, tiled=True),
        lax.all_gather(w_down, ("fsdp", "grp"), axis=0, tiled=True),
    )
    ffn_width = down_full.shape[0]
    both = jnp.dot(acts_two, gate_up_full, preferred_element_type=jnp.float32)
    gate = both[:, :ffn_width]
    up_part = both[:, ffn_width:]
    sigma = jax.nn.sigmoid(gate)
    swish = gate * sigma
    inner_act = (swish * up_part).astype(jnp.bfloat16)
    result = resid + jnp.dot(inner_act, down_full, preferred_element_type=jnp.float32)
    output = result.astype(jnp.bfloat16)
    gate_up_back, down_back = (
        lax.all_gather(w_gate_up, ("fsdp", "grp"), axis=0, tiled=True),
        lax.all_gather(w_down, ("fsdp", "grp"), axis=0, tiled=True),
    )
    qkv_back, forget_back, out_back = (
        lax.all_gather(w_qkv, ("fsdp", "grp"), axis=0, tiled=True),
        lax.all_gather(w_forget, ("fsdp", "grp"), axis=0, tiled=True),
        lax.all_gather(w_out, ("fsdp", "grp"), axis=0, tiled=True),
    )
    grad_down = contract_rows(inner_act, grad_out)
    grad_inner = contract_cols(grad_out, down_back)
    slope = sigma * (1.0 + gate * (1.0 - sigma))
    grad_both = jnp.concatenate([grad_inner * up_part * slope, grad_inner * swish], axis=1).astype(
        jnp.bfloat16
    )
    grad_gate_up = contract_rows(acts_two, grad_both)
    ffn_sums = (
        lax.psum_scatter(grad_gate_up, ("fsdp", "grp"), scatter_dimension=0, tiled=True),
        lax.psum_scatter(grad_down, ("fsdp", "grp"), scatter_dimension=0, tiled=True),
    )
    grad_acts_two = contract_cols(grad_both, gate_up_back)
    gain_two_grad = jnp.sum(grad_acts_two * normed_two, axis=0)
    grad_resid = grad_out.astype(jnp.float32) + norm_back(
        grad_acts_two * gain_ffn, normed_two, scale_two
    )
    grad_branch = grad_resid.astype(jnp.bfloat16)
    grad_out_w = contract_rows(attn_o, grad_branch)
    grad_heads = contract_cols(grad_branch, out_back).astype(jnp.bfloat16)

    def attention_backward_pass(pieces):
        query_part, key_part, value_part, query_decay, key_decay, log_part, grad_part = pieces
        scores = scores_of(query_part, key_part, query_decay, key_decay)
        weights = jnp.exp(scores - log_part[..., None])
        grad_weights = jnp.einsum(
            "qhd,khd->hqk", grad_part, value_part, preferred_element_type=jnp.float32
        )
        row_delta = jnp.sum(weights * grad_weights, axis=-1, keepdims=True)
        grad_scores = weights * (grad_weights - row_delta)
        low_scores = grad_scores.astype(jnp.bfloat16)
        grad_query = (
            jnp.einsum("hqk,khd->qhd", low_scores, key_part, preferred_element_type=jnp.float32)
            * score_scale
        )
        grad_key = (
            jnp.einsum("hqk,qhd->khd", low_scores, query_part, preferred_element_type=jnp.float32)
            * score_scale
        )
        grad_value = jnp.einsum(
            "hqk,qhd->khd",
            weights.astype(jnp.bfloat16),
            grad_part,
            preferred_element_type=jnp.float32,
        )
        return (
            grad_query,
            grad_key,
            grad_value,
            jnp.sum(grad_scores, axis=-1),
            -jnp.sum(grad_scores, axis=1),
        )

    back_inputs = head_inputs + (log_totals, split_heads(grad_heads))
    grad_qh, grad_kh, value_heads_gradient, grad_qc, grad_kc = lax.map(
        attention_backward_pass, back_inputs
    )
    grad_q = combine_head_outputs(grad_qh)
    grad_kset = combine_head_outputs(grad_kh)
    value_group_gradient = combine_head_outputs(value_heads_gradient)
    grad_query_cum = grad_qc.reshape(head_count, tok_rows)
    grad_key_cum = grad_kc.reshape(head_count, 3 * tok_rows)
    (grad_logs,) = decay_back(
        (grad_query_cum, grad_key_cum[:, : 2 * tok_rows], grad_key_cum[:, 2 * tok_rows :])
    )

    def broadcast_across_rows(part):
        whole = jnp.zeros((block_count * tok_rows, model_width), jnp.float32)
        for slot_number, slot_place in ((0, slots[0]), (1, slots[1]), (2, my_index)):
            addend = part[slot_number * tok_rows : (slot_number + 1) * tok_rows]
            current = lax.dynamic_slice_in_dim(whole, slot_place * tok_rows, tok_rows, 0)
            whole = lax.dynamic_update_slice_in_dim(
                whole, current + addend, slot_place * tok_rows, 0
            )
        return whole

    key_grad, value_grad, log_grad = (
        lax.psum_scatter(
            broadcast_across_rows(grad_kset).astype(jnp.bfloat16),
            "grp",
            scatter_dimension=0,
            tiled=True,
        ).astype(jnp.float32),
        lax.psum_scatter(
            broadcast_across_rows(value_group_gradient).astype(jnp.bfloat16),
            "grp",
            scatter_dimension=0,
            tiled=True,
        ).astype(jnp.float32),
        lax.psum_scatter(
            grad_logs.astype(jnp.bfloat16), "grp", scatter_dimension=1, tiled=True
        ).astype(jnp.float32),
    )
    grad_logits = (log_grad.T * jax.nn.sigmoid(-logits)).astype(jnp.bfloat16)
    grad_mixed = jnp.concatenate(
        [
            grad_q.astype(jnp.bfloat16),
            key_grad.astype(jnp.bfloat16),
            value_grad.astype(jnp.bfloat16),
        ],
        axis=1,
    )
    grad_qkv = contract_rows(acts, grad_mixed)
    grad_forget = contract_rows(acts, grad_logits)
    attn_sums = (
        lax.psum_scatter(grad_qkv, ("fsdp", "grp"), scatter_dimension=0, tiled=True),
        lax.psum_scatter(grad_forget, ("fsdp", "grp"), scatter_dimension=0, tiled=True),
        lax.psum_scatter(grad_out_w, ("fsdp", "grp"), scatter_dimension=0, tiled=True),
    )
    grad_acts = contract_cols(grad_mixed, qkv_back) + contract_cols(grad_logits, forget_back)
    gain_one_grad = jnp.sum(grad_acts * normed_one, axis=0)
    bias_grad = jnp.sum(grad_logits.astype(jnp.float32), axis=0)
    grad_inputs = grad_resid + norm_back(grad_acts * gain_attn, normed_one, scale_one)
    small_sums = lax.psum((gain_one_grad, gain_two_grad, bias_grad), ("fsdp", "grp"))
    return (
        output,
        grad_inputs.astype(jnp.bfloat16),
        small_sums[0],
        attn_sums[0],
        attn_sums[1],
        small_sums[2],
        attn_sums[2],
        small_sums[1],
        ffn_sums[0],
        ffn_sums[1],
    )


def solution(mesh):
    in_specs = (
        P(("fsdp", "grp"), None),
        P("fsdp", None),
        P("fsdp", None, None),
        P(),
        P(("fsdp", "grp"), None),
        P(("fsdp", "grp"), None),
        P(),
        P(("fsdp", "grp"), None),
        P(),
        P(("fsdp", "grp"), None),
        P(("fsdp", "grp"), None),
        P(("fsdp", "grp"), None),
    )
    out_specs = (
        P(("fsdp", "grp"), None),
        P(("fsdp", "grp"), None),
        P(),
        P(("fsdp", "grp"), None),
        P(("fsdp", "grp"), None),
        P(),
        P(("fsdp", "grp"), None),
        P(),
        P(("fsdp", "grp"), None),
        P(("fsdp", "grp"), None),
    )
    return jax.shard_map(
        on_device, mesh=mesh, in_specs=in_specs, out_specs=out_specs, check_vma=False
    )
```

profile of v0, /device:TPU:8, one launch (start us, length us, event | category | flops | bytes accessed | tf_op | source)
XLA Modules:
  0.0 2264.9 jit_solution(15640041494288199046)
XLA Ops:
  9.6 104.8 %all-gather.8.cloned.1.call-done = bf16[1536,4608]{1,0:T(8,128)(2,1)} async-done(((bf16[48,4608]{1,0:T(8,128)(2,1)}), bf16[1536,4608]{1,0:T(8,128)(2,1)}) %all-gather.8.cloned.1.call-update) | async-done | bytes 14155792 | tf_op jit(solution)/shard_map/all_gather | solution.py:75
  114.4 11.4 convolution_convert_fusion
  133.2 69.5 %all-gather = bf16[32,48,24]{1,2,0:T(8,128)(2,1)S(1)} all-gather(bf16[1,48,24]{1,2,0:T(8,128)(2,1)S(1)} %bitcast.246), channel_id=1, replica_groups=mesh['fsdp'=8,'grp'=4] {'fsdp','grp'}, dimensions={0}, use_global_device_ids=true | all-gather | bytes 76032 | tf_op jit(solution)/shard_map/all_gather | solution.py:76
  204.1 14.9 all_gather.33
  226.9 82.3 %all-gather.10.cloned.1.call-done = bf16[1536,1536]{1,0:T(8,128)(2,1)} async-done(((bf16[384,1536]{1,0:T(8,128)(2,1)}), bf16[1536,1536]{1,0:T(8,128)(2,1)}) %all-gather.10.cloned.1.call-update) | async-done | bytes 4718608 | tf_op jit(solution)/shard_map/all_gather | solution.py:90
  314.9 5.9 copy.66
  323.8 5.8 copy.68
  329.9 75.8 %while.30 = (s32[]{:T(128)}, bf16[12,384,2,64]{1,3,2,0:T(8,128)(2,1)S(1)}, f32[12,2,384]{2,1,0:T(2,128)S(1)}, bf16[12,1152,2,64]{1,3,2,0:T(8,128)(2,1)}, pred[38...) while((s32[]{:T(128)}, ...), condition=%wide.region_9.10_spmd, body=%wide.region_6.9_spmd.sunk | while | flops 235339008 | bytes 12007545 | solution.py:159
  411.7 119.4 %all-gather.16.cloned.1.call-done = bf16[1536,8192]{1,0:T(8,128)(2,1)} async-done(((bf16[48,8192]{1,0:T(8,128)(2,1)}), bf16[1536,8192]{1,0:T(8,128)(2,1)}) %all-gather.16.cloned.1.call-update) | async-done | bytes 25165840 | tf_op jit(solution)/shard_map/all_gather | solution.py:166
  531.1 17.6 fusion.97
  548.6 80.6 %all-gather.18.cloned.1.call-done = bf16[4096,1536]{1,0:T(8,128)(2,1)} async-done(((bf16[128,1536]{1,0:T(8,128)(2,1)}), bf16[4096,1536]{1,0:T(8,128)(2,1)}) %all-gather.18.cloned.1.call-update) | async-done | bytes 12582928 | tf_op jit(solution)/shard_map/all_gather | solution.py:167
  629.2 20.7 multiply_convert_fusion.1
  649.9 17.4 multiply_reduce_fusion.1
  677.6 165.1 %while.31 = (s32[]{:T(128)}, bf16[12,384,2,64]{1,3,2,0:T(8,128)(2,1)S(1)}, f32[12,1152,2,64]{1,3,2,0:T(8,128)}, f32[12,1152,2,64]{1,3,2,0:T(8,128)}, f32[12,2,38...) while((s32[]{:T(128)}, ...), condition=%wide.region_16.17_spmd, body=%wide.region_12.16_spmd.sunk | while | flops 577927680 | bytes 31502528 | solution.py:240
  842.7 6.7 fusion.108
  850.7 7.5 reduce-window.31
  868.1 6.6 copy.79
  884.1 6.7 copy.77
  896.2 8.2 fusion.69
  904.5 13.6 fusion.111
  918.2 47.2 %reduce-scatter.27.cloned.1.call-done = bf16[384,1536]{1,0:T(8,128)(2,1)} async-done(((bf16[1536,1536]{1,0:T(8,128)(2,1)}), bf16[384,1536]{1,0:T(8,128)(2,1)}) %reduce-scatter.27.cloned.1.call-update) | async-done | bytes 1179664
  967.7 85.8 %reduce-scatter.25.cloned.1.call-done = bf16[384,1536]{1,0:T(8,128)(2,1)} async-done(((bf16[1536,1536]{1,0:T(8,128)(2,1)}), bf16[384,1536]{1,0:T(8,128)(2,1)}) %reduce-scatter.25.cloned.1.call-update) | async-done | bytes 1179664
  1055.9 15.4 fusion.66
  1071.6 23.8 %fusion.51 = f32[1536,8192]{1,0:T(8,128)} fusion(bf16[384,4096]{1,0:T(8,128)(2,1)} %get-tuple-element.208, bf16[384,4096]{1,0:T(8,128)(2,1)} %get-tuple-element.207, f32[384,1536]{1,0:T(8,128)S(1)} %get-tuple-element.233, f32[1536]{0:T(1024)} %param.24, f32[384]{0:T(512)S(1)} %add_rsqrt_fusion), kind=kOutput, calls=%fused_computation.74 | convolution fusion | flops 9678028800 | bytes 58990080 | tf_op jit(solution)/shard_map/dot_general | solution.py:20
  1095.5 11.2 fusion.57
  1106.7 48.5 %reduce-scatter.31.cloned.1.call-done = f32[48,24]{1,0:T(8,128)} async-done(((f32[1536,24]{1,0:T(8,128)}), f32[48,24]{1,0:T(8,128)}) %reduce-scatter.31.cloned.1.call-update) | async-done | bytes 4624
  1156.7 9.9 fusion.67
  1169.5 39.8 %all-reduce.1 = (f32[1536]{0:T(1024)}, f32[24]{0:T(128)}, f32[1536]{0:T(1024)}) all-reduce(f32[1536]{0:T(1024)} %get-tuple-element.145, f32[24]{0:T(128)} %get-tuple-element.197, f32[1536]{0:T(1024)} %get-tuple-element.143), channel_id=1, replica_groups=mesh['fsdp'=8,'grp'=4] {'fsdp','grp'}, use_global_device_ids=true, to_apply=%region_25.26 | all-reduce | flops 3096 | bytes 24768 | tf_op jit(solution)/shard_map/psum | solution.py:299
  1212.7 84.0 %reduce-scatter.19.cloned.1.call-done = f32[48,1536]{1,0:T(8,128)} async-done(((f32[1536,1536]{1,0:T(8,128)}), f32[48,1536]{1,0:T(8,128)}) %reduce-scatter.19.cloned.1.call-update) | async-done | bytes 294928 | tf_op jit(solution)/shard_map/reduce_scatter | solution.py:293
  1296.7 252.2 %reduce-scatter.23.cloned.1.call-done = f32[128,1536]{1,0:T(8,128)} async-done(((f32[4096,1536]{1,0:T(8,128)}), f32[128,1536]{1,0:T(8,128)}) %reduce-scatter.23.cloned.1.call-update) | async-done | bytes 786448 | tf_op jit(solution)/shard_map/reduce_scatter | solution.py:196
  1548.9 271.5 %reduce-scatter.17.cloned.1.call-done = f32[48,4608]{1,0:T(8,128)} async-done(((f32[1536,4608]{1,0:T(8,128)}), f32[48,4608]{1,0:T(8,128)}) %reduce-scatter.17.cloned.1.call-update) | async-done | bytes 884752 | tf_op jit(solution)/shard_map/reduce_scatter | solution.py:291
  1820.4 437.8 %reduce-scatter.21.cloned.1.call-done = f32[48,8192]{1,0:T(8,128)} async-done(((f32[1536,8192]{1,0:T(8,128)}), f32[48,8192]{1,0:T(8,128)}) %reduce-scatter.21.cloned.1.call-update) | async-done | bytes 1572880 | tf_op jit(solution)/shard_map/reduce_scatter | solution.py:195
  (396 shorter events, 319.4 us)
Async XLA Ops:
  7.2 214.6 %copy-start = (s32[1,2,4]{2,1,0:T(2,128)S(1)}, s32[1,2,4]{2,1,0:T(2,128)}, u32[]{:S(2)}) copy-start(s32[1,2,4]{2,1,0:T(2,128)} %param.18) | copy-start | bytes 100
  7.2 107.2 %all-gather.8.cloned.1.call-start = ((), (), s32[]{:S(2)}) async-start(), calls=%async_computation.8 | async-start | bytes 14598144 | tf_op jit(solution)/shard_map/all_gather | solution.py:75
  7.9 218.9 %all-gather.12.cloned.1.call-start = ((), (), s32[]{:S(2)}) async-start(), calls=%async_computation.10 | async-start | bytes 5898240 | tf_op jit(solution)/shard_map/all_gather | solution.py:89
  9.6 193.4 %copy-start.22 = (f32[384]{0:T(512)}, f32[384]{0:T(512)S(1)}, u32[]{:S(2)}) copy-start(f32[384]{0:T(512)S(1)} %add_rsqrt_fusion.1) | copy-start | bytes 4612
  127.4 75.6 %copy-start.2 = (bf16[384,1536]{1,0:T(8,128)(2,1)S(1)}, bf16[384,1536]{1,0:T(8,128)(2,1)}, u32[]{:S(2)}) copy-start(bf16[384,1536]{1,0:T(8,128)(2,1)} %param.16) | copy-start | bytes 3538948
  127.4 75.6 %copy-start.14 = (f32[1536]{0:T(1024)S(1)}, f32[1536]{0:T(1024)}, u32[]{:S(2)}) copy-start(f32[1536]{0:T(1024)} %param.19) | copy-start | bytes 18436
  127.4 75.6 %copy-start.32 = (f32[24]{0:T(128)S(1)}, f32[24]{0:T(128)}, u32[]{:S(2)}) copy-start(f32[24]{0:T(128)} %param.22) | copy-start | bytes 292
  127.4 181.7 %all-gather.10.cloned.1.call-start = ((), (), s32[]{:S(2)}) async-start(), calls=%async_computation.9 | async-start | bytes 5898240 | tf_op jit(solution)/shard_map/all_gather | solution.py:90
  128.2 277.6 %all-gather.14.cloned.1.call-start = ((), (), s32[]{:S(2)}) async-start(), calls=%async_computation.11 | async-start | bytes 4866048 | tf_op jit(solution)/shard_map/all_gather | solution.py:77
  128.8 402.3 %all-gather.16.cloned.1.call-start = ((), (), s32[]{:S(2)}) async-start(), calls=%async_computation.12 | async-start | bytes 25952256 | tf_op jit(solution)/shard_map/all_gather | solution.py:166
  129.3 499.9 %all-gather.18.cloned.1.call-start = ((), (), s32[]{:S(2)}) async-start(), calls=%async_computation.13 | async-start | bytes 12976128 | tf_op jit(solution)/shard_map/all_gather | solution.py:167
  129.9 761.0 %reduce-scatter.29.cloned.1.call-start = ((), (), s32[]{:S(2)}) async-start(), calls=%async_computation.20 | async-start | bytes 491520
  203.0 19.8 copy-start.19
  226.9 86.0 %copy-start.8 = (bf16[384,1536]{1,0:T(8,128)(2,1)S(1)}, bf16[384,1536]{1,0:T(8,128)(2,1)}, u32[]{:S(2)}) copy-start(bf16[384,1536]{1,0:T(8,128)(2,1)} %get-tuple-element.222) | copy-start | bytes 3538948
  314.9 5.9 copy-start.7
  323.8 6.0 copy-start.16
  406.7 124.3 %copy-start.18 = (f32[1536]{0:T(1024)S(1)}, f32[1536]{0:T(1024)}, u32[]{:S(2)}) copy-start(f32[1536]{0:T(1024)} %param.24) | copy-start | bytes 18436
  531.1 98.2 %copy-start.12 = (bf16[384,1536]{1,0:T(8,128)(2,1)S(1)}, bf16[384,1536]{1,0:T(8,128)(2,1)}, u32[]{:S(2)}) copy-start(bf16[384,1536]{1,0:T(8,128)(2,1)} %param.27) | copy-start | bytes 3538948
  842.7 6.7 copy-start.13
  842.7 6.7 copy-start.24
  842.7 15.7 copy-start.29
  859.8 105.5 %reduce-scatter.27.cloned.1.call-start = ((), (), s32[]{:S(2)}) async-start(), calls=%async_computation.19 | async-start | bytes 5898240
  874.8 178.8 %reduce-scatter.25.cloned.1.call-start = ((), (), s32[]{:S(2)}) async-start(), calls=%async_computation.18 | async-start | bytes 5898240
  890.9 264.4 %reduce-scatter.31.cloned.1.call-start = ((), (), s32[]{:S(2)}) async-start(), calls=%async_computation.21 | async-start | bytes 811008
  896.2 400.5 %reduce-scatter.19.cloned.1.call-start = ((), (), s32[]{:S(2)}) async-start(), calls=%async_computation.15 | async-start | bytes 9732096 | tf_op jit(solution)/shard_map/reduce_scatter | solution.py:293
  904.5 644.4 %reduce-scatter.23.cloned.1.call-start = ((), (), s32[]{:S(2)}) async-start(), calls=%async_computation.17 | async-start | bytes 25952256 | tf_op jit(solution)/shard_map/reduce_scatter | solution.py:196
  918.1 902.2 %reduce-scatter.17.cloned.1.call-start = ((), (), s32[]{:S(2)}) async-start(), calls=%async_computation.14 | async-start | bytes 29196288 | tf_op jit(solution)/shard_map/reduce_scatter | solution.py:291
  1071.4 1186.8 %reduce-scatter.21.cloned.1.call-start = ((), (), s32[]{:S(2)}) async-start(), calls=%async_computation.16 | async-start | bytes 51904512 | tf_op jit(solution)/shard_map/reduce_scatter | solution.py:195
  1156.7 10.0 copy-start.20
  1156.7 10.0 copy-start.27
  1166.6 42.7 %copy-start.5 = (f32[384,1536]{1,0:T(8,128)S(1)}, f32[384,1536]{1,0:T(8,128)}, u32[]{:S(2)}) copy-start(f32[384,1536]{1,0:T(8,128)} %copy-done.4) | copy-start | bytes 7077892
  1209.3 1048.8 %copy-start.1 = (s32[1,2,4]{2,1,0:T(2,128)S(1)}, s32[1,2,4]{2,1,0:T(2,128)}, u32[]{:S(2)}) copy-start(s32[1,2,4]{2,1,0:T(2,128)} %param.18) | copy-start | bytes 100
  (26 other events, 72.5 us)
Sparse Core Ops, SparseCore 0:
  10.8 103.4 all-gather.7
  127.6 91.6 all-gather.11
  221.4 87.7 all-gather.9
  311.8 65.1 all-gather.13
  379.8 151.2 all-gather.15
  533.8 95.4 all-gather.17
  859.9 16.3 reduce-scatter.28
  878.7 86.5 reduce-scatter.26
  967.7 85.7 reduce-scatter.24
  1059.3 95.9 reduce-scatter.30
  1162.7 133.9 reduce-scatter.18
  1303.6 245.2 reduce-scatter.22
  1557.0 263.2 reduce-scatter.16
  1828.4 429.7 reduce-scatter.20
where the time goes:
time: 2280 us; the launch traced here: 2260 us
  waiting for transfers between devices  1620 us (71%)
  matrix products  339 us (15%)
  blocking collectives  124 us (5%)
  local copies, waits for them, and re-layouts  106 us (5%)
  other arithmetic  59.2 us (3%)
    reduce_scatter x1, waiting for transfers between devices, on_device(): lax.psum_scatter(grad_gate_up, ('fsdp', 'grp'), scatter_dimension=0, tile...  438 us
    reduce_scatter x1, waiting for transfers between devices, on_device(): lax.psum_scatter(grad_qkv, ('fsdp', 'grp'), scatter_dimension=0, tiled=True)  271 us
    reduce_scatter x1, waiting for transfers between devices, on_device(): lax.psum_scatter(grad_down, ('fsdp', 'grp'), scatter_dimension=0, tiled=T...  252 us
    unnamed x18, waiting for transfers between devices  185 us
    all_gather x1, waiting for transfers between devices, on_device(): lax.all_gather(w_gate_up, ('fsdp', 'grp'), axis=0, tiled=True)  119 us
    all_gather x1, waiting for transfers between devices, on_device(): lax.all_gather(w_qkv, ('fsdp', 'grp'), axis=0, tiled=True)  105 us
    reduce_scatter x1, waiting for transfers between devices, on_device(): lax.psum_scatter(grad_out_w, ('fsdp', 'grp'), scatter_dimension=0, tiled=...  84 us
    all_gather x1, waiting for transfers between devices, on_device(): lax.all_gather(values, 'grp', axis=0, tiled=True)  82.3 us
  transfers between devices with their start and end apart: 14, of which 11 were waited for; matrix products, arithmetic and copies ran while one was open for 11% of the time, Pallas kernels for 0%

commit v1 on v0

v1 whole, which is shorter than its diff:
```python
import functools

import jax
import jax.numpy as jnp
from jax import lax
from jax.experimental import pallas as pl
from jax.experimental.pallas import tpu as pltpu
from jax.sharding import PartitionSpec as P

EPSILON = 1e-05
NEG = -1e30
HIGHEST = lax.Precision.HIGHEST
MESH = pl.DeviceIdType.MESH
F32 = jnp.float32
BF16 = jnp.bfloat16


def flip_bit(value, bit):
    return value + bit - 2 * bit * ((value // bit) % 2)


def flip(value, mask):
    bit = 1
    while bit <= mask:
        if mask & bit:
            value = flip_bit(value, bit)
        bit *= 2
    return value


def swap(value, axis, mask):
    return lax.ppermute(value, axis, [(i, i ^ mask) for i in range(lax.axis_size(axis))])


def gather_parts(shapes):
    return [(w, h) for w, s in enumerate(shapes) for h in (0, 1) if h == 0 or s[1] % 256 == 0]


def gather_kernel(shapes, n_fsdp, n_grp, *refs):
    count = len(shapes)
    ins, outs = refs[:count], refs[count : 2 * count]
    send_sem, recv_sem, local_sem = refs[2 * count :]
    f, z = lax.axis_index("fsdp"), lax.axis_index("grp")
    bits = [1 << i for i in range(1, n_fsdp.bit_length() - 1)]

    def peer(fk, zk):
        return {"fsdp": flip(f, fk), "grp": flip(z, zk)}

    barrier = pltpu.get_barrier_semaphore()
    peers = [(0, k) for k in range(1, n_grp)] + [(b, 0) for b in bits] + [(1, 0)]
    for fk, zk in peers:
        pl.semaphore_signal(barrier, inc=1, device_id=peer(fk, zk), device_id_type=MESH)
    pl.semaphore_wait(barrier, len(peers))

    parts = gather_parts(shapes)
    orders = [bits if h == 0 else bits[::-1] for _, h in parts]
    sends = []

    def half(w, h):
        width = shapes[w][1] // 2
        return pl.ds(0, shapes[w][1]) if width % 128 else pl.ds(h * width, width)

    def piece(w, h, fk, zk):
        return outs[w].at[flip(f, fk) * n_grp + flip(z, zk), :, half(w, h)]

    def send(p, fk, zk, to_f, to_z, own):
        w, h = parts[p]
        copy = pltpu.make_async_remote_copy(
            src_ref=ins[w].at[:, half(w, h)] if own else piece(w, h, fk, zk),
            dst_ref=piece(w, h, fk, zk),
            send_sem=send_sem.at[len(sends)],
            recv_sem=recv_sem.at[p, (fk ^ to_f) * n_grp + (zk ^ to_z)],
            device_id=peer(to_f, to_z),
            device_id_type=MESH,
        )
        copy.start()
        sends.append(copy)

    def arrived(p, fk, zk):
        view = piece(*parts[p], fk, zk)
        pltpu.make_async_remote_copy(
            src_ref=view,
            dst_ref=view,
            send_sem=send_sem.at[0],
            recv_sem=recv_sem.at[p, fk * n_grp + zk],
            device_id=peer(1, 0),
            device_id_type=MESH,
        ).wait_recv()

    def forward(p, stage, fk, zk, own=False):
        for bit in orders[p][stage:]:
            send(p, fk, zk, bit, 0, own)
        send(p, fk, zk, 1, 0, own)

    local = []
    for w in range(count):
        copy = pltpu.make_async_copy(ins[w], outs[w].at[f * n_grp + z], local_sem.at[w])
        copy.start()
        local.append(copy)
    for p in range(len(parts)):
        for k in range(1, n_grp):
            send(p, 0, 0, 0, k, True)
        forward(p, 0, 0, 0, True)
    for k in range(1, n_grp):
        for p in range(len(parts)):
            arrived(p, 0, k)
            forward(p, 0, 0, k)
    have = [[0] for _ in parts]
    for stage in range(len(bits)):
        for a in range(len(have[0])):
            for k in range(n_grp):
                for p in range(len(parts)):
                    fk = have[p][a] ^ orders[p][stage]
                    arrived(p, fk, k)
                    forward(p, stage + 1, fk, k)
        have = [known + [v ^ orders[p][stage] for v in known] for p, known in enumerate(have)]
    for a in range(len(have[0])):
        for k in range(n_grp):
            for p in range(len(parts)):
                arrived(p, have[p][a] ^ 1, k)
    for copy in local:
        copy.wait()
    for copy in sends:
        copy.wait_send()


def gather_rows(weights, collective_id):
    n_fsdp, n_grp = lax.axis_size("fsdp"), lax.axis_size("grp")
    shapes = [w.shape for w in weights]
    count = len(weights)
    per_part = (n_grp - 1) + n_grp * (n_fsdp // 2 - 1) + n_grp * (n_fsdp // 2)
    full = pl.pallas_call(
        functools.partial(gather_kernel, shapes, n_fsdp, n_grp),
        out_shape=[
            jax.ShapeDtypeStruct((n_fsdp * n_grp,) + w.shape, w.dtype) for w in weights
        ],
        in_specs=[pl.BlockSpec(memory_space=pl.ANY)] * count,
        out_specs=[pl.BlockSpec(memory_space=pl.ANY)] * count,
        scratch_shapes=[
            pltpu.SemaphoreType.DMA((per_part * len(gather_parts(shapes)),)),
            pltpu.SemaphoreType.DMA((len(gather_parts(shapes)), n_fsdp * n_grp)),
            pltpu.SemaphoreType.DMA((count,)),
        ],
        compiler_params=pltpu.CompilerParams(
            collective_id=collective_id, has_side_effects=True
        ),
        name="gather_rows",
    )(*weights)
    return [v.reshape(-1, v.shape[2]) for v in full]


def dot_lanes(a, b):
    return lax.dot_general(a, b, (((1,), (1,)), ((), ())), preferred_element_type=F32)


def dot_rows(a, b):
    return lax.dot_general(a, b, (((0,), (0,)), ((), ())), preferred_element_type=F32)


def seen_blocks(block):
    if block == 0:
        return [(0, 0)]
    if block == 1:
        return [(0, None), (1, 0)]
    return [(0, None), (1, None), (block, block - 1)]


def head_setup(c_ref, head_size):
    head = pl.program_id(1)
    lanes = lax.broadcasted_iota(jnp.int32, (1, 2 * head_size), 1)
    mine = lanes // head_size == head
    columns = lax.broadcasted_iota(jnp.int32, (1, c_ref.shape[3]), 1)

    def decay(block):
        return jnp.sum(
            jnp.where(columns == head, c_ref[0, block], 0.0), axis=1, keepdims=True
        )

    return mine, decay


def attend_kernel(blocks, head_size, rel_ref, x_ref, c_ref, mask_ref, o_ref, lse_ref):
    mine, decay = head_setup(c_ref, head_size)
    scale = head_size**-0.5
    decays = [decay(b) for b in range(blocks)]
    for block in range(blocks):
        place = rel_ref[block]
        query = jnp.where(mine, x_ref[place, 0] * scale, 0).astype(BF16)
        scores = []
        for other, mask in seen_blocks(block):
            s = dot_lanes(x_ref[rel_ref[other], 1], query) - decays[other]
            if mask is not None:
                s = s + mask_ref[mask]
            scores.append(s)
        top = functools.reduce(
            jnp.maximum, [jnp.max(s, axis=0, keepdims=True) for s in scores]
        )
        total, mixed = 0.0, 0.0
        for s, (other, _) in zip(scores, seen_blocks(block)):
            weight = jnp.exp(s - top)
            total = total + jnp.sum(weight, axis=0, keepdims=True)
            mixed = mixed + dot_rows(x_ref[rel_ref[other], 2], weight.astype(BF16))
        lse_ref[0, 0, pl.ds(block, 1), :] = top + jnp.log(total)
        result = (mixed / total).T.astype(BF16)
        o_ref[place] = jnp.where(mine, result, o_ref[place])


def attend_back_kernel(
    blocks, head_size, rel_ref, x_ref, do_ref, c_ref, mask_ref, lse_ref, dx_ref, dcq_ref, dck_ref
):
    mine, decay = head_setup(c_ref, head_size)
    scale = head_size**-0.5
    decays = [decay(b) for b in range(blocks)]
    key_grads, value_grads, decay_grads = [None] * blocks, [None] * blocks, [None] * blocks

    def add(store, index, value):
        store[index] = value if store[index] is None else store[index] + value

    def put(place, part, value):
        dx_ref[place, part] = jnp.where(mine, value.astype(BF16), dx_ref[place, part])

    for block in range(blocks):
        place = rel_ref[block]
        query = jnp.where(mine, x_ref[place, 0] * scale, 0).astype(BF16)
        grad_o = jnp.where(mine, do_ref[place], 0).astype(BF16)
        lse = lse_ref[0, 0, pl.ds(block, 1), :]
        weights, grads, delta = [], [], 0.0
        for other, mask in seen_blocks(block):
            s = dot_lanes(x_ref[rel_ref[other], 1], query) - decays[other]
            if mask is not None:
                s = s + mask_ref[mask]
            weight = jnp.exp(s - lse)
            grad = dot_lanes(x_ref[rel_ref[other], 2], grad_o)
            delta = delta + jnp.sum(weight * grad, axis=0, keepdims=True)
            weights.append(weight)
            grads.append(grad)
        query_grad, query_decay = 0.0, 0.0
        for weight, grad, (other, _) in zip(weights, grads, seen_blocks(block)):
            ds = weight * (grad - delta)
            query_decay = query_decay + jnp.sum(ds, axis=0, keepdims=True)
            add(decay_grads, other, jnp.sum(ds, axis=1, keepdims=True))
            low = ds.astype(BF16)
            query_grad = query_grad + dot_rows(x_ref[rel_ref[other], 1], low)
            add(key_grads, other, jnp.dot(low, query, preferred_element_type=F32))
            add(
                value_grads,
                other,
                jnp.dot(weight.astype(BF16), grad_o, preferred_element_type=F32),
            )
        put(place, 0, (query_grad * scale).T)
        dcq_ref[0, 0, pl.ds(block, 1), :] = query_decay
    columns = lax.broadcasted_iota(jnp.int32, (1, dck_ref.shape[3]), 1)
    for block in range(blocks):
        place = rel_ref[block]
        put(place, 1, key_grads[block])
        put(place, 2, value_grads[block])
        dck_ref[0, block] = jnp.where(
            columns == pl.program_id(1), decay_grads[block], dck_ref[0, block]
        )


def attention_specs(blocks, rows, pair_width):
    x_spec = pl.BlockSpec((blocks, 3, rows, pair_width), lambda p, h, rel: (0, 0, 0, p))
    o_spec = pl.BlockSpec((blocks, rows, pair_width), lambda p, h, rel: (0, 0, p))
    c_spec = pl.BlockSpec((1, blocks, rows, 8), lambda p, h, rel: (p, 0, 0, 0))
    m_spec = pl.BlockSpec((3, rows, rows), lambda p, h, rel: (0, 0, 0))
    l_spec = pl.BlockSpec((1, 1, 8, rows), lambda p, h, rel: (p, h, 0, 0))
    return x_spec, o_spec, c_spec, m_spec, l_spec


def attend(rel, x, decay, masks, head_size):
    blocks, _, rows, width = x.shape
    pairs = width // (2 * head_size)
    x_spec, o_spec, c_spec, m_spec, l_spec = attention_specs(blocks, rows, 2 * head_size)
    return pl.pallas_call(
        functools.partial(attend_kernel, blocks, head_size),
        out_shape=[
            jax.ShapeDtypeStruct((blocks, rows, width), BF16),
            jax.ShapeDtypeStruct((pairs, 2, 8, rows), F32),
        ],
        grid_spec=pltpu.PrefetchScalarGridSpec(
            num_scalar_prefetch=1,
            grid=(pairs, 2),
            in_specs=[x_spec, c_spec, m_spec],
            out_specs=[o_spec, l_spec],
        ),
        compiler_params=pltpu.CompilerParams(vmem_limit_bytes=48 << 20),
        cost_estimate=pl.CostEstimate(
            flops=60_000_000_000, bytes_accessed=12_000_000, transcendentals=8_000_000
        ),
        name="attend",
    )(rel, x, decay, masks)


def attend_back(rel, x, grad_o, decay, masks, lse, head_size):
    blocks, _, rows, width = x.shape
    pairs = width // (2 * head_size)
    x_spec, o_spec, c_spec, m_spec, l_spec = attention_specs(blocks, rows, 2 * head_size)
    return pl.pallas_call(
        functools.partial(attend_back_kernel, blocks, head_size),
        out_shape=[
            jax.ShapeDtypeStruct(x.shape, BF16),
            jax.ShapeDtypeStruct((pairs, 2, 8, rows), F32),
            jax.ShapeDtypeStruct((pairs, blocks, rows, 8), F32),
        ],
        grid_spec=pltpu.PrefetchScalarGridSpec(
            num_scalar_prefetch=1,
            grid=(pairs, 2),
            in_specs=[x_spec, o_spec, c_spec, m_spec, l_spec],
            out_specs=[x_spec, l_spec, c_spec],
        ),
        compiler_params=pltpu.CompilerParams(vmem_limit_bytes=56 << 20),
        cost_estimate=pl.CostEstimate(
            flops=120_000_000_000, bytes_accessed=16_000_000, transcendentals=8_000_000
        ),
        name="attend_back",
    )(rel, x, grad_o, decay, masks, lse)


def weight_grad_kernel(count, own_ids, other_ids, l_ref, l_other_ref, r_ref, r_other_ref, *outs):
    def side(ref, ids):
        return jnp.concatenate([ref[ids[k]] for k in range(2 * count)], axis=0)

    total = jnp.dot(side(l_ref, own_ids), r_ref[...], preferred_element_type=F32)
    total = total + jnp.dot(
        side(l_other_ref, other_ids), r_other_ref[...], preferred_element_type=F32
    )
    total = total.astype(BF16).reshape(2 * count, -1, total.shape[1])
    outs[0][...] = total[:count]
    outs[1][...] = total[count:]


def weight_grad(own_ids, other_ids, l_own, l_other, r_own, r_other, start, width):
    count = own_ids.shape[0] // 2
    _, rows, tok = l_own.shape
    limit = 1536 if rows * count < 1024 else 512
    tile = max(t for t in range(128, limit + 1, 128) if width % t == 0 and start % t == 0)
    steps, first = width // tile, start // tile
    whole = lambda v: pl.BlockSpec(v.shape, lambda n, own, other: (0, 0, 0))
    r_spec = pl.BlockSpec((tok, tile), lambda n, own, other: (0, first + n))
    out_spec = pl.BlockSpec((count, rows, tile), lambda n, own, other: (0, 0, n))
    return pl.pallas_call(
        functools.partial(weight_grad_kernel, count),
        out_shape=[jax.ShapeDtypeStruct((count, rows, width), BF16)] * 2,
        grid_spec=pltpu.PrefetchScalarGridSpec(
            num_scalar_prefetch=2,
            grid=(steps,),
            in_specs=[whole(l_own), whole(l_other), r_spec, r_spec],
            out_specs=[out_spec, out_spec],
        ),
        compiler_params=pltpu.CompilerParams(vmem_limit_bytes=48 << 20),
        cost_estimate=pl.CostEstimate(
            flops=8 * count * rows * tok * width,
            bytes_accessed=2 * (2 * count * rows * width + 2 * tok * width),
            transcendentals=0,
        ),
        name="weight_grad",
    )(own_ids, other_ids, l_own, l_other, r_own, r_other)


def split_rows(left):
    n_fsdp = lax.axis_size("fsdp")
    turned = left.T.reshape(n_fsdp, left.shape[1] // n_fsdp, left.shape[0])
    parity = lax.axis_index("fsdp") % 2
    halves = turned.reshape(n_fsdp // 2, 2, *turned.shape[1:])
    away = lax.dynamic_index_in_dim(halves, 1 - parity, 1, keepdims=False)
    return turned, swap(away, "fsdp", 1)


class RowSum:
    def __init__(self, left, columns):
        self.bits = [1 << i for i in range(lax.axis_size("fsdp").bit_length() - 2)]
        f = lax.axis_index("fsdp")
        self.held, self.away, self.orders = [], [], []
        for part, (right, right_other, start, width) in enumerate(columns):
            order = self.bits if part % 2 else self.bits[::-1]
            keep = [0]
            for bit in reversed(order[1:]):
                keep = keep + [k ^ bit for k in keep]
            ids = jnp.stack([flip(f // 2, k) for k in [k ^ order[0] for k in keep] + keep])
            away, held = weight_grad(
                2 * ids + f % 2, ids, left[0], left[1], right, right_other, start, width
            )
            self.held.append(held)
            self.away.append(away)
            self.orders.append(order)

    def after(self, *values):
        tied = lax.optimization_barrier((self.away, self.held) + values)
        self.away, self.held = tied[0], tied[1]
        return tied[2:]

    def send(self):
        self.arrived = [swap(v, "fsdp", 2 * o[0]) for v, o in zip(self.away, self.orders)]

    def halve(self):
        away, held = [], []
        for mine, new, order in zip(self.held, self.arrived, self.orders):
            total = mine.astype(F32) + new.astype(F32)
            count = mine.shape[0] // 2
            held.append(total[:count].astype(BF16))
            away.append(total[count:].astype(BF16))
        self.held, self.away = held, away
        self.orders = [o[1:] for o in self.orders]

    def spread(self):
        n_grp, z = lax.axis_size("grp"), lax.axis_index("grp")
        self.held, self.away = [], []
        for mine, new in zip(self.last, self.arrived):
            total = (mine.astype(F32) + new.astype(F32))[0]
            total = total.reshape(n_grp, total.shape[0] // n_grp, total.shape[1])
            self.held.append(lax.dynamic_index_in_dim(total, z, 0, keepdims=False))
            self.away.append(
                [
                    lax.dynamic_index_in_dim(total, flip(z, k), 0, keepdims=False).astype(BF16)
                    for k in range(1, n_grp)
                ]
            )

    def middle(self):
        for _ in self.bits[1:]:
            self.halve()
            self.send()
        self.last = self.held

    def send_spread(self):
        self.arrived = [
            [swap(v, "grp", k + 1) for k, v in enumerate(pieces)] for pieces in self.away
        ]

    def result(self):
        sums = []
        for mine, pieces in zip(self.held, self.arrived):
            for piece in pieces:
                mine = mine + piece.astype(F32)
            sums.append(mine)
        return jnp.concatenate(sums, axis=1)

    def finish(self):
        self.send()
        self.middle()
        self.spread()
        self.send_spread()
        return self.result()


def sum_everywhere(values):
    for axis in ("grp", "fsdp"):
        mask = 1
        while mask < lax.axis_size(axis):
            values = values + swap(values, axis, mask)
            mask *= 2
    return values


def norm_rows(features):
    row_scale = lax.rsqrt(jnp.mean(features * features, axis=-1, keepdims=True) + EPSILON)
    return (features * row_scale, row_scale)


def norm_back(grad_normed, normed, row_scale):
    average_addend = jnp.mean(grad_normed * normed, axis=-1, keepdims=True)
    return row_scale * (grad_normed - normed * average_addend)


def contract_cols(first_op, second_op):
    return lax.dot_general(
        first_op, second_op, (((1,), (1,)), ((), ())), preferred_element_type=F32
    )


def exchange(by_group):
    z = lax.axis_index("grp")
    parts = []
    for k in range(by_group.shape[0]):
        part = lax.dynamic_index_in_dim(by_group, flip(z, k), 0, keepdims=False)
        parts.append(swap(part, "grp", k) if k else part)
    return jnp.stack(parts)


def exchange_back(by_distance):
    z = lax.axis_index("grp")
    parts = [by_distance[0]]
    for k in range(1, by_distance.shape[0]):
        parts.append(swap(by_distance[k], "grp", k))
    stacked = jnp.stack(parts)
    return [
        lax.dynamic_index_in_dim(stacked, flip(z, g), 0, keepdims=False)
        for g in range(by_distance.shape[0])
    ]


def flip_traced(value, mask):
    return jnp.bitwise_xor(value, mask)


def on_device(
    tokens,
    block_order,
    cont_lengths,
    gain_attn,
    w_qkv,
    w_forget,
    b_forget,
    w_out,
    gain_ffn,
    w_gate_up,
    w_down,
    grad_out,
):
    tok, width = tokens.shape
    heads = w_forget.shape[1]
    head_size = width // heads
    blocks = lax.axis_size("grp")
    z = lax.axis_index("grp")
    own_heads = heads // blocks
    pairs = own_heads // 2
    group_width = width // blocks
    slots = block_order[0]
    rel = flip_traced(slots, z)

    positions = jnp.arange(tok, dtype=jnp.int32)
    causal = positions[None, :] <= positions[:, None]
    seg_ends = jnp.cumsum(cont_lengths[0], axis=1)
    segment = jnp.sum((positions[None, :, None] >= seg_ends[:, None, :]).astype(jnp.int32), axis=2)
    within = jnp.logical_and(segment[:, :, None] == segment[:, None, :], causal[None])
    seen = jnp.concatenate([causal[None], within], axis=0)
    masks = jnp.where(seen.transpose(0, 2, 1), 0.0, NEG).astype(F32)
    summing = jnp.concatenate([causal[None], seen], axis=0).astype(F32)

    forget_pad = 128 - heads
    qkv_full, forget_full = gather_rows(
        [w_qkv, jnp.pad(w_forget, ((0, 0), (0, forget_pad)))], 1
    )
    inputs = tokens.astype(F32)
    normed_one, scale_one = norm_rows(inputs)
    acts = (normed_one * gain_attn).astype(BF16)
    grad_out_other = swap(grad_out, "fsdp", 1)
    acts_rows = split_rows(acts)
    logits = jnp.dot(acts, forget_full, preferred_element_type=F32)[:, :heads] + b_forget
    log_keep = jax.nn.log_sigmoid(logits)
    mixed = jnp.dot(acts, qkv_full, preferred_element_type=F32).astype(BF16)

    by_group = mixed.reshape(tok, 3, blocks, group_width).transpose(2, 1, 0, 3)
    x = exchange(by_group)
    logs = exchange(log_keep.T.reshape(blocks, own_heads, tok))

    gu_in, out_in, _ = lax.optimization_barrier((w_gate_up, w_out, mixed[:8, :128]))
    gate_up_full, out_full = gather_rows([gu_in, out_in], 2)

    logs_block = jnp.stack(
        [lax.dynamic_index_in_dim(logs, rel[b], 0, keepdims=False) for b in range(blocks)]
    )
    local = jnp.einsum("bhj,bij->bhi", logs_block, summing, precision=HIGHEST)
    second = local[1] + local[0][:, -1:]
    decay = jnp.concatenate([local[:1], second[None], local[2:]], axis=0)
    decay_cols = decay.reshape(blocks, pairs, 2, tok).transpose(1, 0, 3, 2)
    decay_cols = jnp.pad(decay_cols, ((0, 0), (0, 0), (0, 0), (0, 6)))
    x, gate_up_full, out_full, down_in = lax.optimization_barrier(
        (x, gate_up_full, out_full, w_down)
    )
    down_full = lax.all_gather(down_in, ("fsdp", "grp"), axis=0, tiled=True)
    head_out, lse = attend(rel, x, decay_cols, masks, head_size)
    attn_o = jnp.concatenate(exchange_back(head_out), axis=1)

    attn_rows = split_rows(attn_o)
    resid = inputs + jnp.dot(attn_o, out_full, preferred_element_type=F32)
    normed_two, scale_two = norm_rows(resid)
    acts_two = (normed_two * gain_ffn).astype(BF16)
    acts_two_rows = split_rows(acts_two)
    ffn_width = down_full.shape[0]
    both = jnp.dot(acts_two, gate_up_full, preferred_element_type=F32)
    gate = both[:, :ffn_width]
    up_part = both[:, ffn_width:]
    sigma = jax.nn.sigmoid(gate)
    swish = gate * sigma
    inner_act = (swish * up_part).astype(BF16)
    half = width // 2
    sum_down = RowSum(
        split_rows(inner_act),
        [(grad_out, grad_out_other, 0, half), (grad_out, grad_out_other, half, half)],
    )
    inner_act, resid = sum_down.after(inner_act, resid)
    sum_down.send()
    result = resid + jnp.dot(inner_act, down_full, preferred_element_type=F32)
    output = result.astype(BF16)

    grad_inner = contract_cols(grad_out, down_full)
    slope = sigma * (1.0 + gate * (1.0 - sigma))
    grad_both = jnp.concatenate(
        [grad_inner * up_part * slope, grad_inner * swish], axis=1
    ).astype(BF16)
    sum_down.middle()
    grad_both_other = swap(grad_both, "fsdp", 1)
    (grad_both,) = sum_down.after(grad_both)
    grad_acts_two = contract_cols(grad_both, gate_up_full)
    gain_two_grad = jnp.sum(grad_acts_two * normed_two, axis=0)
    grad_resid = grad_out.astype(F32) + norm_back(
        grad_acts_two * gain_ffn, normed_two, scale_two
    )
    grad_branch = grad_resid.astype(BF16)
    grad_branch_other = swap(grad_branch, "fsdp", 1)
    grad_heads = contract_cols(grad_branch, out_full).astype(BF16)
    sum_down.spread()
    (grad_heads,) = sum_down.after(grad_heads)
    grad_o = exchange(grad_heads.reshape(tok, blocks, group_width).transpose(1, 0, 2))
    sum_gate_up = RowSum(
        acts_two_rows,
        [
            (grad_both, grad_both_other, 0, ffn_width),
            (grad_both, grad_both_other, ffn_width, ffn_width),
        ],
    )
    sum_gate_up.after()
    sum_gate_up.send()
    sum_down.send_spread()
    sum_out = RowSum(
        attn_rows,
        [
            (grad_branch, grad_branch_other, 0, half),
            (grad_branch, grad_branch_other, half, half),
        ],
    )
    (grad_o,) = sum_out.after(grad_o)
    sum_out.send()

    grad_x, grad_q_decay, grad_k_decay = attend_back(
        rel, x, grad_o, decay_cols, masks, lse, head_size
    )
    sum_gate_up.middle()
    sum_out.middle()
    (grad_x,) = sum_gate_up.after(grad_x)
    (grad_x,) = sum_out.after(grad_x)
    grad_mixed = jnp.stack(exchange_back(grad_x))
    grad_mixed = grad_mixed.transpose(2, 1, 0, 3).reshape(tok, 3 * width)
    grad_q_decay = grad_q_decay[:, :, :blocks].transpose(2, 0, 1, 3).reshape(blocks, own_heads, tok)
    grad_k_decay = grad_k_decay[:, :, :, :2].transpose(1, 0, 3, 2).reshape(blocks, own_heads, tok)
    grad_decay = grad_q_decay - grad_k_decay
    after_second = jnp.sum(grad_q_decay[2:], axis=(0, 2))[None, :, None]
    after_first = after_second + jnp.sum(grad_decay[1], axis=1)[None, :, None]
    after = jnp.concatenate(
        [after_first, after_second, jnp.zeros((blocks - 2, own_heads, 1), F32)], axis=0
    )
    grad_logs = jnp.einsum("bhi,bij->bhj", grad_decay, summing, precision=HIGHEST) + after
    order_back = jnp.stack(
        [
            jnp.sum(jnp.arange(blocks, dtype=jnp.int32) * (rel == k).astype(jnp.int32))
            for k in range(blocks)
        ]
    )
    logs_back = jnp.stack(
        [
            lax.dynamic_index_in_dim(grad_logs, order_back[k], 0, keepdims=False)
            for k in range(blocks)
        ]
    )
    log_grad = jnp.concatenate(exchange_back(logs_back), axis=0)
    grad_logits = log_grad.T * jax.nn.sigmoid(-logits)
    grad_logits = grad_logits.astype(BF16)

    sum_gate_up.spread()
    sum_gate_up.send_spread()
    sum_out.spread()
    sum_out.send_spread()
    part = 3 * width // 2
    narrow = jnp.pad(grad_logits, ((0, 0), (0, forget_pad)))
    last = jnp.concatenate([grad_mixed[:, part:], narrow], axis=1)
    sum_qkv = RowSum(
        acts_rows,
        [
            (grad_mixed, swap(grad_mixed, "fsdp", 1), 0, part),
            (last, swap(last, "fsdp", 1), 0, part + 128),
        ],
    )
    sum_qkv.after()
    grad_wide = sum_qkv.finish()
    grad_qkv, grad_forget = grad_wide[:, : 3 * width], grad_wide[:, 3 * width :][:, :heads]
    grad_acts = contract_cols(grad_mixed, qkv_full) + contract_cols(
        grad_logits, forget_full[:, :heads]
    )
    gain_one_grad = jnp.sum(grad_acts * normed_one, axis=0)
    bias_grad = jnp.sum(grad_logits.astype(F32), axis=0)
    grad_inputs = grad_resid + norm_back(grad_acts * gain_attn, normed_one, scale_one)
    small = sum_everywhere(jnp.concatenate([gain_one_grad, gain_two_grad, bias_grad]))
    return (
        output,
        grad_inputs.astype(BF16),
        small[:width],
        grad_qkv,
        grad_forget,
        small[2 * width :],
        sum_out.result(),
        small[width : 2 * width],
        sum_gate_up.result(),
        sum_down.result(),
    )


def solution(mesh):
    both = P(("fsdp", "grp"), None)
    in_specs = (
        both,
        P("fsdp", None),
        P("fsdp", None, None),
        P(),
        both,
        both,
        P(),
        both,
        P(),
        both,
        both,
        both,
    )
    out_specs = (both, both, P(), both, both, P(), both, P(), both, both)
    return jax.shard_map(
        on_device, mesh=mesh, in_specs=in_specs, out_specs=out_specs, check_vma=False
    )
```

time: 2280 us -> 1170 us (0.51)
  waiting for transfers between devices: 1620 us -> 372 us
  Pallas kernels: 0 us -> 401 us
  matrix products: 339 us -> 99.5 us
  blocking collectives: 124 us -> 0 us
  starting transfers between devices: 0.95 us -> 91.7 us
    reduce_scatter x4 -> x0, waiting for transfers between devices: 1050 us -> none  [the longest x1 438 us: on_device(): lax.psum_scatter(grad_gate_up, ('fsdp', 'grp'), scatter_dimension=0, tile...]
    pallas_call x0 -> x12, Pallas kernels: none -> 401 us  [the longest x2 282 us: gather_rows(): pl.pallas_call(functools.partial(gather_kernel, shapes, n_fsdp, n_grp), o...]
    all_gather x6 -> x1, waiting for transfers between devices: 387 us -> 0.01 us  [on_device(): down_full = lax.all_gather(down_in, ('fsdp', 'grp'), axis=0, tiled=True)]
    ppermute x0 -> x72, waiting for transfers between devices: none -> 372 us  [swap(): lax.ppermute(value, axis, [(i, i ^ mask) for i in range(lax.axis_size(axi...]
    dot_general x95 -> x7, matrix products: 282 us -> 48.2 us  [the longest x1 17.7 us: on_device(): both = jnp.dot(acts_two, gate_up_full, preferred_element_type=F32)]
    unnamed x18 -> x1, waiting for transfers between devices: 185 us -> 0.02 us
    ppermute x0 -> x72, starting transfers between devices: none -> 91.6 us  [swap(): lax.ppermute(value, axis, [(i, i ^ mask) for i in range(lax.axis_size(axi...]
    all_gather x2 -> x0, blocking collectives: 84.3 us -> none  [the longest x1 69.5 us: on_device(): lax.all_gather(w_forget, ('fsdp', 'grp'), axis=0, tiled=True)]
  transfers between devices with their start and end apart: 14 -> 73, of which waited for: 11 -> 30; matrix products, arithmetic and copies ran while one was open for 11% -> 14% of each run, Pallas kernels for 0% -> 28%
where the time goes in v1:
time: 1170 us; the launch traced here: 1160 us
  Pallas kernels  401 us (34%)
  waiting for transfers between devices  372 us (32%)
  local copies, waits for them, and re-layouts  99.9 us (9%)
  matrix products  99.5 us (9%)
  starting transfers between devices  91.7 us (8%)
  other arithmetic  63.8 us (5%)
  between operations  31.6 us (3%)
    ppermute x72, waiting for transfers between devices, swap(): lax.ppermute(value, axis, [(i, i ^ mask) for i in range(lax.axis_size(axi...  372 us
    pallas_call x2, Pallas kernels, gather_rows(): pl.pallas_call(functools.partial(gather_kernel, shapes, n_fsdp, n_grp), o...  282 us
    ppermute x72, starting transfers between devices, swap(): lax.ppermute(value, axis, [(i, i ^ mask) for i in range(lax.axis_size(axi...  91.6 us
    pallas_call x8, Pallas kernels, weight_grad(): pl.pallas_call(functools.partial(weight_grad_kernel, count), out_shape=[j...  63.9 us
    dot_general x5, matrix products, contract_cols(): lax.dot_general(first_op, second_op, (((1,), (1,)), ((), ())), preferred_...  51.4 us
    pallas_call x1, Pallas kernels, attend_back(): pl.pallas_call(functools.partial(attend_back_kernel, blocks, head_size),...  33.9 us
  transfers between devices with their start and end apart: 73, of which 30 were waited for; matrix products, arithmetic and copies ran while one was open for 14% of the time, Pallas kernels for 28%

profile of v1, /device:TPU:8, one launch (start us, length us, event | category | flops | bytes accessed | tf_op | source)
XLA Modules:
  0.0 1159.5 jit_solution(16837291097808325318)
XLA Ops:
  10.3 78.4 %gather_rows.2 = (bf16[32,48,4608]{2,1,0:T(8,128)(2,1)}, bf16[32,48,128]{2,1,0:T(8,128)(2,1)}) custom-call(bf16[48,4608]{1,0:T(8,128)(2,1)} %refs_0_.1, bf16[48,128]{1,0:T(8,128)(2,1)} %pad.12.refs_1_), custom_call_target="tpu_custom_call" | custom-call | tf_op jit(solution)/shard_map/gather_rows/pallas_call | solution.py:132
  88.7 12.6 %convolution_convert_fusion = bf16[384,4608]{1,0:T(8,128)(2,1)} fusion(bf16[1536,4608]{1,0:T(8,128)(2,1)} %bitcast.333, bf16[384,1536]{1,0:T(8,128)(2,1)} %param.12, f32[1536]{0:T(1024)} %param.15, f32[384]{0:T(512)S(1)} %add_rsqrt_fusion.1), kind=kOutput, calls=%fused_computation | convolution fusion | flops 5439946752 | bytes 18882048 | tf_op jit(solution)/shard_map/dot_general | solution.py:542
  120.2 203.5 %gather_rows.3 = (bf16[32,48,8192]{2,1,0:T(8,128)(2,1)}, bf16[32,48,1536]{2,1,0:T(8,128)(2,1)}) custom-call(bf16[48,8192]{1,0:T(8,128)(2,1)} %refs_0_.2, bf16[48,1536]{1,0:T(8,128)(2,1)} %refs_1_), custom_call_target="tpu_custom_call" | custom-call | tf_op jit(solution)/shard_map/gather_rows/pallas_call | solution.py:132
  330.0 16.3 %collective-permute-start.3 = (f32[6,384]{1,0:T(8,128)S(1)}, f32[6,384]{1,0:T(8,128)S(1)}, u32[]{:S(2)}, u32[]{:S(2)}) collective-permute-start(f32[6,384]{1,0:T(8,128)S(1)} %get-tuple-element.259), channel_id=1, source_target_pairs={{0,1},{1,0},{2,3},{3,2},{4,5},{5,4},{6,7},{7,6},{8,9},{9,8},{10,11... | collective-permute-start | bytes 27656 | tf_op jit(solution)/shard_map/ppermute | solution.py:32
  363.0 21.2 %attend.1 = (bf16[4,384,384]{2,1,0:T(8,128)(2,1)S(1)}, f32[3,2,8,384]{3,2,1,0:T(8,128)S(1)}) custom-call(s32[4]{0:T(128)S(1)} %bitcast.275, bf16[4,3,384,384]{3,2,1,0:T(8,128)(2,1)} %pad_maximum_fusion.1.x_ref, f32[3,4,384,8]{3,2,1,0:T(8,128)S(1)} %pad.13.c_ref, f32[3,384,384]{2,1,0:T(8,128)S(1)} %select_bitcast_fusion.mask_ref), custom_call_target="tpu_custom_call" | custom-call | flops 60000002048 | bytes 12000000 | tf_op jit(solution)/shard_map/attend/pallas_call | solution.py:275
  388.8 14.6 %collective-permute-done.6 = bf16[384,384]{1,0:T(8,128)(2,1)S(1)} collective-permute-done((bf16[384,384]{1,0:T(8,128)(2,1)S(1)}, bf16[384,384]{1,0:T(8,128)(2,1)S(1)}, u32[]{:S(2)}, u32[]{:S(2)}) %collective-permute-start.6) | collective-permute-done | bytes 294944 | tf_op jit(solution)/shard_map/ppermute | solution.py:32
  406.7 28.2 %collective-permute-done.8 = bf16[384,384]{1,0:T(8,128)(2,1)S(1)} collective-permute-done((bf16[384,384]{1,0:T(8,128)(2,1)S(1)}, bf16[384,384]{1,0:T(8,128)(2,1)S(1)}, u32[]{:S(2)}, u32[]{:S(2)}) %collective-permute-start.8) | collective-permute-done | bytes 294944 | tf_op jit(solution)/shard_map/ppermute | solution.py:32
  441.4 17.7 %fusion.86 = f32[384,8192]{1,0:T(8,128)} fusion(bf16[1536,8192]{1,0:T(8,128)(2,1)} %bitcast.331, f32[384,1536]{1,0:T(8,128)S(1)} %get-tuple-element.86, f32[1536]{0:T(1024)S(1)} %copy-done.59, f32[384]{0:T(512)S(1)} %add_rsqrt_fusion), kind=kOutput, calls=%fused_computation.248 | convolution fusion | flops 9665445888 | bytes 40115712 | tf_op jit(solution)/shard_map/dot_general | solution.py:572
  459.2 17.9 %fusion.1 = (bf16[384,4096]{1,0:T(8,128)(2,1)}, bf16[384,4096]{1,0:T(8,128)(2,1)}, bf16[384,4096]{1,0:T(8,128)(2,1)}) fusion(f32[384,8192]{1,0:T(8,128)} %fusion.86, bf16[4096,1536]{1,0:T(8,128)(2,1)} %all-gather.2.cloned.1.call-done, bf16[384,1536]{1,0:T(8,128)(2,1)S(1)} %copy-done), kind=kOutput, calls=%fused_computation.5 | convolution fusion | flops 4855431168 | bytes 35782656 | tf_op jit(solution)/shard_map/dot_general | solution.py:467
  483.4 6.8 constant_dynamic-slice_fusion.16
  490.2 8.2 copy.151
  516.8 7.5 weight_grad.9
  524.3 7.4 weight_grad.8
  540.1 9.5 fusion.97
  549.7 19.0 %collective-permute-done.12 = bf16[2,512,768]{2,1,0:T(8,128)(2,1)} collective-permute-done((bf16[2,512,768]{2,1,0:T(8,128)(2,1)S(1)}, bf16[2,512,768]{2,1,0:T(8,128)(2,1)}, u32[]{:S(2)}, u32[]{:S(2)}) %collective-permute-start.12) | collective-permute-done | bytes 1572896 | tf_op jit(solution)/shard_map/ppermute | solution.py:32
  581.2 17.5 %fusion.98 = f32[384,1536]{1,0:T(8,128)} fusion(bf16[384,8192]{1,0:T(8,128)(2,1)} %pad_maximum_fusion.r_ref, bf16[1536,8192]{1,0:T(8,128)(2,1)} %bitcast.332), kind=kOutput, calls=%fused_computation.257 | convolution fusion | flops 9663676416 | bytes 33816576 | tf_op jit(solution)/shard_map/dot_general | solution.py:467
  643.3 12.6 %collective-permute-done.18 = bf16[384,384]{1,0:T(8,128)(2,1)S(1)} collective-permute-done((bf16[384,384]{1,0:T(8,128)(2,1)S(1)}, bf16[384,384]{1,0:T(8,128)(2,1)S(1)}, u32[]{:S(2)}, u32[]{:S(2)}) %collective-permute-start.18) | collective-permute-done | bytes 294944 | tf_op jit(solution)/shard_map/ppermute | solution.py:32
  655.9 7.3 collective-permute-done.19
  676.3 33.9 %attend_back.1 = (bf16[4,3,384,384]{3,2,1,0:T(8,128)(2,1)}, f32[3,2,8,384]{3,2,1,0:T(8,128)}, f32[3,4,384,8]{3,2,1,0:T(8,128)}) custom-call(s32[4]{0:T(128)} %bitcast.276, bf16[4,3,384,384]{3,2,1,0:T(8,128)(2,1)} %pad_maximum_fusion.1.x_ref, bf16[4,384,384]{2,1,0:T(8,128)(2,1)} %pad_maximum_fusion.6.do_ref, f32[3,4,384,8]{3,2,1,0:T(8,128)} %copy-done.4, ...), custom_call_target="tpu_custom_call" | custom-call | flops 120000004096 | bytes 16000000 | tf_op jit(solution)/shard_map/attend_back/pallas_call | solution.py:299
  713.3 10.7 weight_grad.13
  724.0 10.7 weight_grad.12
  754.4 61.1 %collective-permute-done.20 = bf16[2,192,768]{2,1,0:T(8,128)(2,1)S(1)} collective-permute-done((bf16[2,192,768]{2,1,0:T(8,128)(2,1)S(1)}, bf16[2,192,768]{2,1,0:T(8,128)(2,1)S(1)}, u32[]{:S(2)}, u32[]{:S(2)}) %collective-permute-start.20) | collective-permute-done | bytes 589856 | tf_op jit(solution)/shard_map/ppermute | solution.py:32
  816.2 8.8 collective-permute-done.21
  851.8 72.9 %collective-permute-done.53 = bf16[48,768]{1,0:T(8,128)(2,1)S(1)} collective-permute-done((bf16[48,768]{1,0:T(8,128)(2,1)S(1)}, bf16[48,768]{1,0:T(8,128)(2,1)S(1)}, u32[]{:S(2)}, u32[]{:S(2)}) %collective-permute-start.53) | collective-permute-done | bytes 73760 | tf_op jit(solution)/shard_map/ppermute | solution.py:32
  938.7 9.9 fusion.99
  970.5 12.1 %collective-permute-done.35 = f32[3096]{0:T(1024)S(1)} collective-permute-done((f32[3096]{0:T(1024)S(1)}, f32[3096]{0:T(1024)S(1)}, u32[]{:S(2)}, u32[]{:S(2)}) %collective-permute-start.35) | collective-permute-done | bytes 12416 | tf_op jit(solution)/shard_map/ppermute | solution.py:32
  998.1 15.0 %weight_grad.15 = (bf16[2,192,2432]{2,1,0:T(8,128)(2,1)S(1)}, bf16[2,192,2432]{2,1,0:T(8,128)(2,1)S(1)}) custom-call(s32[4]{0:T(128)S(1)} %get-tuple-element.185.own_ids, s32[4]{0:T(128)S(1)} %get-tuple-element.186.other_ids, bf16[8,192,384]{2,1,0:T(8,128)(2,1)S(1)} %bitcast.273, bf16[4,192,384]{2,1,0:T(8,128)(2,1)S(1)} %collective-permute-done.37.l_other_ref, ...), custom_call_target="tpu_custom_call" | custom-call | flops 2868903936 | bytes 7471104 | tf_op jit(solution)/shard_map/weight_grad/pallas_call | solution.py:342
  1023.7 22.9 %collective-permute-done.61 = bf16[48,4096]{1,0:T(8,128)(2,1)S(1)} collective-permute-done((bf16[48,4096]{1,0:T(8,128)(2,1)S(1)}, bf16[48,4096]{1,0:T(8,128)(2,1)S(1)}, u32[]{:S(2)}, u32[]{:S(2)}) %collective-permute-start.61) | collective-permute-done | bytes 393248 | tf_op jit(solution)/shard_map/ppermute | solution.py:32
  1053.2 9.9 collective-permute-done.65
  1066.5 25.1 %collective-permute-done.45 = bf16[2,192,2432]{2,1,0:T(8,128)(2,1)S(1)} collective-permute-done((bf16[2,192,2432]{2,1,0:T(8,128)(2,1)S(1)}, bf16[2,192,2432]{2,1,0:T(8,128)(2,1)S(1)}, u32[]{:S(2)}, u32[]{:S(2)}) %collective-permute-start.45) | collective-permute-done | bytes 1867808 | tf_op jit(solution)/shard_map/ppermute | solution.py:32
  1094.0 14.9 %collective-permute-done.41 = bf16[1,192,2304]{2,1,0:T(8,128)(2,1)S(1)} collective-permute-done((bf16[1,192,2304]{2,1,0:T(8,128)(2,1)S(1)}, bf16[1,192,2304]{2,1,0:T(8,128)(2,1)S(1)}, u32[]{:S(2)}, u32[]{:S(2)}) %collective-permute-start.41) | collective-permute-done | bytes 884768 | tf_op jit(solution)/shard_map/ppermute | solution.py:32
  1125.8 16.6 %collective-permute-done.44 = bf16[48,2304]{1,0:T(8,128)(2,1)S(1)} collective-permute-done((bf16[48,2304]{1,0:T(8,128)(2,1)S(1)}, bf16[48,2304]{1,0:T(8,128)(2,1)S(1)}, u32[]{:S(2)}, u32[]{:S(2)}) %collective-permute-start.44) | collective-permute-done | bytes 221216 | tf_op jit(solution)/shard_map/ppermute | solution.py:32
  (443 shorter events, 296.9 us)
Async XLA Ops:
  7.2 452.0 %all-gather.2.cloned.1.call-start = ((), (), s32[]{:S(2)}) async-start(), calls=%async_computation | async-start | bytes 12976128 | tf_op jit(solution)/shard_map/all_gather | solution.py:562
  110.1 213.7 %collective-permute-start = (bf16[3,384,384]{2,1,0:T(8,128)(2,1)}, bf16[3,384,384]{2,1,0:T(8,128)(2,1)S(1)}, u32[]{:S(2)}, u32[]{:S(2)}) collective-permute-start(bf16[3,384,384]{2,1,0:T(8,128)(2,1)} %bitcast.307), channel_id=1, source_target_pairs={{0,1},{1,0},{2,3},{3,2},{4,5},{5,4},{6,7},{7,6},{8,9},{9,8},{10,11... | collective-permute-start | bytes 2654216 | tf_op jit(solution)/shard_map/ppermute | solution.py:32
  113.2 210.6 %collective-permute-start.1 = (bf16[3,384,384]{2,1,0:T(8,128)(2,1)}, bf16[3,384,384]{2,1,0:T(8,128)(2,1)S(1)}, u32[]{:S(2)}, u32[]{:S(2)}) collective-permute-start(bf16[3,384,384]{2,1,0:T(8,128)(2,1)} %bitcast.308), channel_id=1, source_target_pairs={{0,2},{1,3},{2,0},{3,1},{4,6},{5,7},{6,4},{7,5},{8,10},{9,11},{10,... | collective-permute-start | bytes 2654216 | tf_op jit(solution)/shard_map/ppermute | solution.py:32
  116.4 207.4 %collective-permute-start.2 = (bf16[3,384,384]{2,1,0:T(8,128)(2,1)}, bf16[3,384,384]{2,1,0:T(8,128)(2,1)}, u32[]{:S(2)}, u32[]{:S(2)}) collective-permute-start(bf16[3,384,384]{2,1,0:T(8,128)(2,1)} %bitcast.309), channel_id=1, source_target_pairs={{0,3},{1,2},{2,1},{3,0},{4,7},{5,6},{6,5},{7,4},{8,11},{9,10},{10,... | collective-permute-start | bytes 2654216 | tf_op jit(solution)/shard_map/ppermute | solution.py:32
  387.7 47.1 %collective-permute-start.8 = (bf16[384,384]{1,0:T(8,128)(2,1)S(1)}, bf16[384,384]{1,0:T(8,128)(2,1)S(1)}, u32[]{:S(2)}, u32[]{:S(2)}) collective-permute-start(bf16[384,384]{1,0:T(8,128)(2,1)S(1)} %get-tuple-element.233), channel_id=1, source_target_pairs={{0,3},{1,2},{2,1},{3,0},{4,7},{5,6},{6,5},{7,4},{8,11},{9,10},{10,... | collective-permute-start | bytes 884744 | tf_op jit(solution)/shard_map/ppermute | solution.py:32
  512.1 152.3 %collective-permute-start.13 = (bf16[4,192,384]{2,1,0:T(8,128)(2,1)}, bf16[4,192,384]{2,1,0:T(8,128)(2,1)}, u32[]{:S(2)}, u32[]{:S(2)}) collective-permute-start(bf16[4,192,384]{2,1,0:T(8,128)(2,1)} %dynamic-slice_bitcast_fusion.2), channel_id=1, source_target_pairs={{0,4},{4,0},{8,12},{12,8},{16,20},{20,16},{24,28},{28,24},{1,5},{5... | collective-permute-start | bytes 1769480 | tf_op jit(solution)/shard_map/ppermute | solution.py:32
  531.7 37.0 %collective-permute-start.12 = (bf16[2,512,768]{2,1,0:T(8,128)(2,1)S(1)}, bf16[2,512,768]{2,1,0:T(8,128)(2,1)}, u32[]{:S(2)}, u32[]{:S(2)}) collective-permute-start(bf16[2,512,768]{2,1,0:T(8,128)(2,1)S(1)} %get-tuple-element.92), channel_id=1, source_target_pairs={{0,8},{4,12},{8,0},{12,4},{16,24},{20,28},{24,16},{28,20},{1,9},{5... | collective-permute-start | bytes 4718600 | tf_op jit(solution)/shard_map/ppermute | solution.py:32
  538.7 36.5 %collective-permute-start.11 = (bf16[2,512,768]{2,1,0:T(8,128)(2,1)S(1)}, bf16[2,512,768]{2,1,0:T(8,128)(2,1)S(1)}, u32[]{:S(2)}, u32[]{:S(2)}) collective-permute-start(bf16[2,512,768]{2,1,0:T(8,128)(2,1)S(1)} %get-tuple-element.90), channel_id=1, source_target_pairs={{0,16},{4,20},{8,24},{12,28},{16,0},{20,4},{24,8},{28,12},{1,17},{... | collective-permute-start | bytes 4718600 | tf_op jit(solution)/shard_map/ppermute | solution.py:32
  610.4 55.7 %collective-permute-start.14 = (bf16[384,1536]{1,0:T(8,128)(2,1)S(1)}, bf16[384,1536]{1,0:T(8,128)(2,1)S(1)}, u32[]{:S(2)}, u32[]{:S(2)}) collective-permute-start(bf16[384,1536]{1,0:T(8,128)(2,1)S(1)} %fusion.90.r_ref), channel_id=1, source_target_pairs={{0,4},{4,0},{8,12},{12,8},{16,20},{20,16},{24,28},{28,24},{1,5},{5... | collective-permute-start | bytes 3538952 | tf_op jit(solution)/shard_map/ppermute | solution.py:32
  643.2 70.1 %collective-permute-start.23 = (bf16[384,8192]{1,0:T(8,128)(2,1)}, bf16[384,8192]{1,0:T(8,128)(2,1)}, u32[]{:S(2)}, u32[]{:S(2)}) collective-permute-start(bf16[384,8192]{1,0:T(8,128)(2,1)} %pad_maximum_fusion.r_ref), channel_id=1, source_target_pairs={{0,4},{4,0},{8,12},{12,8},{16,20},{20,16},{24,28},{28,24},{1,5},{5... | collective-permute-start | bytes 18874376 | tf_op jit(solution)/shard_map/ppermute | solution.py:32
  655.9 57.4 %collective-permute-start.22 = (bf16[4,192,384]{2,1,0:T(8,128)(2,1)}, bf16[4,192,384]{2,1,0:T(8,128)(2,1)}, u32[]{:S(2)}, u32[]{:S(2)}) collective-permute-start(bf16[4,192,384]{2,1,0:T(8,128)(2,1)} %dynamic-slice_bitcast_fusion.1), channel_id=1, source_target_pairs={{0,4},{4,0},{8,12},{12,8},{16,20},{20,16},{24,28},{28,24},{1,5},{5... | collective-permute-start | bytes 1769480 | tf_op jit(solution)/shard_map/ppermute | solution.py:32
  663.2 80.8 %collective-permute-start.69 = (bf16[128,768]{1,0:T(8,128)(2,1)}, bf16[128,768]{1,0:T(8,128)(2,1)}, u32[]{:S(2)}, u32[]{:S(2)}) collective-permute-start(bf16[128,768]{1,0:T(8,128)(2,1)} %get-tuple-element.131), channel_id=1, source_target_pairs={{0,1},{1,0},{2,3},{3,2},{4,5},{5,4},{6,7},{7,6},{8,9},{9,8},{10,11... | collective-permute-start | bytes 589832 | tf_op jit(solution)/shard_map/ppermute | solution.py:32
  664.4 81.4 %collective-permute-start.70 = (bf16[128,768]{1,0:T(8,128)(2,1)}, bf16[128,768]{1,0:T(8,128)(2,1)}, u32[]{:S(2)}, u32[]{:S(2)}) collective-permute-start(bf16[128,768]{1,0:T(8,128)(2,1)} %get-tuple-element.132), channel_id=1, source_target_pairs={{0,2},{1,3},{2,0},{3,1},{4,6},{5,7},{6,4},{7,5},{8,10},{9,11},{10,... | collective-permute-start | bytes 589832 | tf_op jit(solution)/shard_map/ppermute | solution.py:32
  666.1 80.6 %collective-permute-start.71 = (bf16[128,768]{1,0:T(8,128)(2,1)}, bf16[128,768]{1,0:T(8,128)(2,1)}, u32[]{:S(2)}, u32[]{:S(2)}) collective-permute-start(bf16[128,768]{1,0:T(8,128)(2,1)} %get-tuple-element.133), channel_id=1, source_target_pairs={{0,3},{1,2},{2,1},{3,0},{4,7},{5,6},{6,5},{7,4},{8,11},{9,10},{10,... | collective-permute-start | bytes 589832 | tf_op jit(solution)/shard_map/ppermute | solution.py:32
  734.7 95.4 %collective-permute-start.24 = (bf16[2,192,4096]{2,1,0:T(8,128)(2,1)}, bf16[2,192,4096]{2,1,0:T(8,128)(2,1)}, u32[]{:S(2)}, u32[]{:S(2)}) collective-permute-start(bf16[2,192,4096]{2,1,0:T(8,128)(2,1)} %get-tuple-element.108), channel_id=1, source_target_pairs={{0,16},{4,20},{8,24},{12,28},{16,0},{20,4},{24,8},{28,12},{1,17},{... | collective-permute-start | bytes 9437192 | tf_op jit(solution)/shard_map/ppermute | solution.py:32
  741.3 92.2 %collective-permute-start.25 = (bf16[2,192,4096]{2,1,0:T(8,128)(2,1)}, bf16[2,192,4096]{2,1,0:T(8,128)(2,1)}, u32[]{:S(2)}, u32[]{:S(2)}) collective-permute-start(bf16[2,192,4096]{2,1,0:T(8,128)(2,1)} %get-tuple-element.110), channel_id=1, source_target_pairs={{0,8},{4,12},{8,0},{12,4},{16,24},{20,28},{24,16},{28,20},{1,9},{5... | collective-permute-start | bytes 9437192 | tf_op jit(solution)/shard_map/ppermute | solution.py:32
  744.0 71.6 %collective-permute-start.20 = (bf16[2,192,768]{2,1,0:T(8,128)(2,1)S(1)}, bf16[2,192,768]{2,1,0:T(8,128)(2,1)S(1)}, u32[]{:S(2)}, u32[]{:S(2)}) collective-permute-start(bf16[2,192,768]{2,1,0:T(8,128)(2,1)S(1)} %copy-done.14), channel_id=1, source_target_pairs={{0,16},{4,20},{8,24},{12,28},{16,0},{20,4},{24,8},{28,12},{1,17},{... | collective-permute-start | bytes 1769480 | tf_op jit(solution)/shard_map/ppermute | solution.py:32
  752.6 72.4 %collective-permute-start.21 = (bf16[2,192,768]{2,1,0:T(8,128)(2,1)S(1)}, bf16[2,192,768]{2,1,0:T(8,128)(2,1)S(1)}, u32[]{:S(2)}, u32[]{:S(2)}) collective-permute-start(bf16[2,192,768]{2,1,0:T(8,128)(2,1)S(1)} %copy-done.12), channel_id=1, source_target_pairs={{0,8},{4,12},{8,0},{12,4},{16,24},{20,28},{24,16},{28,20},{1,9},{5... | collective-permute-start | bytes 1769480 | tf_op jit(solution)/shard_map/ppermute | solution.py:32
  842.3 88.4 %collective-permute-start.26 = (bf16[3,384,384]{2,1,0:T(8,128)(2,1)S(1)}, bf16[3,384,384]{2,1,0:T(8,128)(2,1)S(1)}, u32[]{:S(2)}, u32[]{:S(2)}) collective-permute-start(bf16[3,384,384]{2,1,0:T(8,128)(2,1)S(1)} %get-tuple-element.199), channel_id=1, source_target_pairs={{0,1},{1,0},{2,3},{3,2},{4,5},{5,4},{6,7},{7,6},{8,9},{9,8},{10,11... | collective-permute-start | bytes 2654216 | tf_op jit(solution)/shard_map/ppermute | solution.py:32
  843.7 87.0 %collective-permute-start.27 = (bf16[3,384,384]{2,1,0:T(8,128)(2,1)S(1)}, bf16[3,384,384]{2,1,0:T(8,128)(2,1)S(1)}, u32[]{:S(2)}, u32[]{:S(2)}) collective-permute-start(bf16[3,384,384]{2,1,0:T(8,128)(2,1)S(1)} %get-tuple-element.198), channel_id=1, source_target_pairs={{0,2},{1,3},{2,0},{3,1},{4,6},{5,7},{6,4},{7,5},{8,10},{9,11},{10,... | collective-permute-start | bytes 2654216 | tf_op jit(solution)/shard_map/ppermute | solution.py:32
  845.3 85.4 %collective-permute-start.28 = (bf16[3,384,384]{2,1,0:T(8,128)(2,1)S(1)}, bf16[3,384,384]{2,1,0:T(8,128)(2,1)S(1)}, u32[]{:S(2)}, u32[]{:S(2)}) collective-permute-start(bf16[3,384,384]{2,1,0:T(8,128)(2,1)S(1)} %get-tuple-element.197), channel_id=1, source_target_pairs={{0,3},{1,2},{2,1},{3,0},{4,7},{5,6},{6,5},{7,4},{8,11},{9,10},{10,... | collective-permute-start | bytes 2654216 | tf_op jit(solution)/shard_map/ppermute | solution.py:32
  846.0 78.6 %collective-permute-start.53 = (bf16[48,768]{1,0:T(8,128)(2,1)S(1)}, bf16[48,768]{1,0:T(8,128)(2,1)S(1)}, u32[]{:S(2)}, u32[]{:S(2)}) collective-permute-start(bf16[48,768]{1,0:T(8,128)(2,1)S(1)} %get-tuple-element.237), channel_id=1, source_target_pairs={{0,3},{1,2},{2,1},{3,0},{4,7},{5,6},{6,5},{7,4},{8,11},{9,10},{10,... | collective-permute-start | bytes 221192 | tf_op jit(solution)/shard_map/ppermute | solution.py:32
  847.6 77.1 %collective-permute-start.55 = (bf16[48,768]{1,0:T(8,128)(2,1)S(1)}, bf16[48,768]{1,0:T(8,128)(2,1)S(1)}, u32[]{:S(2)}, u32[]{:S(2)}) collective-permute-start(bf16[48,768]{1,0:T(8,128)(2,1)S(1)} %get-tuple-element.239), channel_id=1, source_target_pairs={{0,1},{1,0},{2,3},{3,2},{4,5},{5,4},{6,7},{7,6},{8,9},{9,8},{10,11... | collective-permute-start | bytes 221192 | tf_op jit(solution)/shard_map/ppermute | solution.py:32
  955.8 35.9 %collective-permute-start.62 = (bf16[1,192,4096]{2,1,0:T(8,128)(2,1)}, bf16[1,192,4096]{2,1,0:T(8,128)(2,1)}, u32[]{:S(2)}, u32[]{:S(2)}) collective-permute-start(bf16[1,192,4096]{2,1,0:T(8,128)(2,1)} %slice.227), channel_id=1, source_target_pairs={{0,16},{4,20},{8,24},{12,28},{16,0},{20,4},{24,8},{28,12},{1,17},{... | collective-permute-start | bytes 4718600 | tf_op jit(solution)/shard_map/ppermute | solution.py:32
  959.3 53.9 %collective-permute-start.38 = (bf16[384,4608]{1,0:T(8,128)(2,1)}, bf16[384,4608]{1,0:T(8,128)(2,1)}, u32[]{:S(2)}, u32[]{:S(2)}) collective-permute-start(bf16[384,4608]{1,0:T(8,128)(2,1)} %reshape.196.r_ref), channel_id=1, source_target_pairs={{0,4},{4,0},{8,12},{12,8},{16,20},{20,16},{24,28},{28,24},{1,5},{5... | collective-permute-start | bytes 10616840 | tf_op jit(solution)/shard_map/ppermute | solution.py:32
  995.1 51.5 %collective-permute-start.61 = (bf16[48,4096]{1,0:T(8,128)(2,1)S(1)}, bf16[48,4096]{1,0:T(8,128)(2,1)S(1)}, u32[]{:S(2)}, u32[]{:S(2)}) collective-permute-start(bf16[48,4096]{1,0:T(8,128)(2,1)S(1)} %get-tuple-element.205), channel_id=1, source_target_pairs={{0,3},{1,2},{2,1},{3,0},{4,7},{5,6},{6,5},{7,4},{8,11},{9,10},{10,... | collective-permute-start | bytes 1179656 | tf_op jit(solution)/shard_map/ppermute | solution.py:32
  996.6 51.8 %collective-permute-start.63 = (bf16[48,4096]{1,0:T(8,128)(2,1)S(1)}, bf16[48,4096]{1,0:T(8,128)(2,1)S(1)}, u32[]{:S(2)}, u32[]{:S(2)}) collective-permute-start(bf16[48,4096]{1,0:T(8,128)(2,1)S(1)} %get-tuple-element.207), channel_id=1, source_target_pairs={{0,1},{1,0},{2,3},{3,2},{4,5},{5,4},{6,7},{7,6},{8,9},{9,8},{10,11... | collective-permute-start | bytes 1179656 | tf_op jit(solution)/shard_map/ppermute | solution.py:32
  1013.2 40.0 %collective-permute-start.64 = (bf16[48,4096]{1,0:T(8,128)(2,1)S(1)}, bf16[48,4096]{1,0:T(8,128)(2,1)}, u32[]{:S(2)}, u32[]{:S(2)}) collective-permute-start(bf16[48,4096]{1,0:T(8,128)(2,1)S(1)} %get-tuple-element.209), channel_id=1, source_target_pairs={{0,2},{1,3},{2,0},{3,1},{4,6},{5,7},{6,4},{7,5},{8,10},{9,11},{10,... | collective-permute-start | bytes 1179656 | tf_op jit(solution)/shard_map/ppermute | solution.py:32
  1020.5 42.5 %collective-permute-start.65 = (bf16[48,4096]{1,0:T(8,128)(2,1)S(1)}, bf16[48,4096]{1,0:T(8,128)(2,1)S(1)}, u32[]{:S(2)}, u32[]{:S(2)}) collective-permute-start(bf16[48,4096]{1,0:T(8,128)(2,1)S(1)} %get-tuple-element.208), channel_id=1, source_target_pairs={{0,3},{1,2},{2,1},{3,0},{4,7},{5,6},{6,5},{7,4},{8,11},{9,10},{10,... | collective-permute-start | bytes 1179656 | tf_op jit(solution)/shard_map/ppermute | solution.py:32
  1022.0 42.2 %collective-permute-start.40 = (bf16[2,192,2304]{2,1,0:T(8,128)(2,1)S(1)}, bf16[2,192,2304]{2,1,0:T(8,128)(2,1)S(1)}, u32[]{:S(2)}, u32[]{:S(2)}) collective-permute-start(bf16[2,192,2304]{2,1,0:T(8,128)(2,1)S(1)} %get-tuple-element.123), channel_id=1, source_target_pairs={{0,16},{4,20},{8,24},{12,28},{16,0},{20,4},{24,8},{28,12},{1,17},{... | collective-permute-start | bytes 5308424 | tf_op jit(solution)/shard_map/ppermute | solution.py:32
  1047.9 43.7 %collective-permute-start.45 = (bf16[2,192,2432]{2,1,0:T(8,128)(2,1)S(1)}, bf16[2,192,2432]{2,1,0:T(8,128)(2,1)S(1)}, u32[]{:S(2)}, u32[]{:S(2)}) collective-permute-start(bf16[2,192,2432]{2,1,0:T(8,128)(2,1)S(1)} %get-tuple-element.125), channel_id=1, source_target_pairs={{0,8},{4,12},{8,0},{12,4},{16,24},{20,28},{24,16},{28,20},{1,9},{5... | collective-permute-start | bytes 5603336 | tf_op jit(solution)/shard_map/ppermute | solution.py:32
  1064.8 44.1 %collective-permute-start.41 = (bf16[1,192,2304]{2,1,0:T(8,128)(2,1)S(1)}, bf16[1,192,2304]{2,1,0:T(8,128)(2,1)S(1)}, u32[]{:S(2)}, u32[]{:S(2)}) collective-permute-start(bf16[1,192,2304]{2,1,0:T(8,128)(2,1)S(1)} %slice.235), channel_id=1, source_target_pairs={{0,8},{4,12},{8,0},{12,4},{16,24},{20,28},{24,16},{28,20},{1,9},{5... | collective-permute-start | bytes 2654216 | tf_op jit(solution)/shard_map/ppermute | solution.py:32
  (119 other events, 1785.0 us)
Sparse Core Ops, SparseCore 0:
  328.6 124.0 all-gather.1

commit v2 on v1

v2 whole, which is shorter than its diff:
```python
import functools
import itertools

import jax
import jax.numpy as jnp
from jax import lax
from jax.experimental import pallas as pl
from jax.experimental.pallas import tpu as pltpu
from jax.sharding import PartitionSpec as P

EPSILON = 1e-05
NEG = -1e30
HIGHEST = lax.Precision.HIGHEST
MESH = pl.DeviceIdType.MESH
F32 = jnp.float32
BF16 = jnp.bfloat16


def flip_bit(value, bit):
    return value + bit - 2 * bit * ((value // bit) % 2)


def flip(value, mask):
    bit = 1
    while bit <= mask:
        if mask & bit:
            value = flip_bit(value, bit)
        bit *= 2
    return value


def swap(value, axis, mask):
    return lax.ppermute(value, axis, [(i, i ^ mask) for i in range(lax.axis_size(axis))])


def gather_parts(shapes):
    return [(w, h) for w, s in enumerate(shapes) for h in (0, 1) if h == 0 or s[1] % 256 == 0]


class Gather:
    def __init__(self, ins, outs, send_sem, recv_sem, local_sem, n_fsdp, n_grp):
        self.ins, self.outs = ins, outs
        self.send_sem, self.recv_sem = send_sem, recv_sem
        self.f, self.z, self.n_grp = lax.axis_index("fsdp"), lax.axis_index("grp"), n_grp
        self.bits = [1 << i for i in range(1, n_fsdp.bit_length() - 1)]
        self.parts = gather_parts([r.shape for r in ins])
        self.orders = [self.bits if h == 0 else self.bits[::-1] for _, h in self.parts]
        self.across = {b: {"fsdp": flip(self.f, b), "grp": self.z} for b in self.bits + [1]}
        self.up = {"fsdp": self.f, "grp": self.z + 1}
        self.down = {"fsdp": self.f, "grp": self.z - 1}
        self.count, self.sent, self.local = 0, [], []
        for w in range(len(ins)):
            self.local.append(
                pltpu.make_async_copy(
                    ins[w], outs[w].at[self.f * n_grp + self.z], local_sem.at[w]
                )
            )
        self.steps = self._steps()

    def _columns(self, part):
        w, h = self.parts[part]
        width = self.ins[w].shape[1]
        return pl.ds(0, width) if width % 256 else pl.ds(h * (width // 2), width // 2)

    def _piece(self, part, fk, place):
        row = flip(self.f, fk) * self.n_grp + place
        return self.outs[self.parts[part][0]].at[row, :, self._columns(part)]

    def _send(self, part, fk, place, to, to_fk, own=False):
        index = self.count
        self.count += 1

        def copy():
            source = self._piece(part, fk, place)
            if own:
                source = self.ins[self.parts[part][0]].at[:, self._columns(part)]
            return pltpu.make_async_remote_copy(
                src_ref=source,
                dst_ref=self._piece(part, fk, place),
                send_sem=self.send_sem.at[index],
                recv_sem=self.recv_sem.at[part, to_fk, place],
                device_id=to,
                device_id_type=MESH,
            )

        copy().start()
        return copy

    def _wait(self, part, fk, place):
        piece = self._piece(part, fk, place)
        pltpu.make_async_remote_copy(
            src_ref=piece,
            dst_ref=piece,
            send_sem=self.send_sem.at[0],
            recv_sem=self.recv_sem.at[part, fk, place],
            device_id=self.across[1],
            device_id_type=MESH,
        ).wait_recv()

    def _forward(self, part, stage, fk, place, own=False):
        return [
            self._send(part, fk, place, self.across[b], fk ^ b, own)
            for b in self.orders[part][stage:] + [1]
        ]

    def _when(self, condition, action):
        copies = []
        pl.when(condition)(lambda: copies.extend(action()))
        self.sent.append((condition, copies))

    def start(self):
        for copy in self.local:
            copy.start()
        last = self.n_grp - 1
        for part in range(len(self.parts)):
            self._when(
                self.z < last, lambda: [self._send(part, 0, self.z, self.up, 0, True)]
            )
            self._when(self.z > 0, lambda: [self._send(part, 0, self.z, self.down, 0, True)])
            self.sent.append((None, self._forward(part, 0, 0, self.z, True)))

    def _line_step(self, part, j):
        z, last = self.z, self.n_grp - 1
        below, above = z - j, z + j

        def arrive(place):
            self._wait(part, 0, place)
            return self._forward(part, 0, 0, place)

        self._when(z >= j, lambda: arrive(below))
        if j < last:
            self._when(
                jnp.logical_and(z >= j, z < last),
                lambda: [self._send(part, 0, below, self.up, 0)],
            )
        self._when(above <= last, lambda: arrive(above))
        if j < last:
            self._when(
                jnp.logical_and(above <= last, z > 0),
                lambda: [self._send(part, 0, above, self.down, 0)],
            )

    def _cross_step(self, part, stage, fk, place):
        self._wait(part, fk, place)
        self.sent.append((None, self._forward(part, stage + 1, fk, place)))

    def _steps(self):
        count = len(self.parts)
        steps = []
        for j in range(1, self.n_grp):
            for part in range(count):
                steps.append(functools.partial(self._line_step, part, j))
        have = [[0] for _ in range(count)]
        for stage in range(len(self.bits)):
            for a in range(len(have[0])):
                for place in range(self.n_grp):
                    for part in range(count):
                        fk = have[part][a] ^ self.orders[part][stage]
                        steps.append(
                            functools.partial(self._cross_step, part, stage, fk, place)
                        )
            have = [
                known + [v ^ self.orders[part][stage] for v in known]
                for part, known in enumerate(have)
            ]
        for a in range(len(have[0])):
            for place in range(self.n_grp):
                for part in range(count):
                    steps.append(functools.partial(self._wait, part, have[part][a] ^ 1, place))
        return steps

    def run(self, until=None):
        done = len(self.all_steps) - len(self.steps) if hasattr(self, "all_steps") else 0
        if done == 0:
            self.all_steps = list(self.steps)
        stop = len(self.all_steps) if until is None else int(until * len(self.all_steps))
        for step in self.all_steps[done:stop]:
            step()
        self.steps = self.all_steps[max(stop, done) :]

    def finish(self):
        self.run()
        for copy in self.local:
            copy.wait()
        for condition, copies in self.sent:
            if condition is None:
                for copy in copies:
                    copy().wait_send()
            else:

                def wait_sent():
                    for copy in copies:
                        copy().wait_send()

                pl.when(condition)(wait_sent)


def gather_scratch(weights, n_fsdp, n_grp):
    parts = len(gather_parts([w.shape for w in weights]))
    bits = n_fsdp.bit_length() - 2
    crossing = n_fsdp // 2 - 1 + n_fsdp // 2
    sends = 2 + (n_grp - 1) * 2 * (bits + 1) + 2 * (n_grp - 2) + n_grp * crossing + bits + 1
    return [
        pltpu.SemaphoreType.DMA((parts * sends,)),
        pltpu.SemaphoreType.DMA((parts, n_fsdp, n_grp)),
        pltpu.SemaphoreType.DMA((len(weights),)),
    ]


def gathered(weights, n_fsdp, n_grp):
    return [jax.ShapeDtypeStruct((n_fsdp * n_grp,) + w.shape, w.dtype) for w in weights]


def meet(n_fsdp, n_grp, line_only):
    f, z = lax.axis_index("fsdp"), lax.axis_index("grp")
    barrier = pltpu.get_barrier_semaphore()
    bits = [1 << i for i in range(n_fsdp.bit_length() - 1)]
    peers = [{"fsdp": flip(f, b), "grp": z} for b in bits]
    peers += [{"fsdp": f, "grp": flip(z, k)} for k in range(1, n_grp)]
    for peer in peers:
        pl.semaphore_signal(barrier, inc=1, device_id=peer, device_id_type=MESH)
    pl.semaphore_wait(barrier, len(peers))


def gather_kernel(count, n_fsdp, n_grp, *refs):
    meet(n_fsdp, n_grp, True)
    gather = Gather(refs[:count], refs[count : 2 * count], *refs[2 * count :], n_fsdp, n_grp)
    gather.start()
    gather.finish()


def gather_rows(weights, collective_id):
    n_fsdp, n_grp = lax.axis_size("fsdp"), lax.axis_size("grp")
    count = len(weights)
    full = pl.pallas_call(
        functools.partial(gather_kernel, count, n_fsdp, n_grp),
        out_shape=gathered(weights, n_fsdp, n_grp),
        in_specs=[pl.BlockSpec(memory_space=pl.ANY)] * count,
        out_specs=[pl.BlockSpec(memory_space=pl.ANY)] * count,
        scratch_shapes=gather_scratch(weights, n_fsdp, n_grp),
        compiler_params=pltpu.CompilerParams(
            collective_id=collective_id, has_side_effects=True
        ),
        name="gather_rows",
    )(*weights)
    return [v.reshape(-1, v.shape[2]) for v in full]


def dot_lanes(a, b):
    return lax.dot_general(a, b, (((1,), (1,)), ((), ())), preferred_element_type=F32)


def dot_rows(a, b):
    return lax.dot_general(a, b, (((0,), (0,)), ((), ())), preferred_element_type=F32)


def seen_blocks(block):
    if block == 0:
        return [(0, 0)]
    if block == 1:
        return [(0, None), (1, 0)]
    return [(0, None), (1, None), (block, block - 1)]


def column(values, index):
    lanes = lax.broadcasted_iota(jnp.int32, (1, values.shape[1]), 1)
    return jnp.sum(jnp.where(lanes == index, values, 0.0), axis=1, keepdims=True)


def pick(slots_ref, place, by_block):
    result = by_block[0]
    for block in range(1, len(by_block)):
        here = jnp.full((1, result.shape[1]), slots_ref[block], jnp.int32) == place
        result = jnp.where(here, by_block[block], result)
    return result


def attend_pair(pair, blocks, head_size, slots_ref, x_ref, c_ref, mask_ref, o_ref, lse_ref):
    scale = head_size**-0.5

    def head(h, carry):
        lanes = lax.broadcasted_iota(jnp.int32, (1, 2 * head_size), 1)
        mine = lanes // head_size == h
        decays = [column(c_ref[b], 2 * pair + h) for b in range(blocks)]
        outs = []
        for block in range(blocks):
            query = jnp.where(mine, x_ref[slots_ref[block], 0] * scale, 0).astype(BF16)
            scores = []
            for other, mask in seen_blocks(block):
                s = dot_lanes(x_ref[slots_ref[other], 1], query) - decays[other]
                if mask is not None:
                    s = s + mask_ref[mask]
                scores.append(s)
            top = functools.reduce(
                jnp.maximum, [jnp.max(s, axis=0, keepdims=True) for s in scores]
            )
            total, mixed = 0.0, 0.0
            for s, (other, _) in zip(scores, seen_blocks(block)):
                weight = jnp.exp(s - top)
                total = total + jnp.sum(weight, axis=0, keepdims=True)
                mixed = mixed + dot_rows(x_ref[slots_ref[other], 2], weight.astype(BF16))
            lse_ref[pair, h, pl.ds(block, 1), :] = top + jnp.log(total)
            outs.append((mixed / total).T.astype(BF16))
        for place in range(blocks):
            o_ref[place] = jnp.where(mine, pick(slots_ref, place, outs), o_ref[place])
        return carry

    lax.fori_loop(0, 2, head, 0)


def sum_decay(blocks, slots_ref, log_ref, seen_ref, c_ref):
    total = 0.0
    for block in range(blocks):
        logs = log_ref[slots_ref[block]]
        high = logs.astype(BF16)
        rest = logs - high.astype(F32)
        middle = rest.astype(BF16)
        low = (rest - middle.astype(F32)).astype(BF16)
        seen = seen_ref[max(block - 1, 0)]
        local = dot_lanes(seen, high) + dot_lanes(seen, middle) + dot_lanes(seen, low)
        c_ref[block] = local + total if block < 2 else local
        if block == 0:
            total = local[local.shape[0] - 1 :, :]


class GroupExchange:
    def __init__(self, n_grp, send_sem, recv_sem):
        self.n_grp, self.send_sem, self.recv_sem = n_grp, send_sem, recv_sem
        self.f, self.z = lax.axis_index("fsdp"), lax.axis_index("grp")
        self.sent, self.landed = [], {}

    def send(self, key, index, source_of, target):
        self.landed[key] = (index, target)
        for k in range(1, self.n_grp):
            place = flip(self.z, k)
            copy = pltpu.make_async_remote_copy(
                src_ref=source_of(place),
                dst_ref=target(self.z),
                send_sem=self.send_sem.at[index, k],
                recv_sem=self.recv_sem.at[index, k],
                device_id={"fsdp": self.f, "grp": place},
                device_id_type=MESH,
            )
            copy.start()
            self.sent.append(copy)

    def wait(self, key):
        index, target = self.landed[key]
        for k in range(1, self.n_grp):
            place = flip(self.z, k)
            pltpu.make_async_remote_copy(
                src_ref=target(place),
                dst_ref=target(place),
                send_sem=self.send_sem.at[index, k],
                recv_sem=self.recv_sem.at[index, k],
                device_id={"fsdp": self.f, "grp": place},
                device_id_type=MESH,
            ).wait_recv()

    def finish(self):
        for copy in self.sent:
            copy.wait_send()


def forward_kernel(count, pairs, head_size, n_fsdp, n_grp, *refs):
    weights, refs = refs[:count], refs[count:]
    slots_ref, mixed_ref, log_ref, mask_ref, seen_ref = refs[:5]
    full, refs = refs[5 : 5 + count], refs[5 + count :]
    o_out, x_out, lse_ref, c_ref = refs[:4]
    gather_sems, refs = refs[4:7], refs[7:]
    x_refs, refs = refs[:pairs], refs[pairs:]
    o_refs, refs = refs[:pairs], refs[pairs:]
    logs_ref, send_sem, recv_sem, copy_sem = refs
    blocks = n_grp
    pair_width = 2 * head_size
    group_width = pairs * pair_width
    width = blocks * group_width
    z = lax.axis_index("grp")

    meet(n_fsdp, n_grp, False)
    gather = Gather(weights, full, *gather_sems, n_fsdp, n_grp)
    swap_heads = GroupExchange(n_grp, send_sem, recv_sem)
    started = itertools.count()

    def keep(source, target):
        copy = pltpu.make_async_copy(source, target, copy_sem.at[next(started)])
        copy.start()
        return copy

    def heads_of(part, place, pair):
        start = part * width + place * group_width + pair * pair_width
        return mixed_ref.at[:, pl.ds(pl.multiple_of(start, 128), pair_width)]

    own_logs = keep(log_ref.at[z], logs_ref.at[z])
    swap_heads.send("logs", 0, lambda place: log_ref.at[place], lambda place: logs_ref.at[place])
    own, late = [], []
    for pair in range(pairs):
        for part in range(3):
            swap_heads.send(
                (pair, part),
                1 + 4 * pair + part,
                lambda place, pair=pair, part=part: heads_of(part, place, pair),
                lambda place, pair=pair, part=part: x_refs[pair].at[place, part],
            )
            own.append(keep(heads_of(part, z, pair), x_refs[pair].at[z, part]))
        if pair == 0:
            gather.start()
    gather.run(0.1)
    own_logs.wait()
    swap_heads.wait("logs")
    sum_decay(blocks, slots_ref, logs_ref, seen_ref, c_ref)
    for pair in range(pairs):
        gather.run(0.16 + 0.12 * pair)
        for part in range(3):
            own[3 * pair + part].wait()
            swap_heads.wait((pair, part))
        attend_pair(
            pair, blocks, head_size, slots_ref, x_refs[pair], c_ref, mask_ref, o_refs[pair], lse_ref
        )
        late.append(keep(x_refs[pair], x_out.at[pair]))

        def columns(place, pair=pair):
            start = place * group_width + pair * pair_width
            return o_out.at[:, pl.ds(pl.multiple_of(start, 128), pair_width)]

        swap_heads.send(
            (pair, 3), 4 + 4 * pair, lambda place: o_refs[pair].at[place], columns
        )
        late.append(keep(o_refs[pair].at[z], columns(z)))
    gather.finish()
    for pair in range(pairs):
        swap_heads.wait((pair, 3))
    swap_heads.finish()
    for copy in late:
        copy.wait()


def forward_attention(weights, slots, mixed, logs, masks, seen, head_size, collective_id):
    n_fsdp, n_grp = lax.axis_size("fsdp"), lax.axis_size("grp")
    count = len(weights)
    tok, width = mixed.shape[0], mixed.shape[1] // 3
    pair_width = 2 * head_size
    pairs = width // n_grp // pair_width
    anywhere = pl.BlockSpec(memory_space=pl.ANY)
    vmem = pl.BlockSpec(memory_space=pltpu.VMEM)
    out = pl.pallas_call(
        functools.partial(forward_kernel, count, pairs, head_size, n_fsdp, n_grp),
        out_shape=gathered(weights, n_fsdp, n_grp)
        + [
            jax.ShapeDtypeStruct((tok, width), BF16),
            jax.ShapeDtypeStruct((pairs, n_grp, 3, tok, pair_width), BF16),
            jax.ShapeDtypeStruct((pairs, 2, 8, tok), F32),
            jax.ShapeDtypeStruct((n_grp, tok, logs.shape[1]), F32),
        ],
        in_specs=[anywhere] * count
        + [pl.BlockSpec(memory_space=pltpu.SMEM), anywhere, anywhere, vmem, vmem],
        out_specs=[anywhere] * count + [anywhere, anywhere, vmem, vmem],
        scratch_shapes=gather_scratch(weights, n_fsdp, n_grp)
        + [pltpu.VMEM((n_grp, 3, tok, pair_width), BF16)] * pairs
        + [pltpu.VMEM((n_grp, tok, pair_width), BF16)] * pairs
        + [
            pltpu.VMEM(logs.shape, F32),
            pltpu.SemaphoreType.DMA((1 + 4 * pairs, n_grp)),
            pltpu.SemaphoreType.DMA((1 + 4 * pairs, n_grp)),
            pltpu.SemaphoreType.DMA((1 + 5 * pairs,)),
        ],
        compiler_params=pltpu.CompilerParams(
            collective_id=collective_id, has_side_effects=True, vmem_limit_bytes=48 << 20
        ),
        name="forward_attention",
    )(*weights, slots, mixed, logs, masks, seen)
    return [v.reshape(-1, v.shape[2]) for v in out[:count]], out[count:]


def attend_back_pair(
    pair,
    blocks,
    head_size,
    slots_ref,
    x_ref,
    do_ref,
    c_ref,
    mask_ref,
    lse_ref,
    dx_ref,
    query_decay_ref,
    key_decay_ref,
):
    scale = head_size**-0.5

    def head(h, carry):
        lanes = lax.broadcasted_iota(jnp.int32, (1, 2 * head_size), 1)
        mine = lanes // head_size == h
        index = 2 * pair + h
        mine_decay = lax.broadcasted_iota(jnp.int32, (1, c_ref.shape[2]), 1) == index
        decays = [column(c_ref[b], index) for b in range(blocks)]
        query_grads = [None] * blocks
        key_grads, value_grads = [None] * blocks, [None] * blocks
        decay_grads = [None] * blocks

        def add(store, at, value):
            store[at] = value if store[at] is None else store[at] + value

        for block in range(blocks):
            query = jnp.where(mine, x_ref[slots_ref[block], 0] * scale, 0).astype(BF16)
            grad_o = jnp.where(mine, do_ref[slots_ref[block]], 0).astype(BF16)
            lse = lse_ref[pair, h, pl.ds(block, 1), :]
            weights, grads, delta = [], [], 0.0
            for other, mask in seen_blocks(block):
                s = dot_lanes(x_ref[slots_ref[other], 1], query) - decays[other]
                if mask is not None:
                    s = s + mask_ref[mask]
                weight = jnp.exp(s - lse)
                grad = dot_lanes(x_ref[slots_ref[other], 2], grad_o)
                delta = delta + jnp.sum(weight * grad, axis=0, keepdims=True)
                weights.append(weight)
                grads.append(grad)
            query_grad, query_decay = 0.0, 0.0
            for weight, grad, (other, _) in zip(weights, grads, seen_blocks(block)):
                ds = weight * (grad - delta)
                query_decay = query_decay + jnp.sum(ds, axis=0, keepdims=True)
                add(decay_grads, other, jnp.sum(ds, axis=1, keepdims=True))
                low = ds.astype(BF16)
                query_grad = query_grad + dot_rows(x_ref[slots_ref[other], 1], low)
                add(key_grads, other, jnp.dot(low, query, preferred_element_type=F32))
                add(
                    value_grads,
                    other,
                    jnp.dot(weight.astype(BF16), grad_o, preferred_element_type=F32),
                )
            query_grads[block] = (query_grad * scale).T
            turned = jnp.broadcast_to(query_decay, (c_ref.shape[2], query_decay.shape[1])).T
            query_decay_ref[block] = jnp.where(mine_decay, turned, query_decay_ref[block])
        for block in range(blocks):
            key_decay_ref[block] = jnp.where(
                mine_decay, decay_grads[block], key_decay_ref[block]
            )
        for part, by_block in enumerate((query_grads, key_grads, value_grads)):
            low = [v.astype(BF16) for v in by_block]
            for place in range(blocks):
                dx_ref[place, part] = jnp.where(
                    mine, pick(slots_ref, place, low), dx_ref[place, part]
                )
        return carry

    lax.fori_loop(0, 2, head, 0)


def split3(values):
    high = values.astype(BF16)
    rest = values - high.astype(F32)
    middle = rest.astype(BF16)
    return high, middle, (rest - middle.astype(F32)).astype(BF16)


def sum_decay_back(blocks, slots_ref, seen_ref, query_decay_ref, key_decay_ref, logs_ref):
    after = 0.0
    for block in range(2, blocks):
        after = after + jnp.sum(query_decay_ref[block], axis=0, keepdims=True)
    by_block = [None] * blocks
    for block in reversed(range(blocks)):
        grad = query_decay_ref[block] - key_decay_ref[block]
        seen = seen_ref[max(block - 1, 0)]
        value = sum(dot_rows(seen, part) for part in split3(grad))
        by_block[block] = value if block >= 2 else value + after
        if block == 1:
            after = after + jnp.sum(grad, axis=0, keepdims=True)
    for place in range(blocks):
        logs_ref[place] = pick(slots_ref, place, by_block)


def halving_orders(n_fsdp):
    bits = [1 << i for i in range(n_fsdp.bit_length() - 2)]
    return bits[::-1], bits


def kept_pieces(order):
    keep = [0]
    for bit in reversed(order[1:]):
        keep = keep + [k ^ bit for k in keep]
    return keep


class Scatter:
    AHEAD = 6

    def __init__(self, parts, send_sem, recv_sem, line_sem, local_sem, n_fsdp, n_grp):
        self.parts, self.n_grp = parts, n_grp
        self.send_sem, self.recv_sem = send_sem, recv_sem
        self.line_sem, self.local_sem = line_sem, local_sem
        self.f, self.z = lax.axis_index("fsdp"), lax.axis_index("grp")
        orders = halving_orders(n_fsdp)
        self.orders = [orders[i % 2] for i in range(len(parts))]
        self.keeps = [kept_pieces(o) for o in self.orders]
        self.up = {"fsdp": self.f, "grp": self.z + 1}
        self.down = {"fsdp": self.f, "grp": self.z - 1}
        self.across = {b: {"fsdp": flip(self.f, 2 * b), "grp": self.z} for b in orders[1]}
        self.sent, self.count = [], [0] * len(parts)

    def stage_of(self, part, k):
        order = self.orders[part]
        return next((i for i, b in enumerate(order) if k & b), len(order))

    def slot(self, part, k, stage):
        slots = [(v, j) for v in self.keeps[part] for j in range(self.stage_of(part, v))]
        return slots.index((k, stage))

    def _send(self, part, source, target, recv_sem, to):
        index = self.count[part]
        self.count[part] += 1

        def copy():
            return pltpu.make_async_remote_copy(
                src_ref=source(),
                dst_ref=target(),
                send_sem=self.send_sem.at[part, index],
                recv_sem=recv_sem(),
                device_id=to,
                device_id_type=MESH,
            )

        copy().start()
        return copy

    def _cross(self, part, place, k, stage, source):
        bit = self.orders[part][stage]
        slot = self.slot(part, k ^ bit, stage)
        copy = self._send(
            part,
            lambda: source,
            lambda: self.parts[part][3].at[slot, place],
            lambda: self.recv_sem.at[part, slot, place],
            self.across[bit],
        )
        self.sent.append((None, [copy]))

    def _arrived(self, target, recv_sem):
        pltpu.make_async_remote_copy(
            src_ref=target,
            dst_ref=target,
            send_sem=self.send_sem.at[0, 0],
            recv_sem=recv_sem,
            device_id=self.across[1],
            device_id_type=MESH,
        ).wait_recv()

    def _load(self, part, place, i):
        kept, held = self.parts[part][1:3]
        return pltpu.make_async_copy(
            kept.at[i, place], held.at[i, place], self.local_sem.at[part, i, place]
        )

    def _begin(self, part, place):
        away = self.parts[part][0]
        for i, k in reversed(list(enumerate(self.keeps[part]))):
            self._cross(part, place, k ^ self.orders[part][0], 0, away.at[i, place])
            self._load(part, place, i).start()

    def _add_arrived(self, part, place, k):
        held, arrived = self.parts[part][2], self.parts[part][3]
        i = self.keeps[part].index(k)
        self._load(part, place, i).wait()
        for stage in range(self.stage_of(part, k)):
            slot = self.slot(part, k, stage)
            self._arrived(arrived.at[slot, place], self.recv_sem.at[part, slot, place])
        total = held[i, place]
        for stage in range(self.stage_of(part, k)):
            total = total + arrived[self.slot(part, k, stage), place]
        held[i, place] = total
        return held.at[i, place]

    def _halve(self, part, place, k):
        source = self._add_arrived(part, place, k)
        self._cross(part, place, k, self.stage_of(part, k), source)

    def _when(self, condition, action):
        copies = []
        pl.when(condition)(lambda: copies.extend(action()))
        self.sent.append((condition, copies))

    def _line(self, part, place, hop):
        last = self.n_grp - 1
        held = self.parts[part][2]
        ways = []
        if hop < place:
            ways.append((self.z == hop, 4, 0, self.up))
        if last - hop > place:
            ways.append((self.z == last - hop, 5, 1, self.down))
        for condition, which, way, to in ways:
            passing = self.parts[part][which]

            def action(passing=passing, way=way, to=to):
                target = lambda: passing.at[place]
                sem = lambda: self.line_sem.at[part, way, place]
                if hop == 0:
                    return [self._send(part, lambda: held.at[0, place], target, sem, to)]
                self._arrived(target(), sem())
                passing[place] = passing[place] + held[0, place]
                return [self._send(part, target, target, sem, to)]

            self._when(condition, action)

    def _result(self, part):
        held, below, above, result, columns = (self.parts[part][i] for i in (2, 4, 5, 6, 7))
        z, last = self.z, self.n_grp - 1
        result[:, columns] = held[0, z].astype(F32)

        def add(passing, index):
            self._arrived(passing.at[z], self.line_sem.at[part, index, z])
            result[:, columns] = result[:, columns] + passing[z].astype(F32)

        pl.when(z > 0)(lambda: add(below, 0))
        pl.when(z < last)(lambda: add(above, 1))

    def waves(self):
        bind = functools.partial
        low, high, places = 0, self.n_grp - 1, []
        while low <= high:
            places += [high] if low == high else [high, low]
            low, high = low + 1, high - 1
        units = []
        for first in range(0, len(self.parts), 2):
            group = range(first, min(first + 2, len(self.parts)))
            units += [(part, place) for place in places for part in group]
        ahead, stages = self.AHEAD, len(self.orders[0])
        length = len(units) + ahead + 2 * stages + 2 * self.n_grp
        waves = [[] for _ in range(length)]
        final = {}
        for n, (part, place) in enumerate(units):
            waves[max(0, n + 1 - ahead)].append(bind(self._begin, part, place))
            at = n + 1
            for stage in range(1, stages):
                for k in self.keeps[part]:
                    if self.stage_of(part, k) == stage:
                        waves[at].append(bind(self._halve, part, place, k))
                at += 2
            waves[at].append(bind(self._add_arrived, part, place, 0))
            for hop in range(self.n_grp - 1):
                waves[at + 2 * hop].append(bind(self._line, part, place, hop))
            final[part] = at + 2 * (self.n_grp - 1)
        for part, at in final.items():
            waves[at].append(bind(self._result, part))
        return waves

    def finish(self):
        for condition, copies in self.sent:
            if condition is None:
                for copy in copies:
                    copy().wait_send()
            else:

                def wait_sent():
                    for copy in copies:
                        copy().wait_send()

                pl.when(condition)(wait_sent)


def scatter_scratch(aways, n_fsdp, n_grp):
    m = n_fsdp.bit_length() - 2
    keep = n_fsdp // 4
    slots = m + sum(i << (m - 1 - i) for i in range(1, m))
    parts = len(aways)
    shapes = [
        pltpu.SemaphoreType.DMA((parts, n_grp * (2 * keep + 2 * n_grp))),
        pltpu.SemaphoreType.DMA((parts, slots, n_grp)),
        pltpu.SemaphoreType.DMA((parts, 2, n_grp)),
        pltpu.SemaphoreType.DMA((parts, keep, n_grp)),
    ]
    for away in aways:
        rows, width = away.shape[2:]
        for leading in ((keep, n_grp), (slots, n_grp), (n_grp,), (n_grp,)):
            shapes.append(pltpu.VMEM(leading + (rows, width), BF16))
    return shapes


def scatter_parts(aways, kepts, buffers, results):
    parts = []
    places = [(ref, columns) for ref, ranges in results for columns in ranges]
    for i, (away, kept) in enumerate(zip(aways, kepts)):
        parts.append((away, kept, *buffers[4 * i : 4 * i + 4], *places[i]))
    return parts


def column_ranges(widths):
    start, ranges = 0, []
    for width in widths:
        ranges.append(pl.ds(start, width))
        start += width
    return ranges


def scatter_kernel(widths, n_fsdp, n_grp, *refs):
    count = sum(len(w) for w in widths)
    aways, kepts, refs = refs[:count], refs[count : 2 * count], refs[2 * count :]
    results, sems, buffers = refs[: len(widths)], refs[len(widths) :][:4], refs[len(widths) + 4 :]
    meet(n_fsdp, n_grp, True)
    places = [(ref, column_ranges(w)) for ref, w in zip(results, widths)]
    scatter = Scatter(scatter_parts(aways, kepts, buffers, places), *sems, n_fsdp, n_grp)
    for wave in scatter.waves():
        for step in wave:
            step()
    scatter.finish()


def scatter_rows(weights, collective_id):
    n_fsdp, n_grp = lax.axis_size("fsdp"), lax.axis_size("grp")
    aways = [away for parts in weights for away, _ in parts]
    kepts = [kept for parts in weights for _, kept in parts]
    widths = [[away.shape[3] for away, _ in parts] for parts in weights]
    return pl.pallas_call(
        functools.partial(scatter_kernel, widths, n_fsdp, n_grp),
        out_shape=[
            jax.ShapeDtypeStruct((parts[0][0].shape[2], sum(w)), F32)
            for parts, w in zip(weights, widths)
        ],
        in_specs=[pl.BlockSpec(memory_space=pl.ANY)] * (2 * len(aways)),
        out_specs=[pl.BlockSpec(memory_space=pltpu.VMEM)] * len(weights),
        scratch_shapes=scatter_scratch(aways, n_fsdp, n_grp),
        compiler_params=pltpu.CompilerParams(
            collective_id=collective_id, has_side_effects=True, vmem_limit_bytes=58 << 20
        ),
        name="scatter_rows",
    )(*aways, *kepts)


def backward_kernel(widths, pairs, head_size, n_fsdp, n_grp, *refs):
    count = sum(len(w) for w in widths)
    aways, kepts, refs = refs[:count], refs[count : 2 * count], refs[2 * count :]
    slots_ref, grad_ref, x_hbm, c_ref, mask_ref, seen_ref, lse_ref = refs[:7]
    results, refs = refs[7 : 7 + len(widths)], refs[7 + len(widths) :]
    mixed_out, logs_out = refs[:2]
    sems, buffers, refs = refs[2:6], refs[6 : 6 + 4 * count], refs[6 + 4 * count :]
    x_refs, refs = refs[:pairs], refs[pairs:]
    do_refs, refs = refs[:pairs], refs[pairs:]
    dx_refs, refs = refs[:pairs], refs[pairs:]
    query_decay_ref, key_decay_ref, logs_ref, send_sem, recv_sem, copy_sem = refs
    blocks = n_grp
    pair_width = 2 * head_size
    group_width = pairs * pair_width
    width = blocks * group_width
    z = lax.axis_index("grp")

    meet(n_fsdp, n_grp, False)
    places = [(ref, column_ranges(w)) for ref, w in zip(results, widths)]
    scatter = Scatter(scatter_parts(aways, kepts, buffers, places), *sems, n_fsdp, n_grp)
    swap_heads = GroupExchange(n_grp, send_sem, recv_sem)
    started = itertools.count()

    def keep(source, target):
        copy = pltpu.make_async_copy(source, target, copy_sem.at[next(started)])
        copy.start()
        return copy

    def heads_of(ref, part, place, pair):
        start = part * width + place * group_width + pair * pair_width
        return ref.at[:, pl.ds(pl.multiple_of(start, 128), pair_width)]

    own, late = [], []
    for pair in range(pairs):
        swap_heads.send(
            (pair, "do"),
            4 * pair,
            lambda place, pair=pair: heads_of(grad_ref, 0, place, pair),
            lambda place, pair=pair: do_refs[pair].at[place],
        )
        own.append(keep(heads_of(grad_ref, 0, z, pair), do_refs[pair].at[z]))
        own.append(keep(x_hbm.at[pair], x_refs[pair]))
    waves = iter(scatter.waves())

    def advance(count=None):
        for wave in itertools.islice(waves, count):
            for step in wave:
                step()

    advance(1)
    for pair in range(pairs):
        own[2 * pair].wait()
        own[2 * pair + 1].wait()
        swap_heads.wait((pair, "do"))
        attend_back_pair(
            pair,
            blocks,
            head_size,
            slots_ref,
            x_refs[pair],
            do_refs[pair],
            c_ref,
            mask_ref,
            lse_ref,
            dx_refs[pair],
            query_decay_ref,
            key_decay_ref,
        )
        for part in range(3):
            swap_heads.send(
                (pair, part),
                1 + 4 * pair + part,
                lambda place, pair=pair, part=part: dx_refs[pair].at[place, part],
                lambda place, pair=pair, part=part: heads_of(mixed_out, part, place, pair),
            )
            late.append(keep(dx_refs[pair].at[z, part], heads_of(mixed_out, part, z, pair)))
        advance(3)
    sum_decay_back(blocks, slots_ref, seen_ref, query_decay_ref, key_decay_ref, logs_ref)
    swap_heads.send(
        "logs",
        4 * pairs,
        lambda place: logs_ref.at[place],
        lambda place: logs_out.at[place],
    )
    late.append(keep(logs_ref.at[z], logs_out.at[z]))
    advance()
    for pair in range(pairs):
        for part in range(3):
            swap_heads.wait((pair, part))
    swap_heads.wait("logs")
    scatter.finish()
    swap_heads.finish()
    for copy in late:
        copy.wait()


def backward_attention(weights, slots, grad, x, decay, masks, seen, lse, head_size, collective_id):
    n_fsdp, n_grp = lax.axis_size("fsdp"), lax.axis_size("grp")
    aways = [away for parts in weights for away, _ in parts]
    kepts = [kept for parts in weights for _, kept in parts]
    widths = [[away.shape[3] for away, _ in parts] for parts in weights]
    pairs, _, _, tok, pair_width = x.shape
    lanes = decay.shape[2]
    anywhere = pl.BlockSpec(memory_space=pl.ANY)
    vmem = pl.BlockSpec(memory_space=pltpu.VMEM)
    out = pl.pallas_call(
        functools.partial(backward_kernel, widths, pairs, head_size, n_fsdp, n_grp),
        out_shape=[
            jax.ShapeDtypeStruct((parts[0][0].shape[2], sum(w)), F32)
            for parts, w in zip(weights, widths)
        ]
        + [
            jax.ShapeDtypeStruct((tok, 3 * grad.shape[1]), BF16),
            jax.ShapeDtypeStruct((n_grp, tok, lanes), F32),
        ],
        in_specs=[anywhere] * (2 * len(aways))
        + [pl.BlockSpec(memory_space=pltpu.SMEM), anywhere, anywhere]
        + [vmem] * 4,
        out_specs=[vmem] * len(weights) + [anywhere] * 2,
        scratch_shapes=scatter_scratch(aways, n_fsdp, n_grp)
        + [pltpu.VMEM((n_grp, 3, tok, pair_width), BF16)] * pairs
        + [pltpu.VMEM((n_grp, tok, pair_width), BF16)] * pairs
        + [pltpu.VMEM((n_grp, 3, tok, pair_width), BF16)] * pairs
        + [pltpu.VMEM((n_grp, tok, lanes), F32)] * 3
        + [
            pltpu.SemaphoreType.DMA((1 + 4 * pairs, n_grp)),
            pltpu.SemaphoreType.DMA((1 + 4 * pairs, n_grp)),
            pltpu.SemaphoreType.DMA((1 + 5 * pairs,)),
        ],
        compiler_params=pltpu.CompilerParams(
            collective_id=collective_id, has_side_effects=True, vmem_limit_bytes=62 << 20
        ),
        name="backward_attention",
    )(*aways, *kepts, slots, grad, x, decay, masks, seen, lse)
    return out[: len(weights)], out[len(weights)], out[len(weights) + 1]


def weight_grad_kernel(count, own_ids, other_ids, l_ref, l_other_ref, r_ref, r_other_ref, *outs):
    def side(ref, ids):
        return jnp.concatenate([ref[ids[k]] for k in range(2 * count)], axis=0)

    total = jnp.dot(side(l_ref, own_ids), r_ref[...], preferred_element_type=F32)
    total = total + jnp.dot(
        side(l_other_ref, other_ids), r_other_ref[...], preferred_element_type=F32
    )
    total = total.astype(BF16).reshape(2 * count, -1, total.shape[1])
    outs[0][...] = total[:count]
    outs[1][...] = total[count:]


def weight_grad(own_ids, other_ids, l_own, l_other, r_own, r_other, start, width):
    count = own_ids.shape[0] // 2
    _, rows, tok = l_own.shape
    limit = 1536 if rows * count < 1024 else 512
    tile = max(t for t in range(128, limit + 1, 128) if width % t == 0 and start % t == 0)
    steps, first = width // tile, start // tile
    whole = lambda v: pl.BlockSpec(v.shape, lambda n, own, other: (0, 0, 0))
    r_spec = pl.BlockSpec((tok, tile), lambda n, own, other: (0, first + n))
    out_spec = pl.BlockSpec((count, rows, tile), lambda n, own, other: (0, 0, n))
    return pl.pallas_call(
        functools.partial(weight_grad_kernel, count),
        out_shape=[jax.ShapeDtypeStruct((count, rows, width), BF16)] * 2,
        grid_spec=pltpu.PrefetchScalarGridSpec(
            num_scalar_prefetch=2,
            grid=(steps,),
            in_specs=[whole(l_own), whole(l_other), r_spec, r_spec],
            out_specs=[out_spec, out_spec],
        ),
        compiler_params=pltpu.CompilerParams(vmem_limit_bytes=48 << 20),
        cost_estimate=pl.CostEstimate(
            flops=8 * count * rows * tok * width,
            bytes_accessed=2 * (2 * count * rows * width + 2 * tok * width),
            transcendentals=0,
        ),
        name="weight_grad",
    )(own_ids, other_ids, l_own, l_other, r_own, r_other)


def split_rows(left):
    n_fsdp = lax.axis_size("fsdp")
    turned = left.T.reshape(n_fsdp, left.shape[1] // n_fsdp, left.shape[0])
    parity = lax.axis_index("fsdp") % 2
    halves = turned.reshape(n_fsdp // 2, 2, *turned.shape[1:])
    away = lax.dynamic_index_in_dim(halves, 1 - parity, 1, keepdims=False)
    return turned, swap(away, "fsdp", 1)


def partial_rows(left, columns):
    n_fsdp, n_grp = lax.axis_size("fsdp"), lax.axis_size("grp")
    f = lax.axis_index("fsdp")
    parts = []
    for part, (right, right_other, start, width) in enumerate(columns):
        order = halving_orders(n_fsdp)[part % 2]
        keep = kept_pieces(order)
        ids = jnp.stack([flip(f // 2, k) for k in [k ^ order[0] for k in keep] + keep])
        pair = weight_grad(
            2 * ids + f % 2, ids, left[0], left[1], right, right_other, start, width
        )
        parts.append(
            tuple(v.reshape(v.shape[0], n_grp, v.shape[1] // n_grp, width) for v in pair)
        )
    return parts


def sum_everywhere(values):
    for axis in ("grp", "fsdp"):
        mask = 1
        while mask < lax.axis_size(axis):
            values = values + swap(values, axis, mask)
            mask *= 2
    return values


def norm_rows(features):
    row_scale = lax.rsqrt(jnp.mean(features * features, axis=-1, keepdims=True) + EPSILON)
    return (features * row_scale, row_scale)


def norm_back(grad_normed, normed, row_scale):
    average_addend = jnp.mean(grad_normed * normed, axis=-1, keepdims=True)
    return row_scale * (grad_normed - normed * average_addend)


def contract_cols(first_op, second_op):
    return lax.dot_general(
        first_op, second_op, (((1,), (1,)), ((), ())), preferred_element_type=F32
    )


def on_device(
    tokens,
    block_order,
    cont_lengths,
    gain_attn,
    w_qkv,
    w_forget,
    b_forget,
    w_out,
    gain_ffn,
    w_gate_up,
    w_down,
    grad_out,
):
    tok, width = tokens.shape
    heads = w_forget.shape[1]
    head_size = width // heads
    blocks = lax.axis_size("grp")
    own_heads = heads // blocks
    pairs = own_heads // 2
    group_width = width // blocks
    slots = block_order[0]

    positions = jnp.arange(tok, dtype=jnp.int32)
    causal = positions[None, :] <= positions[:, None]
    seg_ends = jnp.cumsum(cont_lengths[0], axis=1)
    segment = jnp.sum((positions[None, :, None] >= seg_ends[:, None, :]).astype(jnp.int32), axis=2)
    within = jnp.logical_and(segment[:, :, None] == segment[:, None, :], causal[None])
    seen = jnp.concatenate([causal[None], within], axis=0)
    masks = jnp.where(seen.transpose(0, 2, 1), 0.0, NEG).astype(F32)
    seen_low = seen.astype(BF16)

    forget_pad = 128 - heads
    qkv_full, forget_full = gather_rows(
        [w_qkv, jnp.pad(w_forget, ((0, 0), (0, forget_pad)))], 1
    )
    inputs = tokens.astype(F32)
    normed_one, scale_one = norm_rows(inputs)
    acts = (normed_one * gain_attn).astype(BF16)
    grad_out_other = swap(grad_out, "fsdp", 1)
    acts_rows = split_rows(acts)
    logits = jnp.dot(acts, forget_full, preferred_element_type=F32)[:, :heads] + b_forget
    log_keep = jax.nn.log_sigmoid(logits)
    mixed = jnp.dot(acts, qkv_full, preferred_element_type=F32).astype(BF16)

    logs = jnp.pad(
        log_keep.T.reshape(blocks, own_heads, tok), ((0, 0), (0, 8 - own_heads), (0, 0))
    )
    (out_full, gate_up_full, down_full), (attn_o, x, lse, decay) = forward_attention(
        [w_out, w_gate_up, w_down], slots, mixed, logs, masks, seen_low, head_size, 2
    )

    attn_rows = split_rows(attn_o)
    resid = inputs + jnp.dot(attn_o, out_full, preferred_element_type=F32)
    normed_two, scale_two = norm_rows(resid)
    acts_two = (normed_two * gain_ffn).astype(BF16)
    acts_two_rows = split_rows(acts_two)
    ffn_width = down_full.shape[0]
    both = jnp.dot(acts_two, gate_up_full, preferred_element_type=F32)
    gate = both[:, :ffn_width]
    up_part = both[:, ffn_width:]
    sigma = jax.nn.sigmoid(gate)
    swish = gate * sigma
    inner_act = (swish * up_part).astype(BF16)
    half = width // 2
    down_rows = split_rows(inner_act)
    result = resid + jnp.dot(inner_act, down_full, preferred_element_type=F32)
    output = result.astype(BF16)

    grad_inner = contract_cols(grad_out, down_full)
    slope = sigma * (1.0 + gate * (1.0 - sigma))
    grad_both = jnp.concatenate(
        [grad_inner * up_part * slope, grad_inner * swish], axis=1
    ).astype(BF16)
    grad_both_other = swap(grad_both, "fsdp", 1)
    grad_acts_two = contract_cols(grad_both, gate_up_full)
    gain_two_grad = jnp.sum(grad_acts_two * normed_two, axis=0)
    grad_resid = grad_out.astype(F32) + norm_back(
        grad_acts_two * gain_ffn, normed_two, scale_two
    )
    grad_branch = grad_resid.astype(BF16)
    grad_branch_other = swap(grad_branch, "fsdp", 1)
    grad_heads = contract_cols(grad_branch, out_full).astype(BF16)
    part_down = partial_rows(
        down_rows, [(grad_out, grad_out_other, 0, half), (grad_out, grad_out_other, half, half)]
    )
    part_gate_up = partial_rows(
        acts_two_rows,
        [
            (grad_both, grad_both_other, 0, ffn_width),
            (grad_both, grad_both_other, ffn_width, ffn_width),
        ],
    )
    part_out = partial_rows(
        attn_rows,
        [
            (grad_branch, grad_branch_other, 0, half),
            (grad_branch, grad_branch_other, half, half),
        ],
    )

    (grad_down, grad_gate_up, grad_out_w), grad_mixed, log_grad = backward_attention(
        [part_down, part_gate_up, part_out],
        slots,
        grad_heads,
        x,
        decay,
        masks,
        seen_low,
        lse,
        head_size,
        3,
    )
    log_grad = log_grad[:, :, :own_heads].transpose(1, 0, 2).reshape(tok, heads)
    grad_logits = (log_grad * jax.nn.sigmoid(-logits)).astype(BF16)
    part = 3 * width // 2
    narrow = jnp.pad(grad_logits, ((0, 0), (0, forget_pad)))
    last = jnp.concatenate([grad_mixed[:, part:], narrow], axis=1)
    part_qkv = partial_rows(
        acts_rows,
        [
            (grad_mixed, swap(grad_mixed, "fsdp", 1), 0, part),
            (last, swap(last, "fsdp", 1), 0, part + 128),
        ],
    )
    (grad_wide,) = scatter_rows([part_qkv], 4)
    grad_qkv, grad_forget = grad_wide[:, : 3 * width], grad_wide[:, 3 * width :][:, :heads]
    grad_acts = contract_cols(grad_mixed, qkv_full) + contract_cols(
        grad_logits, forget_full[:, :heads]
    )
    gain_one_grad = jnp.sum(grad_acts * normed_one, axis=0)
    bias_grad = jnp.sum(grad_logits.astype(F32), axis=0)
    grad_inputs = grad_resid + norm_back(grad_acts * gain_attn, normed_one, scale_one)
    small = sum_everywhere(jnp.concatenate([gain_one_grad, gain_two_grad, bias_grad]))
    return (
        output,
        grad_inputs.astype(BF16),
        small[:width],
        grad_qkv,
        grad_forget,
        small[2 * width :],
        grad_out_w,
        small[width : 2 * width],
        grad_gate_up,
        grad_down,
    )


def solution(mesh):
    both = P(("fsdp", "grp"), None)
    in_specs = (
        both,
        P("fsdp", None),
        P("fsdp", None, None),
        P(),
        both,
        both,
        P(),
        both,
        P(),
        both,
        both,
        both,
    )
    out_specs = (both, both, P(), both, both, P(), both, P(), both, both)
    return jax.shard_map(
        on_device, mesh=mesh, in_specs=in_specs, out_specs=out_specs, check_vma=False
    )
```

time: 1170 us -> 872 us (0.75)
  waiting for transfers between devices: 372 us -> 2.64 us
  Pallas kernels: 401 us -> 661 us
  starting transfers between devices: 91.7 us -> 8.67 us
  other arithmetic: 63.8 us -> 22.9 us
  local copies, waits for them, and re-layouts: 99.9 us -> 69.6 us
  between operations: 31.6 us -> 1.73 us
    ppermute x72 -> x14, waiting for transfers between devices: 372 us -> 2.64 us  [swap(): lax.ppermute(value, axis, [(i, i ^ mask) for i in range(lax.axis_size(axi...]
    pallas_call x4, Pallas kernels: 337 us -> 598 us  [the longest x1 226 us: backward_attention(): pl.pallas_call(functools.partial(backward_kernel, widths, pairs, head_siz...]
    ppermute x72 -> x14, starting transfers between devices: 91.6 us -> 8.67 us  [swap(): lax.ppermute(value, axis, [(i, i ^ mask) for i in range(lax.axis_size(axi...]
    another operation x14 -> x0, other arithmetic: 16.4 us -> none
    add x20 -> x1, other arithmetic: 15.3 us -> 0.08 us  [partial_rows(): 2 * ids + f % 2]
    unnamed x166 -> x109, local copies, waits for them, and re-layouts: 20.8 us -> 24.3 us
  transfers between devices with their start and end apart: 73 -> 14, of which waited for: 30 -> 3; matrix products, arithmetic and copies ran while one was open for 14% -> 10% of each run, Pallas kernels for 28% -> 4%
where the time goes in v2:
time: 872 us; the launch traced here: 868 us
  Pallas kernels  661 us (76%)
  matrix products  101 us (12%)
  local copies, waits for them, and re-layouts  69.6 us (8%)
  other arithmetic  22.9 us (3%)
    pallas_call x1, Pallas kernels, backward_attention(): pl.pallas_call(functools.partial(backward_kernel, widths, pairs, head_siz...  226 us
    pallas_call x1, Pallas kernels, forward_attention(): pl.pallas_call(functools.partial(forward_kernel, count, pairs, head_size,...  214 us
    pallas_call x1, Pallas kernels, scatter_rows(): pl.pallas_call(functools.partial(scatter_kernel, widths, n_fsdp, n_grp),...  90.3 us
    pallas_call x1, Pallas kernels, gather_rows(): pl.pallas_call(functools.partial(gather_kernel, count, n_fsdp, n_grp), ou...  67.9 us
    pallas_call x8, Pallas kernels, weight_grad(): pl.pallas_call(functools.partial(weight_grad_kernel, count), out_shape=[j...  63.4 us
    dot_general x5, matrix products, contract_cols(): lax.dot_general(first_op, second_op, (((1,), (1,)), ((), ())), preferred_...  53.7 us
    unnamed x109, local copies, waits for them, and re-layouts  24.3 us
    dot_general x1, matrix products, on_device(): both = jnp.dot(acts_two, gate_up_full, preferred_element_type=F32)  18.3 us
  transfers between devices with their start and end apart: 14, of which 3 were waited for; matrix products, arithmetic and copies ran while one was open for 10% of the time, Pallas kernels for 4%

profile of v2, /device:TPU:8, one launch (start us, length us, event | category | flops | bytes accessed | tf_op | source)
XLA Modules:
  0.0 867.5 jit_solution(4579385002613057047)
XLA Ops:
  4.7 67.9 %gather_rows.1 = (bf16[32,48,4608]{2,1,0:T(8,128)(2,1)}, bf16[32,48,128]{2,1,0:T(8,128)(2,1)}) custom-call(bf16[48,4608]{1,0:T(8,128)(2,1)} %refs_0_.2, bf16[48,128]{1,0:T(8,128)(2,1)} %pad.12.refs_1_), custom_call_target="tpu_custom_call" | custom-call | tf_op jit(solution)/shard_map/gather_rows/pallas_call | solution.py:235
  74.9 12.7 %convolution_convert_fusion.refs_4_ = bf16[384,4608]{1,0:T(8,128)(2,1)} fusion(bf16[1536,4608]{1,0:T(8,128)(2,1)} %bitcast.118, bf16[384,1536]{1,0:T(8,128)(2,1)S(1)} %copy-done.27, f32[1536]{0:T(1024)S(1)} %copy-done.42, f32[384]{0:T(512)S(1)} %add_rsqrt_fusion.1), kind=kOutput, calls=%fused_computation | convolution fusion | flops 5439946752 | bytes 18882048 | tf_op jit(solution)/shard_map/dot_general | solution.py:1099
  87.6 2.3 copy.80.refs_6_.refs_16_
  91.7 213.9 %forward_attention.1 = (bf16[32,48,1536]{2,1,0:T(8,128)(2,1)}, bf16[32,48,8192]{2,1,0:T(8,128)(2,1)}, bf16[32,128,1536]{2,1,0:T(8,128)(2,1)}, bf16[384,1536]{1,0...) custom-call(bf16[48,1536]{1,0:T(8,128)(2,1)S(1)} %copy-done.22, ...), custom_call_target="tpu_custom_call" | custom-call | tf_op jit(solution)/shard_map/forward_attention/pallas_call | solution.py:446
  305.7 5.1 multiply_reduce_fusion.2
  310.9 18.3 %fusion.25 = f32[384,8192]{1,0:T(8,128)} fusion(bf16[1536,8192]{1,0:T(8,128)(2,1)} %bitcast.116, f32[384,1536]{1,0:T(8,128)S(1)} %get-tuple-element.129, f32[1536]{0:T(1024)S(1)} %copy-done.45, f32[384]{0:T(512)S(1)} %add_rsqrt_fusion), kind=kOutput, calls=%fused_computation.68 | convolution fusion | flops 9665445888 | bytes 40115712 | tf_op jit(solution)/shard_map/dot_general | solution.py:1114
  329.2 17.2 %fusion.1 = (bf16[384,4096]{1,0:T(8,128)(2,1)S(1)}, bf16[384,4096]{1,0:T(8,128)(2,1)S(1)}, bf16[384,4096]{1,0:T(8,128)(2,1)}) fusion(f32[384,8192]{1,0:T(8,128)} %fusion.25, bf16[4096,1536]{1,0:T(8,128)(2,1)} %bitcast.120, bf16[384,1536]{1,0:T(8,128)(2,1)S(1)} %copy-done.2), kind=kOutput, calls=%fused_computation.5 | convolution fusion | flops 4855431168 | bytes 35782656 | tf_op jit(solution)/shard_map/dot_general | solution.py:1051
  346.3 3.7 pad_maximum_fusion.r_ref
  351.6 6.2 reshape_reshape.12
  357.8 6.8 constant_dynamic-slice_fusion
  364.6 8.2 copy.82
  372.8 17.6 %multiply_reduce_fusion = (f32[1536]{0:T(1024)}, f32[384]{0:T(512)S(1)}, f32[384,1536]{1,0:T(8,128)}) fusion(f32[384,1536]{1,0:T(8,128)S(1)} %get-tuple-element.129, f32[384]{0:T(512)S(1)} %add_rsqrt_fusion, f32[1536]{0:T(1024)S(1)} %copy-done.45, bf16[1536,8192]{1,0:T(8,128)(2,1)} %bitcast.117, bf16[384,4096]{1,0:T(8,128)(2,1)} %copy-done.34, ...), kind=kOutput, calls=%fused_computation.31 | convolution fusion | flops 9679796224 | bytes 36191232 | tf_op jit(solution)/shard_map/dot_general | solution.py:1051
  390.4 4.1 fusion.29
  398.6 2.4 copy.85
  403.0 4.7 copy.97
  407.7 5.4 convolution_convert_fusion.1.refs_13_
  413.2 3.2 weight_grad.13
  418.1 3.2 weight_grad.12
  422.9 7.5 weight_grad.9
  432.8 7.5 weight_grad.8
  442.7 10.3 %weight_grad.11 = (bf16[2,192,4096]{2,1,0:T(8,128)(2,1)S(1)}, bf16[2,192,4096]{2,1,0:T(8,128)(2,1)}) custom-call(s32[4]{0:T(128)S(1)} %get-tuple-element.116.own_ids, s32[4]{0:T(128)S(1)} %get-tuple-element.117.other_ids, bf16[8,192,384]{2,1,0:T(8,128)(2,1)S(1)} %bitcast.89, bf16[4,192,384]{2,1,0:T(8,128)(2,1)S(1)} %collective-permute-done.2.l_other_ref, ...), custom_call_target="tpu_custom_call" | custom-call | flops 4831838208 | bytes 12582912 | tf_op jit(solution)/shard_map/weight_grad/pallas_call | solution.py:986
  454.6 10.3 %weight_grad.10 = (bf16[2,192,4096]{2,1,0:T(8,128)(2,1)S(1)}, bf16[2,192,4096]{2,1,0:T(8,128)(2,1)}) custom-call(s32[4]{0:T(128)S(1)} %get-tuple-element.131.own_ids, s32[4]{0:T(128)S(1)} %get-tuple-element.132.other_ids, bf16[8,192,384]{2,1,0:T(8,128)(2,1)S(1)} %bitcast.90, bf16[4,192,384]{2,1,0:T(8,128)(2,1)S(1)} %collective-permute-done.2.l_other_ref, ...), custom_call_target="tpu_custom_call" | custom-call | flops 4831838208 | bytes 12582912 | tf_op jit(solution)/shard_map/weight_grad/pallas_call | solution.py:986
  466.6 225.8 %backward_attention.1 = (f32[128,1536]{1,0:T(8,128)}, f32[48,8192]{1,0:T(8,128)}, f32[48,1536]{1,0:T(8,128)}, bf16[384,4608]{1,0:T(8,128)(2,1)}, f32[4,384,8]{2,1,0:T(8,128)}) custom-call(bf16[2,4,128,768]{3,2,1,0:T(8,128)(2,1)} %bitcast.97, bf16[2,4,128,768]{3,2,1,0:T(8,128)(2,1)} %bitcast.95, bf16[2,4,48,4096]{3,2,1,0:T(8,128)(2,1)} %bitcast.84, ...), custom_call_target="tpu_custom_call" | custom-call | tf_op jit(solution)/shard_map/backward_attention/pallas_call | solution.py:932
  694.0 11.2 %fusion.32 = f32[384,1536]{1,0:T(8,128)} fusion(bf16[384,4608]{1,0:T(8,128)(2,1)} %get-tuple-element.61.r_ref, bf16[1536,4608]{1,0:T(8,128)(2,1)} %bitcast.119), kind=kOutput, calls=%fused_computation.73 | convolution fusion | flops 5435817984 | bytes 20054016 | tf_op jit(solution)/shard_map/dot_general | solution.py:1051
  707.8 2.3 convolution_add_fusion
  711.6 2.3 fusion.16
  719.4 9.3 %fusion.9 = bf16[384,1536]{1,0:T(8,128)(2,1)} fusion(f32[384,1536]{1,0:T(8,128)S(1)} %copy-done.31, bf16[384,4096]{1,0:T(8,128)(2,1)S(1)} %copy-done.26, bf16[4096,1536]{1,0:T(8,128)(2,1)} %bitcast.121), kind=kOutput, calls=%fused_computation.21 | convolution fusion | flops 4833017856 | bytes 19267584 | tf_op jit(solution)/shard_map/dot_general | solution.py:1122
  736.9 5.7 fusion.15
  743.8 15.0 %weight_grad.15 = (bf16[2,192,2432]{2,1,0:T(8,128)(2,1)S(1)}, bf16[2,192,2432]{2,1,0:T(8,128)(2,1)S(1)}) custom-call(s32[4]{0:T(128)S(1)} %get-tuple-element.116.own_ids, s32[4]{0:T(128)S(1)} %get-tuple-element.117.other_ids, bf16[8,192,384]{2,1,0:T(8,128)(2,1)S(1)} %bitcast.86, bf16[4,192,384]{2,1,0:T(8,128)(2,1)S(1)} %collective-permute-done.11.l_other_ref, ...), custom_call_target="tpu_custom_call" | custom-call | flops 2868903936 | bytes 7471104 | tf_op jit(solution)/shard_map/weight_grad/pallas_call | solution.py:986
  761.4 6.5 weight_grad.14
  770.3 90.3 %scatter_rows.1 = f32[48,4736]{1,0:T(8,128)} custom-call(bf16[2,4,48,2304]{3,2,1,0:T(8,128)(2,1)} %bitcast.93, bf16[2,4,48,2432]{3,2,1,0:T(8,128)(2,1)} %bitcast.91, bf16[2,4,48,2304]{3,2,1,0:T(8,128)(2,1)} %bitcast.94, bf16[2,4,48,2432]{3,2,1,0:T(8,128)(2,1)} %bitcast.92), custom_call_target="tpu_custom_call" | custom-call | tf_op jit(solution)/shard_map/scatter_rows/pallas_call | solution.py:811
  860.6 2.3 slice.42
  (177 shorter events, 56.6 us)
Async XLA Ops:
  2.1 70.6 %copy-start.42 = (f32[1536]{0:T(1024)S(1)}, f32[1536]{0:T(1024)}, u32[]{:S(2)}) copy-start(f32[1536]{0:T(1024)} %param.15) | copy-start | bytes 18436
  2.1 70.6 %copy-start.51 = (f32[24]{0:T(128)S(1)}, f32[24]{0:T(128)}, u32[]{:S(2)}) copy-start(f32[24]{0:T(128)} %param.18) | copy-start | bytes 292
  3.7 86.3 %copy-start.1 = (bf16[3,384,384]{2,1,0:T(8,128)(2,1)}, bf16[3,384,384]{2,1,0:T(8,128)(2,1)S(1)}, u32[]{:S(2)}) copy-start(bf16[3,384,384]{2,1,0:T(8,128)(2,1)S(1)} %fusion.19.refs_7_.refs_17_) | copy-start | bytes 2654212
  4.0 83.6 %copy-start.46 = (f32[384]{0:T(512)}, f32[384]{0:T(512)S(1)}, u32[]{:S(2)}) copy-start(f32[384]{0:T(512)S(1)} %add_rsqrt_fusion.1) | copy-start | bytes 4612
  89.9 215.7 %copy-start = (f32[3,384,384]{2,1,0:T(8,128)}, f32[3,384,384]{2,1,0:T(8,128)S(1)}, u32[]{:S(2)}) copy-start(f32[3,384,384]{2,1,0:T(8,128)S(1)} %copy.80.refs_6_.refs_16_) | copy-start | bytes 5308420
  91.7 214.0 %copy-start.28 = (bf16[384,1536]{1,0:T(8,128)(2,1)S(1)}, bf16[384,1536]{1,0:T(8,128)(2,1)}, u32[]{:S(2)}) copy-start(bf16[384,1536]{1,0:T(8,128)(2,1)} %param.12) | copy-start | bytes 3538948
  305.7 5.2 copy-start.45
  310.8 62.0 %copy-start.30 = (f32[384,1536]{1,0:T(8,128)}, f32[384,1536]{1,0:T(8,128)S(1)}, u32[]{:S(2)}) copy-start(f32[384,1536]{1,0:T(8,128)S(1)} %get-tuple-element.129) | copy-start | bytes 7077892
  310.9 79.5 %copy-start.48 = (f32[384]{0:T(512)}, f32[384]{0:T(512)S(1)}, u32[]{:S(2)}) copy-start(f32[384]{0:T(512)S(1)} %add_rsqrt_fusion) | copy-start | bytes 4612
  310.9 18.3 %copy-start.2 = (bf16[384,1536]{1,0:T(8,128)(2,1)S(1)}, bf16[384,1536]{1,0:T(8,128)(2,1)}, u32[]{:S(2)}) copy-start(bf16[384,1536]{1,0:T(8,128)(2,1)} %r_ref.3) | copy-start | bytes 3538948
  350.9 91.8 %collective-permute-start.3 = (bf16[384,8192]{1,0:T(8,128)(2,1)}, bf16[384,8192]{1,0:T(8,128)(2,1)}, u32[]{:S(2)}, u32[]{:S(2)}) collective-permute-start(bf16[384,8192]{1,0:T(8,128)(2,1)} %pad_maximum_fusion.r_ref), channel_id=1, source_target_pairs={{0,4},{4,0},{8,12},{12,8},{16,20},{20,16},{24,28},{28,24},{1,5},{5... | collective-permute-start | bytes 18874376 | tf_op jit(solution)/shard_map/ppermute | solution.py:33
  372.8 50.2 %collective-permute-start = (bf16[4,512,384]{2,1,0:T(8,128)(2,1)}, bf16[4,512,384]{2,1,0:T(8,128)(2,1)}, u32[]{:S(2)}, u32[]{:S(2)}) collective-permute-start(bf16[4,512,384]{2,1,0:T(8,128)(2,1)} %bitcast.112), channel_id=1, source_target_pairs={{0,4},{4,0},{8,12},{12,8},{16,20},{20,16},{24,28},{28,24},{1,5},{5... | collective-permute-start | bytes 4718600 | tf_op jit(solution)/shard_map/ppermute | solution.py:33
  394.5 18.7 %collective-permute-start.5 = (bf16[384,1536]{1,0:T(8,128)(2,1)S(1)}, bf16[384,1536]{1,0:T(8,128)(2,1)}, u32[]{:S(2)}, u32[]{:S(2)}) collective-permute-start(bf16[384,1536]{1,0:T(8,128)(2,1)S(1)} %get-tuple-element.123.r_ref), channel_id=1, source_target_pairs={{0,4},{4,0},{8,12},{12,8},{16,20},{20,16},{24,28},{28,24},{1,5},{5... | collective-permute-start | bytes 3538952 | tf_op jit(solution)/shard_map/ppermute | solution.py:33
  395.0 27.9 %collective-permute-start.1 = (bf16[384,1536]{1,0:T(8,128)(2,1)S(1)}, bf16[384,1536]{1,0:T(8,128)(2,1)}, u32[]{:S(2)}, u32[]{:S(2)}) collective-permute-start(bf16[384,1536]{1,0:T(8,128)(2,1)S(1)} %copy-done.2), channel_id=1, source_target_pairs={{0,4},{4,0},{8,12},{12,8},{16,20},{20,16},{24,28},{28,24},{1,5},{5... | collective-permute-start | bytes 3538952 | tf_op jit(solution)/shard_map/ppermute | solution.py:33
  398.1 15.1 %collective-permute-start.4 = (bf16[4,192,384]{2,1,0:T(8,128)(2,1)}, bf16[4,192,384]{2,1,0:T(8,128)(2,1)}, u32[]{:S(2)}, u32[]{:S(2)}) collective-permute-start(bf16[4,192,384]{2,1,0:T(8,128)(2,1)} %dynamic-slice_bitcast_fusion.1), channel_id=1, source_target_pairs={{0,4},{4,0},{8,12},{12,8},{16,20},{20,16},{24,28},{28,24},{1,5},{5... | collective-permute-start | bytes 1769480 | tf_op jit(solution)/shard_map/ppermute | solution.py:33
  407.7 5.4 copy-start.40
  413.2 29.5 %collective-permute-start.2 = (bf16[4,192,384]{2,1,0:T(8,128)(2,1)S(1)}, bf16[4,192,384]{2,1,0:T(8,128)(2,1)S(1)}, u32[]{:S(2)}, u32[]{:S(2)}) collective-permute-start(bf16[4,192,384]{2,1,0:T(8,128)(2,1)S(1)} %copy-done.40), channel_id=1, source_target_pairs={{0,4},{4,0},{8,12},{12,8},{16,20},{20,16},{24,28},{28,24},{1,5},{5... | collective-permute-start | bytes 1769480 | tf_op jit(solution)/shard_map/ppermute | solution.py:33
  432.8 9.9 %copy-start.5 = (bf16[1536,384]{1,0:T(8,128)(2,1)S(1)}, bf16[1536,384]{1,0:T(8,128)(2,1)}, u32[]{:S(2)}) copy-start(bf16[1536,384]{1,0:T(8,128)(2,1)} %copy.85) | copy-start | bytes 3538948
  694.0 11.2 %copy-start.37 = (f32[4,384,8]{2,1,0:T(8,128)S(1)}, f32[4,384,8]{2,1,0:T(8,128)}, u32[]{:S(2)}) copy-start(f32[4,384,8]{2,1,0:T(8,128)} %get-tuple-element.62) | copy-start | bytes 147460
  705.2 56.2 %collective-permute-start.12 = (bf16[384,4608]{1,0:T(8,128)(2,1)}, bf16[384,4608]{1,0:T(8,128)(2,1)}, u32[]{:S(2)}, u32[]{:S(2)}) collective-permute-start(bf16[384,4608]{1,0:T(8,128)(2,1)} %get-tuple-element.61.r_ref), channel_id=1, source_target_pairs={{0,4},{4,0},{8,12},{12,8},{16,20},{20,16},{24,28},{28,24},{1,5},{5... | collective-permute-start | bytes 10616840 | tf_op jit(solution)/shard_map/ppermute | solution.py:33
  711.5 7.9 copy-start.31
  713.9 5.6 copy-start.26
  713.9 3.8 collective-permute-start.6
  717.0 26.8 %collective-permute-start.13 = (bf16[384,2432]{1,0:T(8,128)(2,1)}, bf16[384,2432]{1,0:T(8,128)(2,1)}, u32[]{:S(2)}, u32[]{:S(2)}) collective-permute-start(bf16[384,2432]{1,0:T(8,128)(2,1)} %fusion.18.r_ref), channel_id=1, source_target_pairs={{0,4},{4,0},{8,12},{12,8},{16,20},{20,16},{24,28},{28,24},{1,5},{5... | collective-permute-start | bytes 5603336 | tf_op jit(solution)/shard_map/ppermute | solution.py:33
  718.3 10.4 %copy-start.32 = (bf16[1536,384]{0,1:T(8,128)(2,1)S(1)}, bf16[1536,384]{0,1:T(8,128)(2,1)}, u32[]{:S(2)}) copy-start(bf16[1536,384]{0,1:T(8,128)(2,1)} %get-tuple-element.125) | copy-start | bytes 3538948
  718.3 11.1 %collective-permute-start.7 = (f32[3096]{0:T(1024)}, f32[3096]{0:T(1024)}, u32[]{:S(2)}, u32[]{:S(2)}) collective-permute-start(f32[3096]{0:T(1024)} %fusion.47), channel_id=1, source_target_pairs={{0,2},{1,3},{2,0},{3,1},{4,6},{5,7},{6,4},{7,5},{8,10},{9,11},{10,... | collective-permute-start | bytes 37160 | tf_op jit(solution)/shard_map/ppermute | solution.py:33
  730.2 1.2 collective-permute-start.8
  730.3 13.5 %collective-permute-start.11 = (bf16[4,192,384]{2,1,0:T(8,128)(2,1)S(1)}, bf16[4,192,384]{2,1,0:T(8,128)(2,1)S(1)}, u32[]{:S(2)}, u32[]{:S(2)}) collective-permute-start(bf16[4,192,384]{2,1,0:T(8,128)(2,1)S(1)} %dynamic-slice_bitcast_fusion), channel_id=1, source_target_pairs={{0,4},{4,0},{8,12},{12,8},{16,20},{20,16},{24,28},{28,24},{1,5},{5... | collective-permute-start | bytes 1769480 | tf_op jit(solution)/shard_map/ppermute | solution.py:33
  731.4 3.7 collective-permute-start.9
  735.1 7.5 collective-permute-start.10
  770.3 94.0 %copy-start.41 = (f32[48,1536]{1,0:T(8,128)S(1)}, f32[48,1536]{1,0:T(8,128)}, u32[]{:S(2)}) copy-start(f32[48,1536]{1,0:T(8,128)} %get-tuple-element.149) | copy-start | bytes 884740
  860.6 5.6 copy-start.36
  (34 other events, 80.8 us)

commit v3 on v2

--- a/solution.py
+++ b/solution.py
@@ -10,7 +10,7 @@
 
 EPSILON = 1e-05
 NEG = -1e30
-HIGHEST = lax.Precision.HIGHEST
+AHEAD = 6
 MESH = pl.DeviceIdType.MESH
 F32 = jnp.float32
 BF16 = jnp.bfloat16
@@ -38,32 +38,38 @@
 
 
 class Gather:
-    def __init__(self, ins, outs, send_sem, recv_sem, local_sem, n_fsdp, n_grp):
-        self.ins, self.outs = ins, outs
+    def __init__(self, kinds, ins, outs, send_sem, recv_sem, local_sem, n_fsdp, n_grp):
+        self.kinds, self.ins, self.outs = kinds, ins, outs
         self.send_sem, self.recv_sem = send_sem, recv_sem
         self.f, self.z, self.n_grp = lax.axis_index("fsdp"), lax.axis_index("grp"), n_grp
         self.bits = [1 << i for i in range(1, n_fsdp.bit_length() - 1)]
-        self.parts = gather_parts([r.shape for r in ins])
+        self.parts = gather_parts([r.shape[-2:] for r in ins])
         self.orders = [self.bits if h == 0 else self.bits[::-1] for _, h in self.parts]
         self.across = {b: {"fsdp": flip(self.f, b), "grp": self.z} for b in self.bits + [1]}
         self.up = {"fsdp": self.f, "grp": self.z + 1}
         self.down = {"fsdp": self.f, "grp": self.z - 1}
         self.count, self.sent, self.local = 0, [], []
         for w in range(len(ins)):
+            target = {
+                "full": self.f * n_grp + self.z,
+                "line": self.z,
+                "lined": pl.ds(self.f * n_grp, n_grp),
+            }[kinds[w]]
             self.local.append(
-                pltpu.make_async_copy(
-                    ins[w], outs[w].at[self.f * n_grp + self.z], local_sem.at[w]
-                )
+                pltpu.make_async_copy(ins[w], outs[w].at[target], local_sem.at[w])
             )
-        self.steps = self._steps()
+        self.steps, self.done = self._steps(), 0
 
     def _columns(self, part):
         w, h = self.parts[part]
-        width = self.ins[w].shape[1]
+        width = self.ins[w].shape[-1]
         return pl.ds(0, width) if width % 256 else pl.ds(h * (width // 2), width // 2)
 
+    def kind(self, part):
+        return self.kinds[self.parts[part][0]]
+
     def _piece(self, part, fk, place):
-        row = flip(self.f, fk) * self.n_grp + place
+        row = place if self.kind(part) == "line" else flip(self.f, fk) * self.n_grp + place
         return self.outs[self.parts[part][0]].at[row, :, self._columns(part)]
 
     def _send(self, part, fk, place, to, to_fk, own=False):
@@ -73,7 +79,9 @@
         def copy():
             source = self._piece(part, fk, place)
             if own:
-                source = self.ins[self.parts[part][0]].at[:, self._columns(part)]
+                source = self.ins[self.parts[part][0]]
+                source = source.at[place] if self.kind(part) == "lined" else source
+                source = source.at[:, self._columns(part)]
             return pltpu.make_async_remote_copy(
                 src_ref=source,
                 dst_ref=self._piece(part, fk, place),
@@ -98,6 +106,8 @@
         ).wait_recv()
 
     def _forward(self, part, stage, fk, place, own=False):
+        if self.kind(part) == "line":
+            return []
         return [
             self._send(part, fk, place, self.across[b], fk ^ b, own)
             for b in self.orders[part][stage:] + [1]
@@ -113,6 +123,10 @@
             copy.start()
         last = self.n_grp - 1
         for part in range(len(self.parts)):
+            if self.kind(part) == "lined":
+                for place in range(self.n_grp):
+                    self.sent.append((None, self._forward(part, 0, 0, place, True)))
+                continue
             self._when(
                 self.z < last, lambda: [self._send(part, 0, self.z, self.up, 0, True)]
             )
@@ -145,38 +159,47 @@
         self.sent.append((None, self._forward(part, stage + 1, fk, place)))
 
     def _steps(self):
-        count = len(self.parts)
-        steps = []
+        lines = [p for p in range(len(self.parts)) if self.kind(p) != "lined"]
+        crossing = [p for p in range(len(self.parts)) if self.kind(p) != "line"]
+        early = [p for p in crossing if self.kind(p) == "lined"]
+        bind = functools.partial
+
+        def cross(parts, stage):
+            known = [[0] for _ in parts]
+            for i in range(stage):
+                known = [
+                    k + [v ^ self.orders[p][i] for v in k] for p, k in zip(parts, known)
+                ]
+            return [
+                bind(self._cross_step, p, stage, k[a] ^ self.orders[p][stage], place)
+                for a in range(len(known[0]) if parts else 0)
+                for place in range(self.n_grp)
+                for p, k in zip(parts, known)
+            ]
+
+        ahead = cross(early, 0)
+        steps, self.marks = [], []
         for j in range(1, self.n_grp):
-            for part in range(count):
-                steps.append(functools.partial(self._line_step, part, j))
-        have = [[0] for _ in range(count)]
+            steps += [bind(self._line_step, part, j) for part in lines]
+            self.marks.append(len(steps))
+            share = -(-len(ahead) // (self.n_grp - j))
+            steps, ahead = steps + ahead[:share], ahead[share:]
         for stage in range(len(self.bits)):
-            for a in range(len(have[0])):
-                for place in range(self.n_grp):
-                    for part in range(count):
-                        fk = have[part][a] ^ self.orders[part][stage]
-                        steps.append(
-                            functools.partial(self._cross_step, part, stage, fk, place)
-                        )
-            have = [
-                known + [v ^ self.orders[part][stage] for v in known]
-                for part, known in enumerate(have)
-            ]
-        for a in range(len(have[0])):
+            steps += cross([p for p in crossing if stage or p not in early], stage)
+        everything = [0]
+        for bit in self.bits:
+            everything = everything + [v ^ bit for v in everything]
+        for fk in everything:
             for place in range(self.n_grp):
-                for part in range(count):
-                    steps.append(functools.partial(self._wait, part, have[part][a] ^ 1, place))
+                for p in crossing:
+                    steps.append(bind(self._wait, p, fk ^ 1, place))
         return steps
 
     def run(self, until=None):
-        done = len(self.all_steps) - len(self.steps) if hasattr(self, "all_steps") else 0
-        if done == 0:
-            self.all_steps = list(self.steps)
-        stop = len(self.all_steps) if until is None else int(until * len(self.all_steps))
-        for step in self.all_steps[done:stop]:
+        until = len(self.steps) if until is None else until
+        for step in self.steps[self.done : until]:
             step()
-        self.steps = self.all_steps[max(stop, done) :]
+        self.done = max(self.done, until)
 
     def finish(self):
         self.run()
@@ -196,7 +219,7 @@
 
 
 def gather_scratch(weights, n_fsdp, n_grp):
-    parts = len(gather_parts([w.shape for w in weights]))
+    parts = len(gather_parts([w.shape[-2:] for w in weights]))
     bits = n_fsdp.bit_length() - 2
     crossing = n_fsdp // 2 - 1 + n_fsdp // 2
     sends = 2 + (n_grp - 1) * 2 * (bits + 1) + 2 * (n_grp - 2) + n_grp * crossing + bits + 1
@@ -207,8 +230,13 @@
     ]
 
 
-def gathered(weights, n_fsdp, n_grp):
-    return [jax.ShapeDtypeStruct((n_fsdp * n_grp,) + w.shape, w.dtype) for w in weights]
+def gathered(kinds, weights, n_fsdp, n_grp):
+    return [
+        jax.ShapeDtypeStruct(
+            (n_grp if kind == "line" else n_fsdp * n_grp,) + w.shape[-2:], w.dtype
+        )
+        for kind, w in zip(kinds, weights)
+    ]
 
 
 def meet(n_fsdp, n_grp, line_only):
@@ -222,28 +250,53 @@
     pl.semaphore_wait(barrier, len(peers))
 
 
-def gather_kernel(count, n_fsdp, n_grp, *refs):
+def gather_kernel(kinds, n_fsdp, n_grp, *refs):
     meet(n_fsdp, n_grp, True)
-    gather = Gather(refs[:count], refs[count : 2 * count], *refs[2 * count :], n_fsdp, n_grp)
-    gather.start()
-    gather.finish()
-
-
-def gather_rows(weights, collective_id):
+    count = len(kinds)
+    ins, outs, sems = refs[:count], refs[count : 2 * count], refs[2 * count :]
+    first = [i for i, kind in enumerate(kinds) if kind == "full"]
+    second = [i for i, kind in enumerate(kinds) if kind == "line"]
+    gathers = [
+        Gather(
+            [kinds[i] for i in chosen],
+            [ins[i] for i in chosen],
+            [outs[i] for i in chosen],
+            *sems[3 * n : 3 * n + 3],
+            n_fsdp,
+            n_grp,
+        )
+        for n, chosen in enumerate((first, second))
+    ]
+    gathers[0].start()
+    gathers[0].run(gathers[0].marks[-2])
+    gathers[1].start()
+    gathers[0].run(gathers[0].marks[-1])
+    for n in range(len(gathers[1].steps)):
+        share = (len(gathers[0].steps) - gathers[0].marks[-1]) * (n + 1)
+        gathers[0].run(gathers[0].marks[-1] + share // (2 * len(gathers[1].steps)))
+        gathers[1].run(n + 1)
+    for gather in gathers:
+        gather.finish()
+
+
+def gather_rows(kinds, weights, collective_id):
     n_fsdp, n_grp = lax.axis_size("fsdp"), lax.axis_size("grp")
     count = len(weights)
-    full = pl.pallas_call(
-        functools.partial(gather_kernel, count, n_fsdp, n_grp),
-        out_shape=gathered(weights, n_fsdp, n_grp),
+    return pl.pallas_call(
+        functools.partial(gather_kernel, kinds, n_fsdp, n_grp),
+        out_shape=gathered(kinds, weights, n_fsdp, n_grp),
         in_specs=[pl.BlockSpec(memory_space=pl.ANY)] * count,
         out_specs=[pl.BlockSpec(memory_space=pl.ANY)] * count,
-        scratch_shapes=gather_scratch(weights, n_fsdp, n_grp),
+        scratch_shapes=[
+            v
+            for kind in ("full", "line")
+            for v in gather_scratch([w for k, w in zip(kinds, weights) if k == kind], n_fsdp, n_grp)
+        ],
         compiler_params=pltpu.CompilerParams(
             collective_id=collective_id, has_side_effects=True
         ),
         name="gather_rows",
     )(*weights)
-    return [v.reshape(-1, v.shape[2]) for v in full]
 
 
 def dot_lanes(a, b):
@@ -275,10 +328,12 @@
     return result
 
 
-def attend_pair(pair, blocks, head_size, slots_ref, x_ref, c_ref, mask_ref, o_ref, lse_ref):
+def attend_head(
+    pair, h, blocks, head_size, slots_ref, x_ref, c_ref, mask_ref, o_ref, lse_ref
+):
     scale = head_size**-0.5
 
-    def head(h, carry):
+    def head():
         lanes = lax.broadcasted_iota(jnp.int32, (1, 2 * head_size), 1)
         mine = lanes // head_size == h
         decays = [column(c_ref[b], 2 * pair + h) for b in range(blocks)]
@@ -303,9 +358,8 @@
             outs.append((mixed / total).T.astype(BF16))
         for place in range(blocks):
             o_ref[place] = jnp.where(mine, pick(slots_ref, place, outs), o_ref[place])
-        return carry
-
-    lax.fori_loop(0, 2, head, 0)
+
+    head()
 
 
 def sum_decay(blocks, slots_ref, log_ref, seen_ref, c_ref):
@@ -362,7 +416,8 @@
             copy.wait_send()
 
 
-def forward_kernel(count, pairs, head_size, n_fsdp, n_grp, *refs):
+def forward_kernel(kinds, pairs, head_size, n_fsdp, n_grp, *refs):
+    count = len(kinds)
     weights, refs = refs[:count], refs[count:]
     slots_ref, mixed_ref, log_ref, mask_ref, seen_ref = refs[:5]
     full, refs = refs[5 : 5 + count], refs[5 + count :]
@@ -378,7 +433,7 @@
     z = lax.axis_index("grp")
 
     meet(n_fsdp, n_grp, False)
-    gather = Gather(weights, full, *gather_sems, n_fsdp, n_grp)
+    gather = Gather(kinds, weights, full, *gather_sems, n_fsdp, n_grp)
     swap_heads = GroupExchange(n_grp, send_sem, recv_sem)
     started = itertools.count()
 
@@ -391,10 +446,9 @@
         start = part * width + place * group_width + pair * pair_width
         return mixed_ref.at[:, pl.ds(pl.multiple_of(start, 128), pair_width)]
 
-    own_logs = keep(log_ref.at[z], logs_ref.at[z])
-    swap_heads.send("logs", 0, lambda place: log_ref.at[place], lambda place: logs_ref.at[place])
-    own, late = [], []
-    for pair in range(pairs):
+    own = []
+
+    def send_pair(pair):
         for part in range(3):
             swap_heads.send(
                 (pair, part),
@@ -403,21 +457,33 @@
                 lambda place, pair=pair, part=part: x_refs[pair].at[place, part],
             )
             own.append(keep(heads_of(part, z, pair), x_refs[pair].at[z, part]))
-        if pair == 0:
-            gather.start()
-    gather.run(0.1)
+
+    late = []
+    own_logs = keep(log_ref.at[z], logs_ref.at[z])
+    swap_heads.send("logs", 0, lambda place: log_ref.at[place], lambda place: logs_ref.at[place])
+    gather.start()
+    send_pair(0)
+    for pair in range(1, pairs):
+        if pair <= len(gather.marks):
+            gather.run(gather.marks[pair - 1])
+        send_pair(pair)
     own_logs.wait()
     swap_heads.wait("logs")
     sum_decay(blocks, slots_ref, logs_ref, seen_ref, c_ref)
+    last_wait = len(gather.steps) * 3 // 5
+    share = -(-(last_wait - gather.done) // (2 * pairs))
     for pair in range(pairs):
-        gather.run(0.16 + 0.12 * pair)
         for part in range(3):
             own[3 * pair + part].wait()
             swap_heads.wait((pair, part))
-        attend_pair(
-            pair, blocks, head_size, slots_ref, x_refs[pair], c_ref, mask_ref, o_refs[pair], lse_ref
-        )
-        late.append(keep(x_refs[pair], x_out.at[pair]))
+        for h in range(2):
+            attend_head(
+                pair, h, blocks, head_size, slots_ref, x_refs[pair], c_ref, mask_ref,
+                o_refs[pair], lse_ref,
+            )
+            if h == 0:
+                late.append(keep(x_refs[pair], x_out.at[pair]))
+                gather.run(gather.done + share)
 
         def columns(place, pair=pair):
             start = place * group_width + pair * pair_width
@@ -427,6 +493,7 @@
             (pair, 3), 4 + 4 * pair, lambda place: o_refs[pair].at[place], columns
         )
         late.append(keep(o_refs[pair].at[z], columns(z)))
+        gather.run(gather.done + share)
     gather.finish()
     for pair in range(pairs):
         swap_heads.wait((pair, 3))
@@ -435,7 +502,7 @@
         copy.wait()
 
 
-def forward_attention(weights, slots, mixed, logs, masks, seen, head_size, collective_id):
+def forward_attention(kinds, weights, slots, mixed, logs, masks, seen, head_size, collective_id):
     n_fsdp, n_grp = lax.axis_size("fsdp"), lax.axis_size("grp")
     count = len(weights)
     tok, width = mixed.shape[0], mixed.shape[1] // 3
@@ -444,8 +511,8 @@
     anywhere = pl.BlockSpec(memory_space=pl.ANY)
     vmem = pl.BlockSpec(memory_space=pltpu.VMEM)
     out = pl.pallas_call(
-        functools.partial(forward_kernel, count, pairs, head_size, n_fsdp, n_grp),
-        out_shape=gathered(weights, n_fsdp, n_grp)
+        functools.partial(forward_kernel, kinds, pairs, head_size, n_fsdp, n_grp),
+        out_shape=gathered(kinds, weights, n_fsdp, n_grp)
         + [
             jax.ShapeDtypeStruct((tok, width), BF16),
             jax.ShapeDtypeStruct((pairs, n_grp, 3, tok, pair_width), BF16),
@@ -582,10 +649,12 @@
 
 
 class Scatter:
-    AHEAD = 6
-
-    def __init__(self, parts, send_sem, recv_sem, line_sem, local_sem, n_fsdp, n_grp):
-        self.parts, self.n_grp = parts, n_grp
+    def __init__(
+        self, parts, groups, received, ahead, send_sem, recv_sem, line_sem, local_sem, n_fsdp, n_grp
+    ):
+        self.parts, self.groups, self.n_grp = parts, groups, n_grp
+        self.received, self.ahead = received, ahead
+        self.saved = []
         self.send_sem, self.recv_sem = send_sem, recv_sem
         self.line_sem, self.local_sem = line_sem, local_sem
         self.f, self.z = lax.axis_index("fsdp"), lax.axis_index("grp")
@@ -650,24 +719,48 @@
             kept.at[i, place], held.at[i, place], self.local_sem.at[part, i, place]
         )
 
+    def _fill(self, part, place, i):
+        away, arrived = self.parts[part][0], self.parts[part][3]
+        slot = self.slot(part, self.keeps[part][i], 0)
+        return pltpu.make_async_copy(
+            away.at[i, place], arrived.at[slot, place], self.recv_sem.at[part, slot, place]
+        )
+
     def _begin(self, part, place):
         away = self.parts[part][0]
         for i, k in reversed(list(enumerate(self.keeps[part]))):
-            self._cross(part, place, k ^ self.orders[part][0], 0, away.at[i, place])
-            self._load(part, place, i).start()
+            if part in self.received:
+                self._fill(part, place, i).start()
+            else:
+                self._cross(part, place, k ^ self.orders[part][0], 0, away.at[i, place])
+            if self.parts[part][1] is not None:
+                self._load(part, place, i).start()
 
     def _add_arrived(self, part, place, k):
         held, arrived = self.parts[part][2], self.parts[part][3]
         i = self.keeps[part].index(k)
-        self._load(part, place, i).wait()
+        if self.parts[part][1] is not None:
+            self._load(part, place, i).wait()
         for stage in range(self.stage_of(part, k)):
             slot = self.slot(part, k, stage)
-            self._arrived(arrived.at[slot, place], self.recv_sem.at[part, slot, place])
+            if stage == 0 and part in self.received:
+                self._fill(part, place, i).wait()
+            else:
+                self._arrived(arrived.at[slot, place], self.recv_sem.at[part, slot, place])
         total = held[i, place]
         for stage in range(self.stage_of(part, k)):
             total = total + arrived[self.slot(part, k, stage), place]
         held[i, place] = total
         return held.at[i, place]
+
+    def _save(self, part, place):
+        source = self._add_arrived(part, place, 0)
+        if self.parts[part][4] is None:
+            copy = pltpu.make_async_copy(
+                source, self.parts[part][6].at[place], self.local_sem.at[part, 0, place]
+            )
+            copy.start()
+            self.saved.append(copy)
 
     def _halve(self, part, place, k):
         source = self._add_arrived(part, place, k)
@@ -719,11 +812,12 @@
             places += [high] if low == high else [high, low]
             low, high = low + 1, high - 1
         units = []
-        for first in range(0, len(self.parts), 2):
-            group = range(first, min(first + 2, len(self.parts)))
+        for i, count in enumerate(self.groups):
+            first = sum(self.groups[:i])
+            group = range(first, first + count)
             units += [(part, place) for place in places for part in group]
-        ahead, stages = self.AHEAD, len(self.orders[0])
-        length = len(units) + ahead + 2 * stages + 2 * self.n_grp
+        ahead, stages = self.ahead, len(self.orders[0])
+        length = len(units) + ahead + 2 * stages + 4 * self.n_grp
         waves = [[] for _ in range(length)]
         final = {}
         for n, (part, place) in enumerate(units):
@@ -734,7 +828,9 @@
                     if self.stage_of(part, k) == stage:
                         waves[at].append(bind(self._halve, part, place, k))
                 at += 2
-            waves[at].append(bind(self._add_arrived, part, place, 0))
+            waves[at].append(bind(self._save, part, place))
+            if self.parts[part][4] is None:
+                continue
             for hop in range(self.n_grp - 1):
                 waves[at + 2 * hop].append(bind(self._line, part, place, hop))
             final[part] = at + 2 * (self.n_grp - 1)
@@ -743,6 +839,8 @@
         return waves
 
     def finish(self):
+        for copy in self.saved:
+            copy.wait()
         for condition, copies in self.sent:
             if condition is None:
                 for copy in copies:
@@ -756,30 +854,42 @@
                 pl.when(condition)(wait_sent)
 
 
-def scatter_scratch(aways, n_fsdp, n_grp):
+def scatter_buffers(kind, rows, width, n_fsdp, n_grp):
     m = n_fsdp.bit_length() - 2
     keep = n_fsdp // 4
     slots = m + sum(i << (m - 1 - i) for i in range(1, m))
-    parts = len(aways)
+    leading = {
+        "full": [(keep, n_grp), (slots, n_grp), (n_grp,), (n_grp,)],
+        "cross": [(keep, n_grp), (slots, n_grp)],
+    }[kind]
+    return [pltpu.VMEM(v + (rows, width), BF16) for v in leading]
+
+
+def scatter_scratch(kinds, sizes, n_fsdp, n_grp, parts=None):
+    m = n_fsdp.bit_length() - 2
+    keep = n_fsdp // 4
+    slots = m + sum(i << (m - 1 - i) for i in range(1, m))
+    parts = parts or len(kinds)
     shapes = [
         pltpu.SemaphoreType.DMA((parts, n_grp * (2 * keep + 2 * n_grp))),
         pltpu.SemaphoreType.DMA((parts, slots, n_grp)),
         pltpu.SemaphoreType.DMA((parts, 2, n_grp)),
         pltpu.SemaphoreType.DMA((parts, keep, n_grp)),
     ]
-    for away in aways:
-        rows, width = away.shape[2:]
-        for leading in ((keep, n_grp), (slots, n_grp), (n_grp,), (n_grp,)):
-            shapes.append(pltpu.VMEM(leading + (rows, width), BF16))
+    for kind, (rows, width) in zip(kinds, sizes):
+        shapes += scatter_buffers(kind, rows, width, n_fsdp, n_grp)
     return shapes
 
 
-def scatter_parts(aways, kepts, buffers, results):
-    parts = []
-    places = [(ref, columns) for ref, ranges in results for columns in ranges]
-    for i, (away, kept) in enumerate(zip(aways, kepts)):
-        parts.append((away, kept, *buffers[4 * i : 4 * i + 4], *places[i]))
-    return parts
+def scatter_parts(kinds, aways, kepts, buffers, results):
+    parts, buffers = [], list(buffers)
+    for kind, away, kept, result in zip(kinds, aways, kepts, results):
+        count = {"full": 4, "cross": 2}[kind]
+        mine, buffers = buffers[:count], buffers[count:]
+        if kind == "cross":
+            mine = mine + [None, None]
+        parts.append((away, kept, *mine, *result))
+    return parts, buffers
 
 
 def column_ranges(widths):
@@ -790,47 +900,231 @@
     return ranges
 
 
-def scatter_kernel(widths, n_fsdp, n_grp, *refs):
-    count = sum(len(w) for w in widths)
-    aways, kepts, refs = refs[:count], refs[count : 2 * count], refs[2 * count :]
-    results, sems, buffers = refs[: len(widths)], refs[len(widths) :][:4], refs[len(widths) + 4 :]
-    meet(n_fsdp, n_grp, True)
-    places = [(ref, column_ranges(w)) for ref, w in zip(results, widths)]
-    scatter = Scatter(scatter_parts(aways, kepts, buffers, places), *sems, n_fsdp, n_grp)
-    for wave in scatter.waves():
-        for step in wave:
-            step()
+def last_kernel(widths, lines, n_fsdp, n_grp, *refs):
+    mixed_ref, narrow_ref, l_ref, l_other_ref, w_hbm, forget_ref = refs[:6]
+    tokens_ref, scale_ref, gain_ref, resid_ref, small_ref = refs[6:11]
+    count, more = len(widths), sum(len(w) for w in lines)
+    lined, refs = refs[11 : 11 + more], refs[11 + more :]
+    wide_ref, narrow_result, grad_ref, dgain_refs = refs[0], refs[1], refs[2], refs[3:6]
+    results, refs = refs[6 : 6 + len(lines)], refs[6 + len(lines) :]
+    sems, refs = refs[:4], refs[4:]
+    ranges = column_ranges(widths)
+    gathered_refs, aways, refs = refs[:more], refs[more : more + count], refs[more + count :]
+    places = [(wide_ref, c) for c in ranges[:-1]] + [(narrow_result, pl.ds(0, widths[-1]))]
+    parts, refs = scatter_parts(["full"] * count, aways, [None] * count, refs, places)
+    mixed_other, narrow_other, rows_ref, w_ref, act_ref, incoming, send_sem, recv_sem, w_sem, own_sem, group_send, group_recv, total_ref = refs
+    f, z = lax.axis_index("fsdp"), lax.axis_index("grp")
+    tok, width = act_ref.shape
+    pieces = n_fsdp // 2
+
+    meet(n_fsdp, n_grp, False)
+
+    def exchange(source, target, index, peer):
+        return pltpu.make_async_remote_copy(
+            src_ref=source,
+            dst_ref=target,
+            send_sem=send_sem.at[index],
+            recv_sem=recv_sem.at[index],
+            device_id=peer,
+            device_id_type=MESH,
+        )
+
+    sibling = {"fsdp": flip(f, 1), "grp": z}
+    others = []
+    for i in range(count):
+        if i < count - 1:
+            pair = (mixed_ref.at[:, ranges[i]], mixed_other.at[:, ranges[i]])
+        else:
+            pair = (narrow_ref, narrow_other)
+        others.append(exchange(*pair, i, sibling))
+        others[-1].start()
+
+    chunk = w_ref.shape[2]
+    chunks = w_hbm.shape[1] // chunk
+
+    def fetch(i):
+        return pltpu.make_async_copy(
+            w_hbm.at[:, pl.ds(i * chunk, chunk)], w_ref.at[i % 2], w_sem.at[i % 2]
+        )
+
+    fetch(0).start()
+    for k in range(pieces):
+        row = flip(f // 2, k) * 2 + f % 2
+        rows_ref[k, :, :tok] = l_ref[row]
+        rows_ref[k, :, tok:] = l_other_ref[row]
+
+    scatter = Scatter(parts, [count], (), AHEAD, *sems, n_fsdp, n_grp)
+    waves = iter(scatter.waves())
+
+    def advance(steps=None):
+        for wave in itertools.islice(waves, steps):
+            for step in wave:
+                step()
+
+    direct = GroupExchange(n_grp, group_send, group_recv)
+    own = []
+    for i, (source, target) in enumerate(zip(lined, gathered_refs)):
+        direct.send(
+            i, i, lambda place, source=source: source.at[place],
+            lambda place, target=target: target.at[place],
+        )
+        own.append(pltpu.make_async_copy(source.at[z], target.at[z], own_sem.at[i]))
+        own[-1].start()
+
+    def products(part, ks, target):
+        if part < count - 1:
+            right = (mixed_ref[:, ranges[part]], mixed_other[:, ranges[part]])
+        else:
+            right = (narrow_ref[...], narrow_other[...])
+        right = jnp.concatenate(right, axis=0)
+        left = jnp.concatenate([rows_ref[k] for k in ks], axis=0)
+        value = jnp.dot(left, right, preferred_element_type=F32).astype(BF16)
+        target[...] = value.reshape(target.shape)
+
+    for part in range(count):
+        others[part].wait_recv()
+        first = scatter.orders[part][0]
+        products(part, [k ^ first for k in scatter.keeps[part]], aways[part])
+    advance(1)
+    for part in range(count):
+        products(part, scatter.keeps[part], parts[part][2])
+    act_ref[...] = dot_lanes(narrow_ref[...], forget_ref[...])
+    for i in range(chunks):
+        if i + 1 < chunks:
+            fetch(i + 1).start()
+        fetch(i).wait()
+        act_ref[...] += dot_lanes(mixed_ref[:, pl.ds(i * chunk, chunk)], w_ref[i % 2])
+        advance(1)
+
+    block = next(t for t in (64, 32, 16, 8) if tok % t == 0)
+    total_ref[0] = small_ref[...]
+
+    def finish_rows(i, carry):
+        rows = pl.ds(pl.multiple_of(i * block, block), block)
+        scale = scale_ref[rows, :]
+        normed = tokens_ref[rows, :].astype(F32) * scale
+        act = act_ref[rows, :]
+        total_ref[0, :, :width] += jnp.sum(act * normed, axis=0, keepdims=True)
+        scaled = act * gain_ref[...]
+        average = jnp.mean(scaled * normed, axis=1, keepdims=True)
+        grad_ref[rows, :] = (
+            resid_ref[rows, :] + scale * (scaled - normed * average)
+        ).astype(BF16)
+        return carry
+
+    lax.fori_loop(0, tok // block, finish_rows, 0)
+    peers = [{"fsdp": f, "grp": flip(z, 1 << i)} for i in range(n_grp.bit_length() - 1)]
+    peers += [{"fsdp": flip(f, 1 << i), "grp": z} for i in range(n_fsdp.bit_length() - 1)]
+    sent = []
+    for i, peer in enumerate(peers):
+        copy = exchange(total_ref.at[i], incoming.at[i], count + i, peer)
+        copy.start()
+        sent.append(copy)
+        advance(1)
+        copy.wait_recv()
+        total_ref[i + 1] = total_ref[i] + incoming[i]
+    total = total_ref[len(peers)]
+    for ref, start in zip(dgain_refs, (0, width, 2 * width)):
+        ref[...] = total[:, start : start + ref.shape[1]]
+    advance()
+    i = 0
+    for ref, line in zip(results, lines):
+        for columns in column_ranges(line):
+            own[i].wait()
+            direct.wait(i)
+            value = gathered_refs[i][0].astype(F32)
+            for place in range(1, n_grp):
+                value = value + gathered_refs[i][place].astype(F32)
+            ref[:, columns] = value
+            i += 1
     scatter.finish()
-
-
-def scatter_rows(weights, collective_id):
+    direct.finish()
+    for copy in others + sent:
+        copy.wait_send()
+
+
+def last_gradients(
+    acts, mixed, narrow, w_qkv, forget, tokens, scale, gain, resid, small, lines, collective_id
+):
     n_fsdp, n_grp = lax.axis_size("fsdp"), lax.axis_size("grp")
-    aways = [away for parts in weights for away, _ in parts]
-    kepts = [kept for parts in weights for _, kept in parts]
-    widths = [[away.shape[3] for away, _ in parts] for parts in weights]
+    tok, wide = mixed.shape
+    width = tokens.shape[1]
+    own_rows = width // (n_fsdp * n_grp)
+    split = 4 if wide % 512 == 0 else 2
+    more = sum(len(w) for w in lines)
+    widths = [wide // split] * split + [narrow.shape[1]]
+    keep = n_fsdp // 4
+    rounds = n_fsdp.bit_length() + n_grp.bit_length() - 2
+    aways = [jax.ShapeDtypeStruct((keep, n_grp, own_rows, w), BF16) for w in widths]
+    chunk = next(t for t in (512, 384, 256, 128) if wide % t == 0)
+    vmem = pl.BlockSpec(memory_space=pltpu.VMEM)
+    anywhere = pl.BlockSpec(memory_space=pl.ANY)
     return pl.pallas_call(
-        functools.partial(scatter_kernel, widths, n_fsdp, n_grp),
+        functools.partial(
+            last_kernel, widths, [[v.shape[2] for v in w] for w in lines], n_fsdp, n_grp
+        ),
         out_shape=[
-            jax.ShapeDtypeStruct((parts[0][0].shape[2], sum(w)), F32)
-            for parts, w in zip(weights, widths)
+            jax.ShapeDtypeStruct((own_rows, wide), F32),
+            jax.ShapeDtypeStruct((own_rows, widths[-1]), F32),
+            jax.ShapeDtypeStruct(tokens.shape, BF16),
+            jax.ShapeDtypeStruct((1, width), F32),
+            jax.ShapeDtypeStruct((1, width), F32),
+            jax.ShapeDtypeStruct((1, widths[-1]), F32),
+        ]
+        + [
+            jax.ShapeDtypeStruct((w[0].shape[1], sum(v.shape[2] for v in w)), F32) for w in lines
         ],
-        in_specs=[pl.BlockSpec(memory_space=pl.ANY)] * (2 * len(aways)),
-        out_specs=[pl.BlockSpec(memory_space=pltpu.VMEM)] * len(weights),
-        scratch_shapes=scatter_scratch(aways, n_fsdp, n_grp),
+        in_specs=[vmem] * 4
+        + [anywhere]
+        + [vmem] * 6
+        + [anywhere] * sum(len(w) for w in lines),
+        out_specs=[vmem] * (6 + len(lines)),
+        scratch_shapes=scatter_scratch([], [], n_fsdp, n_grp, len(widths))
+        + [pltpu.VMEM(v.shape, BF16) for w in lines for v in w]
+        + [pltpu.VMEM(a.shape, BF16) for a in aways]
+        + [v for a in aways for v in scatter_buffers("full", *a.shape[2:], n_fsdp, n_grp)]
+        + [
+            pltpu.VMEM(mixed.shape, BF16),
+            pltpu.VMEM(narrow.shape, BF16),
+            pltpu.VMEM((n_fsdp // 2, n_grp * own_rows, 2 * tok), BF16),
+            pltpu.VMEM((2, width, chunk), BF16),
+            pltpu.VMEM((tok, width), F32),
+            pltpu.VMEM((rounds, 1, small.shape[1]), F32),
+            pltpu.SemaphoreType.DMA((len(widths) + rounds,)),
+            pltpu.SemaphoreType.DMA((len(widths) + rounds,)),
+            pltpu.SemaphoreType.DMA((2,)),
+            pltpu.SemaphoreType.DMA((max(1, more),)),
+            pltpu.SemaphoreType.DMA((max(1, more), n_grp)),
+            pltpu.SemaphoreType.DMA((max(1, more), n_grp)),
+            pltpu.VMEM((rounds + 1, 1, small.shape[1]), F32),
+        ],
         compiler_params=pltpu.CompilerParams(
             collective_id=collective_id, has_side_effects=True, vmem_limit_bytes=58 << 20
         ),
-        name="scatter_rows",
-    )(*aways, *kepts)
-
-
-def backward_kernel(widths, pairs, head_size, n_fsdp, n_grp, *refs):
+        name="last_gradients",
+    )(
+        mixed, narrow, acts[0], acts[1], w_qkv, forget, tokens, scale, gain, resid, small,
+        *(v for w in lines for v in w),
+    )
+
+
+def backward_kernel(kinds, widths, received, pairs, head_size, n_fsdp, n_grp, *refs):
     count = sum(len(w) for w in widths)
     aways, kepts, refs = refs[:count], refs[count : 2 * count], refs[2 * count :]
     slots_ref, grad_ref, x_hbm, c_ref, mask_ref, seen_ref, lse_ref = refs[:7]
-    results, refs = refs[7 : 7 + len(widths)], refs[7 + len(widths) :]
+    refs = refs[7:]
+    results, part_kinds = [], []
+    for kind, w in zip(kinds, widths):
+        if kind == "full":
+            results += [(refs[0], columns) for columns in column_ranges(w)]
+            refs = refs[1:]
+        else:
+            results += [(ref, None) for ref in refs[: len(w)]]
+            refs = refs[len(w) :]
+        part_kinds += [kind] * len(w)
     mixed_out, logs_out = refs[:2]
-    sems, buffers, refs = refs[2:6], refs[6 : 6 + 4 * count], refs[6 + 4 * count :]
+    sems = refs[2:6]
+    parts, refs = scatter_parts(part_kinds, aways, kepts, refs[6:], results)
     x_refs, refs = refs[:pairs], refs[pairs:]
     do_refs, refs = refs[:pairs], refs[pairs:]
     dx_refs, refs = refs[:pairs], refs[pairs:]
@@ -842,8 +1136,7 @@
     z = lax.axis_index("grp")
 
     meet(n_fsdp, n_grp, False)
-    places = [(ref, column_ranges(w)) for ref, w in zip(results, widths)]
-    scatter = Scatter(scatter_parts(aways, kepts, buffers, places), *sems, n_fsdp, n_grp)
+    scatter = Scatter(parts, [len(w) for w in widths], received, AHEAD, *sems, n_fsdp, n_grp)
     swap_heads = GroupExchange(n_grp, send_sem, recv_sem)
     started = itertools.count()
 
@@ -920,7 +1213,9 @@
         copy.wait()
 
 
-def backward_attention(weights, slots, grad, x, decay, masks, seen, lse, head_size, collective_id):
+def backward_attention(
+    kinds, weights, received, slots, grad, x, decay, masks, seen, lse, head_size, collective_id
+):
     n_fsdp, n_grp = lax.axis_size("fsdp"), lax.axis_size("grp")
     aways = [away for parts in weights for away, _ in parts]
     kepts = [kept for parts in weights for _, kept in parts]
@@ -929,12 +1224,21 @@
     lanes = decay.shape[2]
     anywhere = pl.BlockSpec(memory_space=pl.ANY)
     vmem = pl.BlockSpec(memory_space=pltpu.VMEM)
+    shapes, specs = [], []
+    for kind, parts, w in zip(kinds, weights, widths):
+        own_rows = parts[0][0].shape[2]
+        if kind == "full":
+            shapes.append(jax.ShapeDtypeStruct((own_rows, sum(w)), F32))
+            specs.append(vmem)
+        else:
+            shapes += [jax.ShapeDtypeStruct((n_grp, own_rows, v), BF16) for v in w]
+            specs += [anywhere] * len(w)
+    part_kinds = [kind for kind, w in zip(kinds, widths) for _ in w]
     out = pl.pallas_call(
-        functools.partial(backward_kernel, widths, pairs, head_size, n_fsdp, n_grp),
-        out_shape=[
-            jax.ShapeDtypeStruct((parts[0][0].shape[2], sum(w)), F32)
-            for parts, w in zip(weights, widths)
-        ]
+        functools.partial(
+            backward_kernel, kinds, widths, received, pairs, head_size, n_fsdp, n_grp
+        ),
+        out_shape=shapes
         + [
             jax.ShapeDtypeStruct((tok, 3 * grad.shape[1]), BF16),
             jax.ShapeDtypeStruct((n_grp, tok, lanes), F32),
@@ -942,8 +1246,10 @@
         in_specs=[anywhere] * (2 * len(aways))
         + [pl.BlockSpec(memory_space=pltpu.SMEM), anywhere, anywhere]
         + [vmem] * 4,
-        out_specs=[vmem] * len(weights) + [anywhere] * 2,
-        scratch_shapes=scatter_scratch(aways, n_fsdp, n_grp)
+        out_specs=specs + [anywhere] * 2,
+        scratch_shapes=scatter_scratch(
+            part_kinds, [v.shape[2:] for v in aways], n_fsdp, n_grp
+        )
         + [pltpu.VMEM((n_grp, 3, tok, pair_width), BF16)] * pairs
         + [pltpu.VMEM((n_grp, tok, pair_width), BF16)] * pairs
         + [pltpu.VMEM((n_grp, 3, tok, pair_width), BF16)] * pairs
@@ -958,57 +1264,216 @@
         ),
         name="backward_attention",
     )(*aways, *kepts, slots, grad, x, decay, masks, seen, lse)
-    return out[: len(weights)], out[len(weights)], out[len(weights) + 1]
-
-
-def weight_grad_kernel(count, own_ids, other_ids, l_ref, l_other_ref, r_ref, r_other_ref, *outs):
-    def side(ref, ids):
-        return jnp.concatenate([ref[ids[k]] for k in range(2 * count)], axis=0)
-
-    total = jnp.dot(side(l_ref, own_ids), r_ref[...], preferred_element_type=F32)
-    total = total + jnp.dot(
-        side(l_other_ref, other_ids), r_other_ref[...], preferred_element_type=F32
+    return out[:-2], out[-2], out[-1]
+
+
+def feed_forward_kernel(
+    o_ref,
+    tokens_ref,
+    grad_ref,
+    gain_ref,
+    w_out_ref,
+    gate_ref,
+    up_ref,
+    down_ref,
+    inner_ref,
+    dgate_ref,
+    dup_ref,
+    o_turned_ref,
+    act_turned_ref,
+    out_ref,
+    dresid_ref,
+    dbranch_ref,
+    do_ref,
+    dgain_ref,
+    resid_ref,
+    act_ref,
+    sum_ref,
+    dact_ref,
+):
+    tok = o_ref.shape[0]
+    block = next(t for t in (128, 64, 32, 16, 8) if tok % t == 0)
+
+    def rows_of(i):
+        return pl.ds(pl.multiple_of(i * block, block), block)
+
+    def norm(rows):
+        resid = resid_ref[rows, :]
+        scale = lax.rsqrt(jnp.mean(resid * resid, axis=1, keepdims=True) + EPSILON)
+        return resid, resid * scale, scale
+
+    @pl.when(pl.program_id(0) == 0)
+    def _():
+        def begin(i, carry):
+            rows = rows_of(i)
+            resid_ref[rows, :] = tokens_ref[rows, :].astype(F32) + jnp.dot(
+                o_ref[rows, :], w_out_ref[...], preferred_element_type=F32
+            )
+            _, normed, _ = norm(rows)
+            act_ref[rows, :] = (normed * gain_ref[...]).astype(BF16)
+            return carry
+
+        lax.fori_loop(0, tok // block, begin, 0)
+        sum_ref[...] = jnp.zeros_like(sum_ref)
+        dact_ref[...] = jnp.zeros_like(dact_ref)
+        o_turned_ref[...] = o_ref[...].T
+        act_turned_ref[...] = act_ref[...].T
+
+    act = act_ref[...]
+    gate = jnp.dot(act, gate_ref[...], preferred_element_type=F32)
+    up = jnp.dot(act, up_ref[...], preferred_element_type=F32)
+    grad_inner = dot_lanes(grad_ref[...], down_ref[...])
+    sigma = jax.nn.sigmoid(gate)
+    swish = gate * sigma
+    inner = (swish * up).astype(BF16)
+    dgate = (grad_inner * up * (sigma * (1.0 + gate * (1.0 - sigma)))).astype(BF16)
+    dup = (grad_inner * swish).astype(BF16)
+    inner_ref[...] = inner.T
+    dgate_ref[...] = dgate
+    dup_ref[...] = dup
+    sum_ref[...] += jnp.dot(inner, down_ref[...], preferred_element_type=F32)
+    dact_ref[...] += dot_lanes(dgate, gate_ref[...]) + dot_lanes(dup, up_ref[...])
+
+    @pl.when(pl.program_id(0) == pl.num_programs(0) - 1)
+    def _():
+        dgain_ref[...] = jnp.zeros_like(dgain_ref)
+
+        def end(i, carry):
+            rows = rows_of(i)
+            resid, normed, scale = norm(rows)
+            out_ref[rows, :] = (resid + sum_ref[rows, :]).astype(BF16)
+            dact = dact_ref[rows, :]
+            dgain_ref[...] += jnp.sum(dact * normed, axis=0, keepdims=True)
+            scaled = dact * gain_ref[...]
+            average = jnp.mean(scaled * normed, axis=1, keepdims=True)
+            dresid = grad_ref[rows, :].astype(F32) + scale * (scaled - normed * average)
+            dresid_ref[rows, :] = dresid
+            dbranch = dresid.astype(BF16)
+            dbranch_ref[rows, :] = dbranch
+            do_ref[rows, :] = dot_lanes(dbranch, w_out_ref[...]).astype(BF16)
+            return carry
+
+        lax.fori_loop(0, tok // block, end, 0)
+
+
+def feed_forward(attn_o, tokens, grad, gain, w_out, gate_up, down):
+    tok, width = tokens.shape
+    hidden = down.shape[0]
+    tile = 512
+    steps = hidden // tile
+    once = lambda rows, columns: pl.BlockSpec(
+        (rows, columns), lambda j: (0, 0), pipeline_mode=pl.Buffered(1)
+    )
+    rows = once(tok, width)
+    columns = pl.BlockSpec((tok, tile), lambda j: (0, j))
+    low = lambda *shape: jax.ShapeDtypeStruct(shape, BF16)
+    return pl.pallas_call(
+        feed_forward_kernel,
+        out_shape=[
+            low(hidden, tok),
+            low(tok, hidden),
+            low(tok, hidden),
+            low(width, tok),
+            low(width, tok),
+            low(tok, width),
+            jax.ShapeDtypeStruct((tok, width), F32),
+            low(tok, width),
+            low(tok, width),
+            jax.ShapeDtypeStruct((1, width), F32),
+        ],
+        grid=(steps,),
+        in_specs=[
+            rows,
+            rows,
+            rows,
+            once(1, width),
+            once(width, width),
+            pl.BlockSpec((width, tile), lambda j: (0, j)),
+            pl.BlockSpec((width, tile), lambda j: (0, steps + j)),
+            pl.BlockSpec((tile, width), lambda j: (j, 0)),
+        ],
+        out_specs=[
+            pl.BlockSpec((tile, tok), lambda j: (j, 0)),
+            columns,
+            columns,
+            once(width, tok),
+            once(width, tok),
+            rows,
+            rows,
+            rows,
+            rows,
+            once(1, width),
+        ],
+        scratch_shapes=[
+            pltpu.VMEM((tok, width), F32),
+            pltpu.VMEM((tok, width), BF16),
+            pltpu.VMEM((tok, width), F32),
+            pltpu.VMEM((tok, width), F32),
+        ],
+        compiler_params=pltpu.CompilerParams(vmem_limit_bytes=60 << 20),
+        cost_estimate=pl.CostEstimate(
+            flops=12 * tok * width * hidden,
+            bytes_accessed=6 * width * hidden,
+            transcendentals=tok * hidden,
+        ),
+        name="feed_forward",
+    )(attn_o, tokens, grad, gain, w_out, gate_up, gate_up, down)
+
+
+def weight_grad_kernel(count, ids, *refs):
+    own, other, (r_ref, r_other_ref, *outs) = (
+        refs[: 2 * count],
+        refs[2 * count : 4 * count],
+        refs[4 * count :],
+    )
+    rows = [jnp.concatenate([ref[0] for ref in side], axis=0) for side in (own, other)]
+    total = jnp.dot(
+        jnp.concatenate(rows, axis=1),
+        jnp.concatenate([r_ref[...], r_other_ref[...]], axis=0),
+        preferred_element_type=F32,
     )
     total = total.astype(BF16).reshape(2 * count, -1, total.shape[1])
     outs[0][...] = total[:count]
     outs[1][...] = total[count:]
 
 
-def weight_grad(own_ids, other_ids, l_own, l_other, r_own, r_other, start, width):
-    count = own_ids.shape[0] // 2
+def weight_grad(ids, l_own, l_other, r_own, r_other, start, width):
+    count = ids.shape[0] // 2
     _, rows, tok = l_own.shape
-    limit = 1536 if rows * count < 1024 else 512
+    limit = 1024 if rows * count < 1024 else 384
     tile = max(t for t in range(128, limit + 1, 128) if width % t == 0 and start % t == 0)
     steps, first = width // tile, start // tile
-    whole = lambda v: pl.BlockSpec(v.shape, lambda n, own, other: (0, 0, 0))
-    r_spec = pl.BlockSpec((tok, tile), lambda n, own, other: (0, first + n))
-    out_spec = pl.BlockSpec((count, rows, tile), lambda n, own, other: (0, 0, n))
+    pieces = [
+        pl.BlockSpec(
+            (1, rows, tok), lambda n, ids, k=k: (ids[k], 0, 0), pipeline_mode=pl.Buffered(1)
+        )
+        for k in range(2 * count)
+    ]
+    r_spec = pl.BlockSpec((tok, tile), lambda n, ids: (0, first + n))
+    out_spec = pl.BlockSpec((count, rows, tile), lambda n, ids: (0, 0, n))
     return pl.pallas_call(
         functools.partial(weight_grad_kernel, count),
         out_shape=[jax.ShapeDtypeStruct((count, rows, width), BF16)] * 2,
         grid_spec=pltpu.PrefetchScalarGridSpec(
-            num_scalar_prefetch=2,
+            num_scalar_prefetch=1,
             grid=(steps,),
-            in_specs=[whole(l_own), whole(l_other), r_spec, r_spec],
+            in_specs=pieces * 2 + [r_spec, r_spec],
             out_specs=[out_spec, out_spec],
         ),
-        compiler_params=pltpu.CompilerParams(vmem_limit_bytes=48 << 20),
+        compiler_params=pltpu.CompilerParams(vmem_limit_bytes=60 << 20),
         cost_estimate=pl.CostEstimate(
             flops=8 * count * rows * tok * width,
             bytes_accessed=2 * (2 * count * rows * width + 2 * tok * width),
             transcendentals=0,
         ),
         name="weight_grad",
-    )(own_ids, other_ids, l_own, l_other, r_own, r_other)
-
-
-def split_rows(left):
+    )(ids, *[l_own] * (2 * count), *[l_other] * (2 * count), r_own, r_other)
+
+
+def both_cores(turned):
     n_fsdp = lax.axis_size("fsdp")
-    turned = left.T.reshape(n_fsdp, left.shape[1] // n_fsdp, left.shape[0])
-    parity = lax.axis_index("fsdp") % 2
-    halves = turned.reshape(n_fsdp // 2, 2, *turned.shape[1:])
-    away = lax.dynamic_index_in_dim(halves, 1 - parity, 1, keepdims=False)
-    return turned, swap(away, "fsdp", 1)
+    turned = turned.reshape(n_fsdp, turned.shape[0] // n_fsdp, turned.shape[1])
+    return turned, swap(turned, "fsdp", 1)
 
 
 def partial_rows(left, columns):
@@ -1020,21 +1485,12 @@
         keep = kept_pieces(order)
         ids = jnp.stack([flip(f // 2, k) for k in [k ^ order[0] for k in keep] + keep])
         pair = weight_grad(
-            2 * ids + f % 2, ids, left[0], left[1], right, right_other, start, width
+            2 * ids + f % 2, left[0], left[1], right, right_other, start, width
         )
         parts.append(
             tuple(v.reshape(v.shape[0], n_grp, v.shape[1] // n_grp, width) for v in pair)
         )
     return parts
-
-
-def sum_everywhere(values):
-    for axis in ("grp", "fsdp"):
-        mask = 1
-        while mask < lax.axis_size(axis):
-            values = values + swap(values, axis, mask)
-            mask *= 2
-    return values
 
 
 def norm_rows(features):
@@ -1086,14 +1542,17 @@
     seen_low = seen.astype(BF16)
 
     forget_pad = 128 - heads
-    qkv_full, forget_full = gather_rows(
-        [w_qkv, jnp.pad(w_forget, ((0, 0), (0, forget_pad)))], 1
-    )
+    qkv_full, forget_full, out_line, down_line = gather_rows(
+        ("full", "full", "line", "line"),
+        [w_qkv, jnp.pad(w_forget, ((0, 0), (0, forget_pad))), w_out, w_down],
+        1,
+    )
+    qkv_full, forget_full = (v.reshape(-1, v.shape[2]) for v in (qkv_full, forget_full))
     inputs = tokens.astype(F32)
     normed_one, scale_one = norm_rows(inputs)
     acts = (normed_one * gain_attn).astype(BF16)
     grad_out_other = swap(grad_out, "fsdp", 1)
-    acts_rows = split_rows(acts)
+    acts_rows = both_cores(acts.T)
     logits = jnp.dot(acts, forget_full, preferred_element_type=F32)[:, :heads] + b_forget
     log_keep = jax.nn.log_sigmoid(logits)
     mixed = jnp.dot(acts, qkv_full, preferred_element_type=F32).astype(BF16)
@@ -1102,49 +1561,40 @@
         log_keep.T.reshape(blocks, own_heads, tok), ((0, 0), (0, 8 - own_heads), (0, 0))
     )
     (out_full, gate_up_full, down_full), (attn_o, x, lse, decay) = forward_attention(
-        [w_out, w_gate_up, w_down], slots, mixed, logs, masks, seen_low, head_size, 2
-    )
-
-    attn_rows = split_rows(attn_o)
-    resid = inputs + jnp.dot(attn_o, out_full, preferred_element_type=F32)
-    normed_two, scale_two = norm_rows(resid)
-    acts_two = (normed_two * gain_ffn).astype(BF16)
-    acts_two_rows = split_rows(acts_two)
-    ffn_width = down_full.shape[0]
-    both = jnp.dot(acts_two, gate_up_full, preferred_element_type=F32)
-    gate = both[:, :ffn_width]
-    up_part = both[:, ffn_width:]
-    sigma = jax.nn.sigmoid(gate)
-    swish = gate * sigma
-    inner_act = (swish * up_part).astype(BF16)
-    half = width // 2
-    down_rows = split_rows(inner_act)
-    result = resid + jnp.dot(inner_act, down_full, preferred_element_type=F32)
-    output = result.astype(BF16)
-
-    grad_inner = contract_cols(grad_out, down_full)
-    slope = sigma * (1.0 + gate * (1.0 - sigma))
-    grad_both = jnp.concatenate(
-        [grad_inner * up_part * slope, grad_inner * swish], axis=1
-    ).astype(BF16)
-    grad_both_other = swap(grad_both, "fsdp", 1)
-    grad_acts_two = contract_cols(grad_both, gate_up_full)
-    gain_two_grad = jnp.sum(grad_acts_two * normed_two, axis=0)
-    grad_resid = grad_out.astype(F32) + norm_back(
-        grad_acts_two * gain_ffn, normed_two, scale_two
-    )
-    grad_branch = grad_resid.astype(BF16)
+        ("lined", "full", "lined"), [out_line, w_gate_up, down_line], slots, mixed, logs, masks, seen_low, head_size, 2
+    )
+
+    half, hidden = width // 2, down_full.shape[0]
+    (
+        inner_turned,
+        grad_gate,
+        grad_up,
+        attn_turned,
+        acts_two_turned,
+        output,
+        grad_resid,
+        grad_branch,
+        grad_heads,
+        gain_two_grad,
+    ) = feed_forward(attn_o, tokens, grad_out, gain_ffn[None], out_full, gate_up_full, down_full)
+    down_rows = both_cores(inner_turned)
+    acts_two_rows = both_cores(acts_two_turned)
+    attn_rows = both_cores(attn_turned)
     grad_branch_other = swap(grad_branch, "fsdp", 1)
-    grad_heads = contract_cols(grad_branch, out_full).astype(BF16)
     part_down = partial_rows(
         down_rows, [(grad_out, grad_out_other, 0, half), (grad_out, grad_out_other, half, half)]
     )
+    orders = halving_orders(lax.axis_size("fsdp"))
+    part_down, grad_gate, grad_up, grad_branch = lax.optimization_barrier(
+        (part_down, grad_gate, grad_up, grad_branch)
+    )
+    part_down = [
+        (swap(away, "fsdp", 2 * order[0]), kept)
+        for (away, kept), order in zip(part_down, orders)
+    ]
     part_gate_up = partial_rows(
         acts_two_rows,
-        [
-            (grad_both, grad_both_other, 0, ffn_width),
-            (grad_both, grad_both_other, ffn_width, ffn_width),
-        ],
+        [(v, swap(v, "fsdp", 1), 0, hidden) for v in (grad_gate, grad_up)],
     )
     part_out = partial_rows(
         attn_rows,
@@ -1154,8 +1604,10 @@
         ],
     )
 
-    (grad_down, grad_gate_up, grad_out_w), grad_mixed, log_grad = backward_attention(
+    sums, grad_mixed, log_grad = backward_attention(
+        ("cross", "full", "cross"),
         [part_down, part_gate_up, part_out],
+        range(len(part_down)),
         slots,
         grad_heads,
         x,
@@ -1168,35 +1620,41 @@
     )
     log_grad = log_grad[:, :, :own_heads].transpose(1, 0, 2).reshape(tok, heads)
     grad_logits = (log_grad * jax.nn.sigmoid(-logits)).astype(BF16)
-    part = 3 * width // 2
     narrow = jnp.pad(grad_logits, ((0, 0), (0, forget_pad)))
-    last = jnp.concatenate([grad_mixed[:, part:], narrow], axis=1)
-    part_qkv = partial_rows(
+    bias_grad = jnp.sum(narrow.astype(F32), axis=0)
+    (
+        grad_qkv,
+        grad_forget,
+        grad_tokens,
+        grad_gain,
+        grad_gain_two,
+        grad_bias,
+        grad_down,
+        grad_out_w,
+    ) = last_gradients(
         acts_rows,
-        [
-            (grad_mixed, swap(grad_mixed, "fsdp", 1), 0, part),
-            (last, swap(last, "fsdp", 1), 0, part + 128),
-        ],
-    )
-    (grad_wide,) = scatter_rows([part_qkv], 4)
-    grad_qkv, grad_forget = grad_wide[:, : 3 * width], grad_wide[:, 3 * width :][:, :heads]
-    grad_acts = contract_cols(grad_mixed, qkv_full) + contract_cols(
-        grad_logits, forget_full[:, :heads]
-    )
-    gain_one_grad = jnp.sum(grad_acts * normed_one, axis=0)
-    bias_grad = jnp.sum(grad_logits.astype(F32), axis=0)
-    grad_inputs = grad_resid + norm_back(grad_acts * gain_attn, normed_one, scale_one)
-    small = sum_everywhere(jnp.concatenate([gain_one_grad, gain_two_grad, bias_grad]))
+        grad_mixed,
+        narrow,
+        qkv_full,
+        forget_full,
+        tokens,
+        scale_one,
+        gain_attn[None],
+        grad_resid,
+        jnp.concatenate([jnp.zeros((width,), F32), gain_two_grad[0], bias_grad])[None],
+        [sums[:2], sums[3:]],
+        4,
+    )
     return (
         output,
-        grad_inputs.astype(BF16),
-        small[:width],
+        grad_tokens,
+        grad_gain[0],
         grad_qkv,
-        grad_forget,
-        small[2 * width :],
+        grad_forget[:, :heads],
+        grad_bias[0, :heads],
         grad_out_w,
-        small[width : 2 * width],
-        grad_gate_up,
+        grad_gain_two[0],
+        sums[2],
         grad_down,
     )
 

time: 872 us -> 731 us (0.84)
  matrix products: 101 us -> 12.9 us
  local copies, waits for them, and re-layouts: 69.6 us -> 24 us
  waiting for transfers between devices: 2.64 us -> 20.7 us
  other arithmetic: 22.9 us -> 7.14 us
    dot_general x8 -> x0, matrix products: 86.4 us -> none  [the longest x5 53.7 us: contract_cols(): lax.dot_general(first_op, second_op, (((1,), (1,)), ((), ())), preferred_...]
    pallas_call x8 -> x6, Pallas kernels: 63.4 us -> 43.4 us  [weight_grad(): pl.pallas_call(functools.partial(weight_grad_kernel, count), out_shape=[j...]
    ppermute x14 -> x10, waiting for transfers between devices: 2.64 us -> 20.7 us  [swap(): lax.ppermute(value, axis, [(i, i ^ mask) for i in range(lax.axis_size(axi...]
    dynamic_slice x2 -> x0, local copies, waits for them, and re-layouts: 15 us -> none  [split_rows(): away = lax.dynamic_index_in_dim(halves, 1 - parity, 1, keepdims=False)]
    pallas_call x4 -> x5, Pallas kernels: 598 us -> 610 us  [the longest x1 194 us: forward_attention(): pl.pallas_call(functools.partial(forward_kernel, kinds, pairs, head_size,...]
    unnamed x109 -> x55, local copies, waits for them, and re-layouts: 24.3 us -> 12.7 us
    convert_element_type x2 -> x1, other arithmetic: 9.88 us -> 0.06 us  [on_device(): grad_logits = (log_grad * jax.nn.sigmoid(-logits)).astype(BF16)]
  transfers between devices with their start and end apart: 14 -> 10, of which waited for: 3 -> 5; matrix products, arithmetic and copies ran while one was open for 10% -> 1% of each run, Pallas kernels for 4% -> 30%
where the time goes in v3:
time: 731 us; the launch traced here: 724 us
  Pallas kernels  653 us (89%)
  local copies, waits for them, and re-layouts  24 us (3%)
  waiting for transfers between devices  20.7 us (3%)
  matrix products  12.9 us (2%)
    pallas_call x1, Pallas kernels, forward_attention(): pl.pallas_call(functools.partial(forward_kernel, kinds, pairs, head_size,...  194 us
    pallas_call x1, Pallas kernels, backward_attention(): pl.pallas_call(functools.partial(backward_kernel, kinds, widths, received...  192 us
    pallas_call x1, Pallas kernels, last_gradients(): pl.pallas_call(functools.partial(last_kernel, widths, [[v.shape[2] for v...  100 us
    pallas_call x1, Pallas kernels, gather_rows(): pl.pallas_call(functools.partial(gather_kernel, kinds, n_fsdp, n_grp), ou...  72.4 us
    pallas_call x1, Pallas kernels, feed_forward(): pl.pallas_call(feed_forward_kernel, out_shape=[low(hidden, tok), low(tok,...  51.4 us
    pallas_call x6, Pallas kernels, weight_grad(): pl.pallas_call(functools.partial(weight_grad_kernel, count), out_shape=[j...  43.4 us
    ppermute x10, waiting for transfers between devices, swap(): lax.ppermute(value, axis, [(i, i ^ mask) for i in range(lax.axis_size(axi...  20.7 us
  transfers between devices with their start and end apart: 10, of which 5 were waited for; matrix products, arithmetic and copies ran while one was open for 1% of the time, Pallas kernels for 30%

profile of v3, /device:TPU:8, one launch (start us, length us, event | category | flops | bytes accessed | tf_op | source)
XLA Modules:
  0.0 724.4 jit_solution(9200772293303035485)
XLA Ops:
  2.0 1.4 select_bitcast_fusion
  4.6 72.4 %gather_rows.1 = (bf16[32,48,4608]{2,1,0:T(8,128)(2,1)}, bf16[32,48,128]{2,1,0:T(8,128)(2,1)}, bf16[4,48,1536]{2,1,0:T(8,128)(2,1)}, bf16[4,128,1536]{2,1,0:T(8,128)(2,1)}) custom-call(bf16[48,4608]{1,0:T(8,128)(2,1)} %refs_0_.1, bf16[48,128]{1,0:T(8,128)(2,1)} %pad.12.refs_1_, bf16[48,1536]{1,0:T(8,128)(2,1)} %refs_2_.1, bf16[128,1536]{1,0:T(8,128)(2,1)} %refs_3_.1), custom_call_target="tpu_custom_call" | custom-call | tf_op jit(solution)/shard_map/gather_rows/pallas_call | solution.py:285
  77.0 12.4 %convolution_convert_fusion.refs_4_ = bf16[384,4608]{1,0:T(8,128)(2,1)} fusion(bf16[1536,4608]{1,0:T(8,128)(2,1)} %bitcast.61, bf16[384,1536]{1,0:T(8,128)(2,1)S(1)} %copy-done.11, f32[1536]{0:T(1024)S(1)} %copy-done.19, f32[384]{0:T(512)S(1)} %add_rsqrt_fusion), kind=kOutput, calls=%fused_computation | convolution fusion | flops 5439946752 | bytes 18882048 | tf_op jit(solution)/shard_map/dot_general | solution.py:1558
  90.2 3.0 copy.54.refs_6_.refs_16_
  93.9 1.4 copy-done.1
  95.3 193.9 %forward_attention.1 = (bf16[32,48,1536]{2,1,0:T(8,128)(2,1)}, bf16[32,48,8192]{2,1,0:T(8,128)(2,1)}, bf16[32,128,1536]{2,1,0:T(8,128)(2,1)}, bf16[384,1536]{1,0...) custom-call(bf16[4,48,1536]{2,1,0:T(8,128)(2,1)S(1)} %copy-done.4, ...), custom_call_target="tpu_custom_call" | custom-call | tf_op jit(solution)/shard_map/forward_attention/pallas_call | solution.py:513
  290.1 1.0 copy-done.7
  291.1 51.4 %feed_forward.1 = (bf16[4096,384]{1,0:T(8,128)(2,1)}, bf16[384,4096]{1,0:T(8,128)(2,1)}, bf16[384,4096]{1,0:T(8,128)(2,1)}, bf16[1536,384]{1,0:T(8,128)(2,1)}, b...) custom-call(bf16[384,1536]{1,0:T(8,128)(2,1)} %copy-done.7, ...), custom_call_target="tpu_custom_call" | custom-call | flops 28991029248 | bytes 37748736 | tf_op jit(solution)/shard_map/feed_forward/pallas_call | solution.py:1370
  343.8 6.2 collective-permute-done.1.refs_9_
  350.2 1.7 copy-done.8
  351.9 7.3 %weight_grad.6 = (bf16[2,512,768]{2,1,0:T(8,128)(2,1)}, bf16[2,512,768]{2,1,0:T(8,128)(2,1)}) custom-call(s32[4]{0:T(128)} %get-tuple-element.160.ids, bf16[8,512,384]{2,1,0:T(8,128)(2,1)} %bitcast.44, bf16[8,512,384]{2,1,0:T(8,128)(2,1)} %bitcast.45, bf16[8,512,384]{2,1,0:T(8,128)(2,1)} %bitcast.46, bf16[8,512,384]{2,1,0:T(8,128)(2,1)} %bitcast.47, ...), custom_call_target="tpu_custom_call" | custom-call | flops 2415919104 | bytes 4325376 | tf_op jit(solution)/shard_map/weight_grad/pallas_call | solution.py:1454
  359.2 7.5 %weight_grad.7 = (bf16[2,512,768]{2,1,0:T(8,128)(2,1)}, bf16[2,512,768]{2,1,0:T(8,128)(2,1)}) custom-call(s32[4]{0:T(128)} %get-tuple-element.161.ids, bf16[8,512,384]{2,1,0:T(8,128)(2,1)} %bitcast.48, bf16[8,512,384]{2,1,0:T(8,128)(2,1)} %bitcast.49, bf16[8,512,384]{2,1,0:T(8,128)(2,1)} %bitcast.50, bf16[8,512,384]{2,1,0:T(8,128)(2,1)} %bitcast.51, ...), custom_call_target="tpu_custom_call" | custom-call | flops 2415919104 | bytes 4325376 | tf_op jit(solution)/shard_map/weight_grad/pallas_call | solution.py:1454
  369.3 6.5 collective-permute-done.7.refs_4_.refs_5_.refs_6_.refs_7_
  375.8 1.5 collective-permute-start.2
  377.3 3.3 collective-permute-done.8.refs_9_
  380.6 1.6 collective-permute-start.3
  382.5 1.6 copy.58
  384.2 4.5 weight_grad.10
  388.6 4.6 weight_grad.11
  393.4 9.7 %weight_grad.8 = (bf16[2,192,4096]{2,1,0:T(8,128)(2,1)}, bf16[2,192,4096]{2,1,0:T(8,128)(2,1)}) custom-call(s32[4]{0:T(128)} %get-tuple-element.160.ids, bf16[8,192,384]{2,1,0:T(8,128)(2,1)} %bitcast.86, bf16[8,192,384]{2,1,0:T(8,128)(2,1)} %bitcast.87, bf16[8,192,384]{2,1,0:T(8,128)(2,1)} %bitcast.88, bf16[8,192,384]{2,1,0:T(8,128)(2,1)} %bitcast.89, ...), custom_call_target="tpu_custom_call" | custom-call | flops 4831838208 | bytes 12582912 | tf_op jit(solution)/shard_map/weight_grad/pallas_call | solution.py:1454
  403.1 9.7 %weight_grad.9 = (bf16[2,192,4096]{2,1,0:T(8,128)(2,1)}, bf16[2,192,4096]{2,1,0:T(8,128)(2,1)}) custom-call(s32[4]{0:T(128)} %get-tuple-element.161.ids, bf16[8,192,384]{2,1,0:T(8,128)(2,1)} %bitcast.90, bf16[8,192,384]{2,1,0:T(8,128)(2,1)} %bitcast.91, bf16[8,192,384]{2,1,0:T(8,128)(2,1)} %bitcast.92, bf16[8,192,384]{2,1,0:T(8,128)(2,1)} %bitcast.93, ...), custom_call_target="tpu_custom_call" | custom-call | flops 4831838208 | bytes 12582912 | tf_op jit(solution)/shard_map/weight_grad/pallas_call | solution.py:1454
  412.8 4.5 collective-permute-done.3.refs_1_
  417.4 192.2 %backward_attention.1 = (bf16[4,128,768]{2,1,0:T(8,128)(2,1)}, bf16[4,128,768]{2,1,0:T(8,128)(2,1)}, f32[48,8192]{1,0:T(8,128)}, bf16[4,48,768]{2,1,0:T(8,128)(2...) custom-call(bf16[2,4,128,768]{3,2,1,0:T(8,128)(2,1)} %collective-permute-done.2.refs_0_, ...), custom_call_target="tpu_custom_call" | custom-call | tf_op jit(solution)/shard_map/backward_attention/pallas_call | solution.py:1237
  609.6 1.2 slice_bitcast_fusion
  612.7 100.1 %last_gradients.1 = (f32[48,4608]{1,0:T(8,128)}, f32[48,128]{1,0:T(8,128)}, bf16[384,1536]{1,0:T(8,128)(2,1)}, f32[1,1536]{1,0:T(1,128)}, f32[1,1536]{1,0:T(1,12...) custom-call(bf16[384,4608]{1,0:T(8,128)(2,1)} %get-tuple-element.103.refs_0_, ...), custom_call_target="tpu_custom_call" | custom-call | tf_op jit(solution)/shard_map/last_gradients/pallas_call | solution.py:1062
  712.7 1.4 reduce.1
  714.1 1.4 copy.60
  715.5 1.1 slice_bitcast_fusion.1
  716.7 1.3 reduce.2
  718.0 2.4 copy.67
  720.4 0.9 copy.68
  722.1 1.1 copy.70
  (91 shorter events, 12.8 us)
Async XLA Ops:
  2.0 1.6 copy-start.21
  2.0 1.7 copy-start.11
  3.4 73.6 %copy-start.19 = (f32[1536]{0:T(1024)S(1)}, f32[1536]{0:T(1024)}, u32[]{:S(2)}) copy-start(f32[1536]{0:T(1024)} %param.15) | copy-start | bytes 18436
  3.6 90.3 %copy-start = (bf16[3,384,384]{2,1,0:T(8,128)(2,1)}, bf16[3,384,384]{2,1,0:T(8,128)(2,1)S(1)}, u32[]{:S(2)}) copy-start(bf16[3,384,384]{2,1,0:T(8,128)(2,1)S(1)} %fusion.3.refs_7_.refs_17_) | copy-start | bytes 2654212
  77.0 12.4 %copy-start.17 = (bf16[32,48,128]{2,1,0:T(8,128)(2,1)S(1)}, bf16[32,48,128]{2,1,0:T(8,128)(2,1)}, u32[]{:S(2)}) copy-start(bf16[32,48,128]{2,1,0:T(8,128)(2,1)} %get-tuple-element.68) | copy-start | bytes 1179652
  77.0 12.4 %copy-start.23 = (f32[24]{0:T(128)S(1)}, f32[24]{0:T(128)}, u32[]{:S(2)}) copy-start(f32[24]{0:T(128)} %param.18) | copy-start | bytes 292
  90.2 3.0 copy-start.20
  90.2 3.6 copy-start.2
  90.2 3.6 copy-start.4
  90.2 3.6 copy-start.6
  93.9 1.4 copy-start.1
  291.1 51.4 %copy-start.5 = (f32[3,2,8,384]{3,2,1,0:T(8,128)}, f32[3,2,8,384]{3,2,1,0:T(8,128)S(1)}, u32[]{:S(2)}) copy-start(f32[3,2,8,384]{3,2,1,0:T(8,128)S(1)} %get-tuple-element.102.refs_18_) | copy-start | bytes 221188
  342.6 7.6 %collective-permute-start = (bf16[8,512,384]{2,1,0:T(8,128)(2,1)}, bf16[8,512,384]{2,1,0:T(8,128)(2,1)S(1)}, u32[]{:S(2)}, u32[]{:S(2)}) collective-permute-start(bf16[8,512,384]{2,1,0:T(8,128)(2,1)} %bitcast.43), channel_id=1, source_target_pairs={{0,4},{4,0},{8,12},{12,8},{16,20},{20,16},{24,28},{28,24},{1,5},{5... | collective-permute-start | bytes 9437192 | tf_op jit(solution)/shard_map/ppermute | solution.py:33
  342.6 7.3 %collective-permute-start.1 = (bf16[384,1536]{1,0:T(8,128)(2,1)}, bf16[384,1536]{1,0:T(8,128)(2,1)}, u32[]{:S(2)}, u32[]{:S(2)}) collective-permute-start(bf16[384,1536]{1,0:T(8,128)(2,1)} %refs_8_.3), channel_id=1, source_target_pairs={{0,4},{4,0},{8,12},{12,8},{16,20},{20,16},{24,28},{28,24},{1,5},{5... | collective-permute-start | bytes 3538952 | tf_op jit(solution)/shard_map/ppermute | solution.py:33
  350.2 1.7 copy-start.8
  359.2 8.1 %copy-start.9 = (bf16[1536,384]{1,0:T(8,128)(2,1)S(1)}, bf16[1536,384]{1,0:T(8,128)(2,1)}, u32[]{:S(2)}) copy-start(bf16[1536,384]{1,0:T(8,128)(2,1)} %get-tuple-element.89) | copy-start | bytes 3538948
  359.2 23.0 %copy-start.12 = (bf16[384,1536]{1,0:T(8,128)(2,1)S(1)}, bf16[384,1536]{1,0:T(8,128)(2,1)}, u32[]{:S(2)}) copy-start(bf16[384,1536]{1,0:T(8,128)(2,1)} %refs_6_.1) | copy-start | bytes 3538948
  366.7 26.6 %collective-permute-start.5 = (bf16[384,4096]{1,0:T(8,128)(2,1)}, bf16[384,4096]{1,0:T(8,128)(2,1)}, u32[]{:S(2)}, u32[]{:S(2)}) collective-permute-start(bf16[384,4096]{1,0:T(8,128)(2,1)} %get-tuple-element.85.refs_8_), channel_id=1, source_target_pairs={{0,4},{4,0},{8,12},{12,8},{16,20},{20,16},{24,28},{28,24},{1,5},{5... | collective-permute-start | bytes 9437192 | tf_op jit(solution)/shard_map/ppermute | solution.py:33
  366.9 36.2 %collective-permute-start.6 = (bf16[384,4096]{1,0:T(8,128)(2,1)}, bf16[384,4096]{1,0:T(8,128)(2,1)}, u32[]{:S(2)}, u32[]{:S(2)}) collective-permute-start(bf16[384,4096]{1,0:T(8,128)(2,1)} %get-tuple-element.87.refs_8_), channel_id=1, source_target_pairs={{0,4},{4,0},{8,12},{12,8},{16,20},{20,16},{24,28},{28,24},{1,5},{5... | collective-permute-start | bytes 9437192 | tf_op jit(solution)/shard_map/ppermute | solution.py:33
  367.2 8.5 %collective-permute-start.7 = (bf16[8,192,384]{2,1,0:T(8,128)(2,1)S(1)}, bf16[8,192,384]{2,1,0:T(8,128)(2,1)S(1)}, u32[]{:S(2)}, u32[]{:S(2)}) collective-permute-start(bf16[8,192,384]{2,1,0:T(8,128)(2,1)S(1)} %bitcast.60), channel_id=1, source_target_pairs={{0,4},{4,0},{8,12},{12,8},{16,20},{20,16},{24,28},{28,24},{1,5},{5... | collective-permute-start | bytes 3538952 | tf_op jit(solution)/shard_map/ppermute | solution.py:33
  367.4 13.2 %collective-permute-start.8 = (bf16[384,1536]{1,0:T(8,128)(2,1)}, bf16[384,1536]{1,0:T(8,128)(2,1)}, u32[]{:S(2)}, u32[]{:S(2)}) collective-permute-start(bf16[384,1536]{1,0:T(8,128)(2,1)} %get-tuple-element.90.refs_8_), channel_id=1, source_target_pairs={{0,4},{4,0},{8,12},{12,8},{16,20},{20,16},{24,28},{28,24},{1,5},{5... | collective-permute-start | bytes 3538952 | tf_op jit(solution)/shard_map/ppermute | solution.py:33
  367.8 25.5 %collective-permute-start.4 = (bf16[8,192,384]{2,1,0:T(8,128)(2,1)}, bf16[8,192,384]{2,1,0:T(8,128)(2,1)}, u32[]{:S(2)}, u32[]{:S(2)}) collective-permute-start(bf16[8,192,384]{2,1,0:T(8,128)(2,1)} %bitcast.85), channel_id=1, source_target_pairs={{0,4},{4,0},{8,12},{12,8},{16,20},{20,16},{24,28},{28,24},{1,5},{5... | collective-permute-start | bytes 3538952 | tf_op jit(solution)/shard_map/ppermute | solution.py:33
  375.8 8.4 %copy-start.10 = (bf16[8,192,384]{2,1,0:T(8,128)(2,1)}, bf16[8,192,384]{2,1,0:T(8,128)(2,1)S(1)}, u32[]{:S(2)}) copy-start(bf16[8,192,384]{2,1,0:T(8,128)(2,1)S(1)} %collective-permute-done.7.refs_4_.refs_5_.refs_6_.refs_7_) | copy-start | bytes 3538948
  375.8 37.1 %collective-permute-start.2 = (bf16[2,4,128,768]{3,2,1,0:T(8,128)(2,1)}, bf16[2,4,128,768]{3,2,1,0:T(8,128)(2,1)}, u32[]{:S(2)}, u32[]{:S(2)}) collective-permute-start(bf16[2,4,128,768]{3,2,1,0:T(8,128)(2,1)} %bitcast.83), channel_id=1, source_target_pairs={{0,16},{4,20},{8,24},{12,28},{16,0},{20,4},{24,8},{28,12},{1,17},{... | collective-permute-start | bytes 4718600 | tf_op jit(solution)/shard_map/ppermute | solution.py:33
  380.6 36.8 %collective-permute-start.3 = (bf16[2,4,128,768]{3,2,1,0:T(8,128)(2,1)}, bf16[2,4,128,768]{3,2,1,0:T(8,128)(2,1)}, u32[]{:S(2)}, u32[]{:S(2)}) collective-permute-start(bf16[2,4,128,768]{3,2,1,0:T(8,128)(2,1)} %bitcast.84), channel_id=1, source_target_pairs={{0,8},{4,12},{8,0},{12,4},{16,24},{20,28},{24,16},{28,20},{1,9},{5... | collective-permute-start | bytes 4718600 | tf_op jit(solution)/shard_map/ppermute | solution.py:33
  382.5 1.6 copy-start.22
  388.6 4.6 copy-start.13
  393.3 219.4 %collective-permute-start.9 = (bf16[8,192,384]{2,1,0:T(8,128)(2,1)S(1)}, bf16[8,192,384]{2,1,0:T(8,128)(2,1)}, u32[]{:S(2)}, u32[]{:S(2)}) collective-permute-start(bf16[8,192,384]{2,1,0:T(8,128)(2,1)S(1)} %bitcast.64), channel_id=1, source_target_pairs={{0,4},{4,0},{8,12},{12,8},{16,20},{20,16},{24,28},{28,24},{1,5},{5... | collective-permute-start | bytes 3538952 | tf_op jit(solution)/shard_map/ppermute | solution.py:33
  712.7 7.7 %copy-start.15 = (f32[48,4608]{1,0:T(8,128)S(1)}, f32[48,4608]{1,0:T(8,128)}, u32[]{:S(2)}) copy-start(f32[48,4608]{1,0:T(8,128)} %get-tuple-element.175) | copy-start | bytes 2654212
  718.0 3.3 copy-start.18
  720.4 1.7 copy-start.14
  721.3 2.0 copy-start.16
  (2 other events, 1.9 us)

commit v4 on v3

--- a/solution.py
+++ b/solution.py
@@ -1267,6 +1267,33 @@
     return out[:-2], out[-2], out[-1]
 
 
+def project_kernel(act_ref, w_ref, out_ref):
+    out_ref[...] = jnp.dot(act_ref[...], w_ref[...], preferred_element_type=F32).astype(BF16)
+
+
+def project(act, w):
+    tok, width = act.shape
+    columns = w.shape[1]
+    tile = next(t for t in (768, 512, 384, 256, 128) if columns % t == 0)
+    return pl.pallas_call(
+        project_kernel,
+        out_shape=jax.ShapeDtypeStruct((tok, columns), BF16),
+        grid=(columns // tile,),
+        in_specs=[
+            pl.BlockSpec((tok, width), lambda j: (0, 0), pipeline_mode=pl.Buffered(1)),
+            pl.BlockSpec((width, tile), lambda j: (0, j)),
+        ],
+        out_specs=pl.BlockSpec((tok, tile), lambda j: (0, j)),
+        compiler_params=pltpu.CompilerParams(vmem_limit_bytes=60 << 20),
+        cost_estimate=pl.CostEstimate(
+            flops=2 * tok * width * columns,
+            bytes_accessed=2 * (width + tok) * columns,
+            transcendentals=0,
+        ),
+        name="project",
+    )(act, w)
+
+
 def feed_forward_kernel(
     o_ref,
     tokens_ref,
@@ -1304,11 +1331,11 @@
 
     @pl.when(pl.program_id(0) == 0)
     def _():
+        resid_ref[...] = jnp.dot(o_ref[...], w_out_ref[...], preferred_element_type=F32)
+
         def begin(i, carry):
             rows = rows_of(i)
-            resid_ref[rows, :] = tokens_ref[rows, :].astype(F32) + jnp.dot(
-                o_ref[rows, :], w_out_ref[...], preferred_element_type=F32
-            )
+            resid_ref[rows, :] = tokens_ref[rows, :].astype(F32) + resid_ref[rows, :]
             _, normed, _ = norm(rows)
             act_ref[rows, :] = (normed * gain_ref[...]).astype(BF16)
             return carry
@@ -1348,12 +1375,11 @@
             average = jnp.mean(scaled * normed, axis=1, keepdims=True)
             dresid = grad_ref[rows, :].astype(F32) + scale * (scaled - normed * average)
             dresid_ref[rows, :] = dresid
-            dbranch = dresid.astype(BF16)
-            dbranch_ref[rows, :] = dbranch
-            do_ref[rows, :] = dot_lanes(dbranch, w_out_ref[...]).astype(BF16)
+            dbranch_ref[rows, :] = dresid.astype(BF16)
             return carry
 
         lax.fori_loop(0, tok // block, end, 0)
+        do_ref[...] = dot_lanes(dbranch_ref[...], w_out_ref[...]).astype(BF16)
 
 
 def feed_forward(attn_o, tokens, grad, gain, w_out, gate_up, down):
@@ -1555,7 +1581,8 @@
     acts_rows = both_cores(acts.T)
     logits = jnp.dot(acts, forget_full, preferred_element_type=F32)[:, :heads] + b_forget
     log_keep = jax.nn.log_sigmoid(logits)
-    mixed = jnp.dot(acts, qkv_full, preferred_element_type=F32).astype(BF16)
+    mixed = project(acts, qkv_full)
+    mixed, grad_out_other = lax.optimization_barrier((mixed, grad_out_other))
 
     logs = jnp.pad(
         log_keep.T.reshape(blocks, own_heads, tok), ((0, 0), (0, 8 - own_heads), (0, 0))
@@ -1578,9 +1605,11 @@
         gain_two_grad,
     ) = feed_forward(attn_o, tokens, grad_out, gain_ffn[None], out_full, gate_up_full, down_full)
     down_rows = both_cores(inner_turned)
-    acts_two_rows = both_cores(acts_two_turned)
-    attn_rows = both_cores(attn_turned)
-    grad_branch_other = swap(grad_branch, "fsdp", 1)
+    down_rows, *later = lax.optimization_barrier(
+        (down_rows, grad_gate, grad_up, grad_branch, acts_two_turned, attn_turned)
+    )
+    grad_gate_other, grad_up_other, grad_branch_other = (swap(v, "fsdp", 1) for v in later[:3])
+    acts_two_rows, attn_rows = both_cores(later[3]), both_cores(later[4])
     part_down = partial_rows(
         down_rows, [(grad_out, grad_out_other, 0, half), (grad_out, grad_out_other, half, half)]
     )
@@ -1594,7 +1623,7 @@
     ]
     part_gate_up = partial_rows(
         acts_two_rows,
-        [(v, swap(v, "fsdp", 1), 0, hidden) for v in (grad_gate, grad_up)],
+        [(grad_gate, grad_gate_other, 0, hidden), (grad_up, grad_up_other, 0, hidden)],
     )
     part_out = partial_rows(
         attn_rows,

time: 731 us -> 719 us (0.984)
  matrix products: 12.9 us -> 1.47 us
  Pallas kernels: 653 us -> 664 us
  waiting for transfers between devices: 20.7 us -> 12.4 us
    dot_general x1 -> x0, matrix products: 12.4 us -> none  [on_device(): mixed = jnp.dot(acts, qkv_full, preferred_element_type=F32).astype(BF16)]
    pallas_call x0 -> x1, Pallas kernels: none -> 11.7 us  [project(): pl.pallas_call(project_kernel, out_shape=jax.ShapeDtypeStruct((tok, colum...]
    ppermute x10, waiting for transfers between devices: 20.7 us -> 12.4 us  [swap(): lax.ppermute(value, axis, [(i, i ^ mask) for i in range(lax.axis_size(axi...]
  transfers between devices with their start and end apart: 10 -> 10, of which waited for: 5 -> 3; matrix products, arithmetic and copies ran while one was open for 1% -> 2% of each run, Pallas kernels for 30% -> 45%
where the time goes in v4:
time: 719 us; the launch traced here: 713 us
  Pallas kernels  664 us (92%)
  local copies, waits for them, and re-layouts  22.2 us (3%)
  waiting for transfers between devices  12.4 us (2%)
  other arithmetic  8.25 us (1%)
    pallas_call x1, Pallas kernels, forward_attention(): pl.pallas_call(functools.partial(forward_kernel, kinds, pairs, head_size,...  195 us
    pallas_call x1, Pallas kernels, backward_attention(): pl.pallas_call(functools.partial(backward_kernel, kinds, widths, received...  192 us
    pallas_call x1, Pallas kernels, last_gradients(): pl.pallas_call(functools.partial(last_kernel, widths, [[v.shape[2] for v...  99.1 us
    pallas_call x1, Pallas kernels, gather_rows(): pl.pallas_call(functools.partial(gather_kernel, kinds, n_fsdp, n_grp), ou...  73.1 us
    pallas_call x1, Pallas kernels, feed_forward(): pl.pallas_call(feed_forward_kernel, out_shape=[low(hidden, tok), low(tok,...  49.6 us
    pallas_call x6, Pallas kernels, weight_grad(): pl.pallas_call(functools.partial(weight_grad_kernel, count), out_shape=[j...  43.1 us
  transfers between devices with their start and end apart: 10, of which 3 were waited for; matrix products, arithmetic and copies ran while one was open for 2% of the time, Pallas kernels for 45%

profile of v4, /device:TPU:8, one launch (start us, length us, event | category | flops | bytes accessed | tf_op | source)
XLA Modules:
  0.0 712.6 jit_solution(13553608625435138178)
XLA Ops:
  1.6 1.6 fusion
  3.8 1.0 fusion.2.act_ref
  4.9 73.1 %gather_rows.1 = (bf16[32,48,4608]{2,1,0:T(8,128)(2,1)}, bf16[32,48,128]{2,1,0:T(8,128)(2,1)}, bf16[4,48,1536]{2,1,0:T(8,128)(2,1)}, bf16[4,128,1536]{2,1,0:T(8,128)(2,1)}) custom-call(bf16[48,4608]{1,0:T(8,128)(2,1)} %refs_0_.1, bf16[48,128]{1,0:T(8,128)(2,1)} %pad.12.refs_1_, bf16[48,1536]{1,0:T(8,128)(2,1)} %refs_2_.1, bf16[128,1536]{1,0:T(8,128)(2,1)} %refs_3_.1), custom_call_target="tpu_custom_call" | custom-call | tf_op jit(solution)/shard_map/gather_rows/pallas_call | solution.py:285
  78.0 1.5 convolution_add_fusion
  80.6 1.9 copy.54.refs_6_.refs_16_
  83.2 11.7 %project.1.refs_4_ = bf16[384,4608]{1,0:T(8,128)(2,1)} custom-call(bf16[384,1536]{1,0:T(8,128)(2,1)} %copy-done.11, bf16[1536,4608]{1,0:T(8,128)(2,1)} %bitcast.61), custom_call_target="tpu_custom_call" | custom-call | flops 5435817984 | bytes 17694720 | tf_op jit(solution)/shard_map/project/pallas_call | solution.py:1278
  94.9 1.1 copy-done.4
  96.0 195.3 %forward_attention.1 = (bf16[32,48,1536]{2,1,0:T(8,128)(2,1)}, bf16[32,48,8192]{2,1,0:T(8,128)(2,1)}, bf16[32,128,1536]{2,1,0:T(8,128)(2,1)}, bf16[384,1536]{1,0...) custom-call(bf16[4,48,1536]{2,1,0:T(8,128)(2,1)S(1)} %copy-done.4, ...), custom_call_target="tpu_custom_call" | custom-call | tf_op jit(solution)/shard_map/forward_attention/pallas_call | solution.py:513
  292.8 1.0 copy-done.7
  293.8 49.6 %feed_forward.1 = (bf16[4096,384]{1,0:T(8,128)(2,1)}, bf16[384,4096]{1,0:T(8,128)(2,1)}, bf16[384,4096]{1,0:T(8,128)(2,1)}, bf16[1536,384]{1,0:T(8,128)(2,1)}, b...) custom-call(bf16[384,1536]{1,0:T(8,128)(2,1)} %copy-done.7, ...), custom_call_target="tpu_custom_call" | custom-call | flops 28991029248 | bytes 37748736 | tf_op jit(solution)/shard_map/feed_forward/pallas_call | solution.py:1396
  343.5 5.9 collective-permute-done.1.refs_4_.refs_5_.refs_6_.refs_7_
  353.2 7.3 %weight_grad.6 = (bf16[2,512,768]{2,1,0:T(8,128)(2,1)}, bf16[2,512,768]{2,1,0:T(8,128)(2,1)}) custom-call(s32[4]{0:T(128)} %fusion.7.ids, bf16[8,512,384]{2,1,0:T(8,128)(2,1)} %bitcast.44, bf16[8,512,384]{2,1,0:T(8,128)(2,1)} %bitcast.45, bf16[8,512,384]{2,1,0:T(8,128)(2,1)} %bitcast.46, bf16[8,512,384]{2,1,0:T(8,128)(2,1)} %bitcast.47, ...), custom_call_target="tpu_custom_call" | custom-call | flops 2415919104 | bytes 4325376 | tf_op jit(solution)/shard_map/weight_grad/pallas_call | solution.py:1480
  360.5 7.6 %weight_grad.7 = (bf16[2,512,768]{2,1,0:T(8,128)(2,1)}, bf16[2,512,768]{2,1,0:T(8,128)(2,1)}) custom-call(s32[4]{0:T(128)} %fusion.8.ids, bf16[8,512,384]{2,1,0:T(8,128)(2,1)} %bitcast.48, bf16[8,512,384]{2,1,0:T(8,128)(2,1)} %bitcast.49, bf16[8,512,384]{2,1,0:T(8,128)(2,1)} %bitcast.50, bf16[8,512,384]{2,1,0:T(8,128)(2,1)} %bitcast.51, ...), custom_call_target="tpu_custom_call" | custom-call | flops 2415919104 | bytes 4325376 | tf_op jit(solution)/shard_map/weight_grad/pallas_call | solution.py:1480
  368.1 1.6 collective-permute-start.2
  370.5 0.9 copy.58
  371.6 4.4 weight_grad.10
  375.9 4.4 weight_grad.11
  380.5 9.7 %weight_grad.8 = (bf16[2,192,4096]{2,1,0:T(8,128)(2,1)}, bf16[2,192,4096]{2,1,0:T(8,128)(2,1)}) custom-call(s32[4]{0:T(128)} %fusion.7.ids, bf16[8,192,384]{2,1,0:T(8,128)(2,1)} %bitcast.85, bf16[8,192,384]{2,1,0:T(8,128)(2,1)} %bitcast.86, bf16[8,192,384]{2,1,0:T(8,128)(2,1)} %bitcast.87, bf16[8,192,384]{2,1,0:T(8,128)(2,1)} %bitcast.88, ...), custom_call_target="tpu_custom_call" | custom-call | flops 4831838208 | bytes 12582912 | tf_op jit(solution)/shard_map/weight_grad/pallas_call | solution.py:1480
  390.2 9.7 %weight_grad.9 = (bf16[2,192,4096]{2,1,0:T(8,128)(2,1)}, bf16[2,192,4096]{2,1,0:T(8,128)(2,1)}) custom-call(s32[4]{0:T(128)} %fusion.8.ids, bf16[8,192,384]{2,1,0:T(8,128)(2,1)} %bitcast.89, bf16[8,192,384]{2,1,0:T(8,128)(2,1)} %bitcast.90, bf16[8,192,384]{2,1,0:T(8,128)(2,1)} %bitcast.91, bf16[8,192,384]{2,1,0:T(8,128)(2,1)} %bitcast.92, ...), custom_call_target="tpu_custom_call" | custom-call | flops 4831838208 | bytes 12582912 | tf_op jit(solution)/shard_map/weight_grad/pallas_call | solution.py:1480
  399.8 5.3 collective-permute-done.2.refs_0_
  405.1 1.3 collective-permute-done.3.refs_1_
  406.4 191.9 %backward_attention.1 = (bf16[4,128,768]{2,1,0:T(8,128)(2,1)}, bf16[4,128,768]{2,1,0:T(8,128)(2,1)}, f32[48,8192]{1,0:T(8,128)}, bf16[4,48,768]{2,1,0:T(8,128)(2...) custom-call(bf16[2,4,128,768]{3,2,1,0:T(8,128)(2,1)} %collective-permute-done.2.refs_0_, ...), custom_call_target="tpu_custom_call" | custom-call | tf_op jit(solution)/shard_map/backward_attention/pallas_call | solution.py:1237
  598.3 1.2 slice_bitcast_fusion
  601.3 99.1 %last_gradients.1 = (f32[48,4608]{1,0:T(8,128)}, f32[48,128]{1,0:T(8,128)}, bf16[384,1536]{1,0:T(8,128)(2,1)}, f32[1,1536]{1,0:T(1,128)}, f32[1,1536]{1,0:T(1,12...) custom-call(bf16[384,4608]{1,0:T(8,128)(2,1)} %get-tuple-element.121.refs_0_, ...), custom_call_target="tpu_custom_call" | custom-call | tf_op jit(solution)/shard_map/last_gradients/pallas_call | solution.py:1062
  700.4 1.4 reduce.1
  701.8 1.4 copy.60
  703.2 1.2 slice_bitcast_fusion.1
  704.4 1.3 reduce.2
  705.7 2.4 copy.67
  708.1 0.9 copy.68
  709.8 1.1 copy.70
  711.5 0.9 copy.71
  (89 shorter events, 13.0 us)
Async XLA Ops:
  0.6 3.2 copy-start.9
  0.7 94.3 %collective-permute-start = (bf16[384,1536]{1,0:T(8,128)(2,1)}, bf16[384,1536]{1,0:T(8,128)(2,1)}, u32[]{:S(2)}, u32[]{:S(2)}) collective-permute-start(bf16[384,1536]{1,0:T(8,128)(2,1)} %refs_8_.3), channel_id=1, source_target_pairs={{0,4},{4,0},{8,12},{12,8},{16,20},{20,16},{24,28},{28,24},{1,5},{5... | collective-permute-start | bytes 3538952 | tf_op jit(solution)/shard_map/ppermute | solution.py:33
  3.8 74.1 %copy-start.21 = (f32[24]{0:T(128)S(1)}, f32[24]{0:T(128)}, u32[]{:S(2)}) copy-start(f32[24]{0:T(128)} %param.18) | copy-start | bytes 292
  4.9 74.7 %copy-start.11 = (bf16[384,1536]{1,0:T(8,128)(2,1)}, bf16[384,1536]{1,0:T(8,128)(2,1)S(1)}, u32[]{:S(2)}) copy-start(bf16[384,1536]{1,0:T(8,128)(2,1)S(1)} %fusion.2.act_ref) | copy-start | bytes 3538948
  4.9 74.7 %copy-start.20 = (s32[1,2,4]{2,1,0:T(2,128)S(1)}, s32[1,2,4]{2,1,0:T(2,128)}, u32[]{:S(2)}) copy-start(s32[1,2,4]{2,1,0:T(2,128)} %param.14) | copy-start | bytes 100
  80.5 1.9 copy-start.18
  83.2 11.7 %copy-start = (bf16[3,384,384]{2,1,0:T(8,128)(2,1)}, bf16[3,384,384]{2,1,0:T(8,128)(2,1)S(1)}, u32[]{:S(2)}) copy-start(bf16[3,384,384]{2,1,0:T(8,128)(2,1)S(1)} %fusion.3.refs_7_.refs_17_) | copy-start | bytes 2654212
  83.2 11.7 %copy-start.1 = (bf16[4,128,1536]{2,1,0:T(8,128)(2,1)S(1)}, bf16[4,128,1536]{2,1,0:T(8,128)(2,1)}, u32[]{:S(2)}) copy-start(bf16[4,128,1536]{2,1,0:T(8,128)(2,1)} %get-tuple-element.75.refs_2_) | copy-start | bytes 4718596
  83.2 11.7 %copy-start.2 = (bf16[48,8192]{1,0:T(8,128)(2,1)S(1)}, bf16[48,8192]{1,0:T(8,128)(2,1)}, u32[]{:S(2)}) copy-start(bf16[48,8192]{1,0:T(8,128)(2,1)} %refs_1_.1) | copy-start | bytes 2359300
  83.2 11.7 %copy-start.6 = (s32[1,4]{1,0:T(1,128)S(1)}, s32[1,4]{1,0:T(1,128)}, u32[]{:S(2)}) copy-start(s32[1,4]{1,0:T(1,128)} %param.13) | copy-start | bytes 52
  94.9 1.1 copy-start.4
  291.3 0.9 copy-start.3
  292.2 0.6 copy-start.5
  292.8 1.0 copy-start.7
  293.8 58.8 %copy-start.17 = (f32[1536]{0:T(1024)S(1)}, f32[1536]{0:T(1024)}, u32[]{:S(2)}) copy-start(f32[1536]{0:T(1024)} %param.15) | copy-start | bytes 18436
  343.4 5.9 collective-permute-start.1
  349.3 3.9 copy-start.8
  349.3 31.1 %collective-permute-start.5 = (bf16[384,4096]{1,0:T(8,128)(2,1)}, bf16[384,4096]{1,0:T(8,128)(2,1)}, u32[]{:S(2)}, u32[]{:S(2)}) collective-permute-start(bf16[384,4096]{1,0:T(8,128)(2,1)} %get-tuple-element.101.refs_8_), channel_id=1, source_target_pairs={{0,4},{4,0},{8,12},{12,8},{16,20},{20,16},{24,28},{28,24},{1,5},{5... | collective-permute-start | bytes 9437192 | tf_op jit(solution)/shard_map/ppermute | solution.py:33
  349.5 40.7 %collective-permute-start.6 = (bf16[384,4096]{1,0:T(8,128)(2,1)}, bf16[384,4096]{1,0:T(8,128)(2,1)}, u32[]{:S(2)}, u32[]{:S(2)}) collective-permute-start(bf16[384,4096]{1,0:T(8,128)(2,1)} %get-tuple-element.104.refs_8_), channel_id=1, source_target_pairs={{0,4},{4,0},{8,12},{12,8},{16,20},{20,16},{24,28},{28,24},{1,5},{5... | collective-permute-start | bytes 9437192 | tf_op jit(solution)/shard_map/ppermute | solution.py:33
  349.8 18.3 %collective-permute-start.7 = (bf16[8,192,384]{2,1,0:T(8,128)(2,1)}, bf16[8,192,384]{2,1,0:T(8,128)(2,1)}, u32[]{:S(2)}, u32[]{:S(2)}) collective-permute-start(bf16[8,192,384]{2,1,0:T(8,128)(2,1)} %bitcast.52), channel_id=1, source_target_pairs={{0,4},{4,0},{8,12},{12,8},{16,20},{20,16},{24,28},{28,24},{1,5},{5... | collective-permute-start | bytes 3538952 | tf_op jit(solution)/shard_map/ppermute | solution.py:33
  350.0 19.7 %collective-permute-start.8 = (bf16[384,1536]{1,0:T(8,128)(2,1)}, bf16[384,1536]{1,0:T(8,128)(2,1)}, u32[]{:S(2)}, u32[]{:S(2)}) collective-permute-start(bf16[384,1536]{1,0:T(8,128)(2,1)} %get-tuple-element.108.refs_8_), channel_id=1, source_target_pairs={{0,4},{4,0},{8,12},{12,8},{16,20},{20,16},{24,28},{28,24},{1,5},{5... | collective-permute-start | bytes 3538952 | tf_op jit(solution)/shard_map/ppermute | solution.py:33
  351.0 29.4 %collective-permute-start.4 = (bf16[8,192,384]{2,1,0:T(8,128)(2,1)}, bf16[8,192,384]{2,1,0:T(8,128)(2,1)}, u32[]{:S(2)}, u32[]{:S(2)}) collective-permute-start(bf16[8,192,384]{2,1,0:T(8,128)(2,1)} %bitcast.84), channel_id=1, source_target_pairs={{0,4},{4,0},{8,12},{12,8},{16,20},{20,16},{24,28},{28,24},{1,5},{5... | collective-permute-start | bytes 3538952 | tf_op jit(solution)/shard_map/ppermute | solution.py:33
  360.5 9.7 %copy-start.10 = (bf16[384,1536]{1,0:T(8,128)(2,1)S(1)}, bf16[384,1536]{1,0:T(8,128)(2,1)}, u32[]{:S(2)}) copy-start(bf16[384,1536]{1,0:T(8,128)(2,1)} %refs_6_.1) | copy-start | bytes 3538948
  368.1 37.0 %collective-permute-start.2 = (bf16[2,4,128,768]{3,2,1,0:T(8,128)(2,1)}, bf16[2,4,128,768]{3,2,1,0:T(8,128)(2,1)}, u32[]{:S(2)}, u32[]{:S(2)}) collective-permute-start(bf16[2,4,128,768]{3,2,1,0:T(8,128)(2,1)} %bitcast.14), channel_id=1, source_target_pairs={{0,16},{4,20},{8,24},{12,28},{16,0},{20,4},{24,8},{28,12},{1,17},{... | collective-permute-start | bytes 4718600 | tf_op jit(solution)/shard_map/ppermute | solution.py:33
  369.7 36.7 %collective-permute-start.3 = (bf16[2,4,128,768]{3,2,1,0:T(8,128)(2,1)}, bf16[2,4,128,768]{3,2,1,0:T(8,128)(2,1)}, u32[]{:S(2)}, u32[]{:S(2)}) collective-permute-start(bf16[2,4,128,768]{3,2,1,0:T(8,128)(2,1)} %bitcast.83), channel_id=1, source_target_pairs={{0,8},{4,12},{8,0},{12,4},{16,24},{20,28},{24,16},{28,20},{1,9},{5... | collective-permute-start | bytes 4718600 | tf_op jit(solution)/shard_map/ppermute | solution.py:33
  370.5 1.0 copy-start.19
  371.5 8.9 %copy-start.12 = (bf16[1536,384]{1,0:T(8,128)(2,1)}, bf16[1536,384]{1,0:T(8,128)(2,1)S(1)}, u32[]{:S(2)}) copy-start(bf16[1536,384]{1,0:T(8,128)(2,1)S(1)} %copy.58) | copy-start | bytes 3538948
  380.4 221.0 %collective-permute-start.9 = (bf16[8,192,384]{2,1,0:T(8,128)(2,1)S(1)}, bf16[8,192,384]{2,1,0:T(8,128)(2,1)}, u32[]{:S(2)}, u32[]{:S(2)}) collective-permute-start(bf16[8,192,384]{2,1,0:T(8,128)(2,1)S(1)} %bitcast.63), channel_id=1, source_target_pairs={{0,4},{4,0},{8,12},{12,8},{16,20},{20,16},{24,28},{28,24},{1,5},{5... | collective-permute-start | bytes 3538952 | tf_op jit(solution)/shard_map/ppermute | solution.py:33
  700.4 7.7 %copy-start.14 = (f32[48,4608]{1,0:T(8,128)S(1)}, f32[48,4608]{1,0:T(8,128)}, u32[]{:S(2)}) copy-start(f32[48,4608]{1,0:T(8,128)} %get-tuple-element.191) | copy-start | bytes 2654212
  705.7 3.3 copy-start.16
  708.1 1.7 copy-start.13
  709.8 1.7 copy-start.15

commit v5 on v4

--- a/solution.py
+++ b/solution.py
@@ -10,7 +10,7 @@
 
 EPSILON = 1e-05
 NEG = -1e30
-AHEAD = 6
+AHEAD = 10
 MESH = pl.DeviceIdType.MESH
 F32 = jnp.float32
 BF16 = jnp.bfloat16

time: 719 us -> 703 us (0.978)
  Pallas kernels: 664 us -> 648 us
    pallas_call x1, Pallas kernels: 192 us -> 177 us  [backward_attention(): pl.pallas_call(functools.partial(backward_kernel, kinds, widths, received...]
  transfers between devices with their start and end apart: 10 -> 10, of which waited for: 3 -> 3; matrix products, arithmetic and copies ran while one was open for 2% -> 2% of each run, Pallas kernels for 45% -> 44%
where the time goes in v5:
time: 703 us; the launch traced here: 697 us
  Pallas kernels  648 us (92%)
  local copies, waits for them, and re-layouts  22.2 us (3%)
  waiting for transfers between devices  12.4 us (2%)
  other arithmetic  8.25 us (1%)
    pallas_call x1, Pallas kernels, forward_attention(): pl.pallas_call(functools.partial(forward_kernel, kinds, pairs, head_size,...  195 us
    pallas_call x1, Pallas kernels, backward_attention(): pl.pallas_call(functools.partial(backward_kernel, kinds, widths, received...  177 us
    pallas_call x1, Pallas kernels, last_gradients(): pl.pallas_call(functools.partial(last_kernel, widths, [[v.shape[2] for v...  98.6 us
    pallas_call x1, Pallas kernels, gather_rows(): pl.pallas_call(functools.partial(gather_kernel, kinds, n_fsdp, n_grp), ou...  73.1 us
    pallas_call x1, Pallas kernels, feed_forward(): pl.pallas_call(feed_forward_kernel, out_shape=[low(hidden, tok), low(tok,...  49.6 us
    pallas_call x6, Pallas kernels, weight_grad(): pl.pallas_call(functools.partial(weight_grad_kernel, count), out_shape=[j...  43.1 us
  transfers between devices with their start and end apart: 10, of which 3 were waited for; matrix products, arithmetic and copies ran while one was open for 2% of the time, Pallas kernels for 44%

profile of v5, /device:TPU:8, one launch (start us, length us, event | category | flops | bytes accessed | tf_op | source)
XLA Modules:
  0.0 696.9 jit_solution(3514647381129772324)
XLA Ops:
  1.6 1.6 fusion
  3.8 1.0 fusion.2.act_ref
  4.9 73.1 %gather_rows.1 = (bf16[32,48,4608]{2,1,0:T(8,128)(2,1)}, bf16[32,48,128]{2,1,0:T(8,128)(2,1)}, bf16[4,48,1536]{2,1,0:T(8,128)(2,1)}, bf16[4,128,1536]{2,1,0:T(8,128)(2,1)}) custom-call(bf16[48,4608]{1,0:T(8,128)(2,1)} %refs_0_.1, bf16[48,128]{1,0:T(8,128)(2,1)} %pad.12.refs_1_, bf16[48,1536]{1,0:T(8,128)(2,1)} %refs_2_.1, bf16[128,1536]{1,0:T(8,128)(2,1)} %refs_3_.1), custom_call_target="tpu_custom_call" | custom-call | tf_op jit(solution)/shard_map/gather_rows/pallas_call | solution.py:285
  78.0 1.5 convolution_add_fusion
  80.6 1.9 copy.54.refs_6_.refs_16_
  83.2 11.7 %project.1.refs_4_ = bf16[384,4608]{1,0:T(8,128)(2,1)} custom-call(bf16[384,1536]{1,0:T(8,128)(2,1)} %copy-done.11, bf16[1536,4608]{1,0:T(8,128)(2,1)} %bitcast.61), custom_call_target="tpu_custom_call" | custom-call | flops 5435817984 | bytes 17694720 | tf_op jit(solution)/shard_map/project/pallas_call | solution.py:1278
  94.9 1.1 copy-done.4
  96.0 195.3 %forward_attention.1 = (bf16[32,48,1536]{2,1,0:T(8,128)(2,1)}, bf16[32,48,8192]{2,1,0:T(8,128)(2,1)}, bf16[32,128,1536]{2,1,0:T(8,128)(2,1)}, bf16[384,1536]{1,0...) custom-call(bf16[4,48,1536]{2,1,0:T(8,128)(2,1)S(1)} %copy-done.4, ...), custom_call_target="tpu_custom_call" | custom-call | tf_op jit(solution)/shard_map/forward_attention/pallas_call | solution.py:513
  292.8 1.0 copy-done.7
  293.8 49.6 %feed_forward.1 = (bf16[4096,384]{1,0:T(8,128)(2,1)}, bf16[384,4096]{1,0:T(8,128)(2,1)}, bf16[384,4096]{1,0:T(8,128)(2,1)}, bf16[1536,384]{1,0:T(8,128)(2,1)}, b...) custom-call(bf16[384,1536]{1,0:T(8,128)(2,1)} %copy-done.7, ...), custom_call_target="tpu_custom_call" | custom-call | flops 28991029248 | bytes 37748736 | tf_op jit(solution)/shard_map/feed_forward/pallas_call | solution.py:1396
  343.5 5.9 collective-permute-done.1.refs_4_.refs_5_.refs_6_.refs_7_
  353.2 7.3 %weight_grad.6 = (bf16[2,512,768]{2,1,0:T(8,128)(2,1)}, bf16[2,512,768]{2,1,0:T(8,128)(2,1)}) custom-call(s32[4]{0:T(128)} %fusion.7.ids, bf16[8,512,384]{2,1,0:T(8,128)(2,1)} %bitcast.44, bf16[8,512,384]{2,1,0:T(8,128)(2,1)} %bitcast.45, bf16[8,512,384]{2,1,0:T(8,128)(2,1)} %bitcast.46, bf16[8,512,384]{2,1,0:T(8,128)(2,1)} %bitcast.47, ...), custom_call_target="tpu_custom_call" | custom-call | flops 2415919104 | bytes 4325376 | tf_op jit(solution)/shard_map/weight_grad/pallas_call | solution.py:1480
  360.5 7.6 %weight_grad.7 = (bf16[2,512,768]{2,1,0:T(8,128)(2,1)}, bf16[2,512,768]{2,1,0:T(8,128)(2,1)}) custom-call(s32[4]{0:T(128)} %fusion.8.ids, bf16[8,512,384]{2,1,0:T(8,128)(2,1)} %bitcast.48, bf16[8,512,384]{2,1,0:T(8,128)(2,1)} %bitcast.49, bf16[8,512,384]{2,1,0:T(8,128)(2,1)} %bitcast.50, bf16[8,512,384]{2,1,0:T(8,128)(2,1)} %bitcast.51, ...), custom_call_target="tpu_custom_call" | custom-call | flops 2415919104 | bytes 4325376 | tf_op jit(solution)/shard_map/weight_grad/pallas_call | solution.py:1480
  368.1 1.6 collective-permute-start.2
  370.5 0.9 copy.58
  371.6 4.4 weight_grad.10
  375.9 4.4 weight_grad.11
  380.5 9.7 %weight_grad.8 = (bf16[2,192,4096]{2,1,0:T(8,128)(2,1)}, bf16[2,192,4096]{2,1,0:T(8,128)(2,1)}) custom-call(s32[4]{0:T(128)} %fusion.7.ids, bf16[8,192,384]{2,1,0:T(8,128)(2,1)} %bitcast.85, bf16[8,192,384]{2,1,0:T(8,128)(2,1)} %bitcast.86, bf16[8,192,384]{2,1,0:T(8,128)(2,1)} %bitcast.87, bf16[8,192,384]{2,1,0:T(8,128)(2,1)} %bitcast.88, ...), custom_call_target="tpu_custom_call" | custom-call | flops 4831838208 | bytes 12582912 | tf_op jit(solution)/shard_map/weight_grad/pallas_call | solution.py:1480
  390.2 9.7 %weight_grad.9 = (bf16[2,192,4096]{2,1,0:T(8,128)(2,1)}, bf16[2,192,4096]{2,1,0:T(8,128)(2,1)}) custom-call(s32[4]{0:T(128)} %fusion.8.ids, bf16[8,192,384]{2,1,0:T(8,128)(2,1)} %bitcast.89, bf16[8,192,384]{2,1,0:T(8,128)(2,1)} %bitcast.90, bf16[8,192,384]{2,1,0:T(8,128)(2,1)} %bitcast.91, bf16[8,192,384]{2,1,0:T(8,128)(2,1)} %bitcast.92, ...), custom_call_target="tpu_custom_call" | custom-call | flops 4831838208 | bytes 12582912 | tf_op jit(solution)/shard_map/weight_grad/pallas_call | solution.py:1480
  399.8 5.3 collective-permute-done.2.refs_0_
  405.1 1.3 collective-permute-done.3.refs_1_
  406.4 176.6 %backward_attention.1 = (bf16[4,128,768]{2,1,0:T(8,128)(2,1)}, bf16[4,128,768]{2,1,0:T(8,128)(2,1)}, f32[48,8192]{1,0:T(8,128)}, bf16[4,48,768]{2,1,0:T(8,128)(2...) custom-call(bf16[2,4,128,768]{3,2,1,0:T(8,128)(2,1)} %collective-permute-done.2.refs_0_, ...), custom_call_target="tpu_custom_call" | custom-call | tf_op jit(solution)/shard_map/backward_attention/pallas_call | solution.py:1237
  583.0 1.2 slice_bitcast_fusion
  586.1 98.6 %last_gradients.1 = (f32[48,4608]{1,0:T(8,128)}, f32[48,128]{1,0:T(8,128)}, bf16[384,1536]{1,0:T(8,128)(2,1)}, f32[1,1536]{1,0:T(1,128)}, f32[1,1536]{1,0:T(1,12...) custom-call(bf16[384,4608]{1,0:T(8,128)(2,1)} %get-tuple-element.121.refs_0_, ...), custom_call_target="tpu_custom_call" | custom-call | tf_op jit(solution)/shard_map/last_gradients/pallas_call | solution.py:1062
  684.7 1.4 reduce.1
  686.1 1.4 copy.60
  687.5 1.2 slice_bitcast_fusion.1
  688.7 1.3 reduce.2
  690.0 2.4 copy.67
  692.4 0.9 copy.68
  694.1 1.1 copy.70
  695.8 0.9 copy.71
  (89 shorter events, 13.0 us)
Async XLA Ops:
  0.6 3.2 copy-start.9
  0.7 94.3 %collective-permute-start = (bf16[384,1536]{1,0:T(8,128)(2,1)}, bf16[384,1536]{1,0:T(8,128)(2,1)}, u32[]{:S(2)}, u32[]{:S(2)}) collective-permute-start(bf16[384,1536]{1,0:T(8,128)(2,1)} %refs_8_.3), channel_id=1, source_target_pairs={{0,4},{4,0},{8,12},{12,8},{16,20},{20,16},{24,28},{28,24},{1,5},{5... | collective-permute-start | bytes 3538952 | tf_op jit(solution)/shard_map/ppermute | solution.py:33
  3.8 74.1 %copy-start.21 = (f32[24]{0:T(128)S(1)}, f32[24]{0:T(128)}, u32[]{:S(2)}) copy-start(f32[24]{0:T(128)} %param.18) | copy-start | bytes 292
  4.9 74.7 %copy-start.11 = (bf16[384,1536]{1,0:T(8,128)(2,1)}, bf16[384,1536]{1,0:T(8,128)(2,1)S(1)}, u32[]{:S(2)}) copy-start(bf16[384,1536]{1,0:T(8,128)(2,1)S(1)} %fusion.2.act_ref) | copy-start | bytes 3538948
  4.9 74.7 %copy-start.20 = (s32[1,2,4]{2,1,0:T(2,128)S(1)}, s32[1,2,4]{2,1,0:T(2,128)}, u32[]{:S(2)}) copy-start(s32[1,2,4]{2,1,0:T(2,128)} %param.14) | copy-start | bytes 100
  80.5 1.9 copy-start.18
  83.2 11.7 %copy-start = (bf16[3,384,384]{2,1,0:T(8,128)(2,1)}, bf16[3,384,384]{2,1,0:T(8,128)(2,1)S(1)}, u32[]{:S(2)}) copy-start(bf16[3,384,384]{2,1,0:T(8,128)(2,1)S(1)} %fusion.3.refs_7_.refs_17_) | copy-start | bytes 2654212
  83.2 11.7 %copy-start.1 = (bf16[4,128,1536]{2,1,0:T(8,128)(2,1)S(1)}, bf16[4,128,1536]{2,1,0:T(8,128)(2,1)}, u32[]{:S(2)}) copy-start(bf16[4,128,1536]{2,1,0:T(8,128)(2,1)} %get-tuple-element.75.refs_2_) | copy-start | bytes 4718596
  83.2 11.7 %copy-start.2 = (bf16[48,8192]{1,0:T(8,128)(2,1)S(1)}, bf16[48,8192]{1,0:T(8,128)(2,1)}, u32[]{:S(2)}) copy-start(bf16[48,8192]{1,0:T(8,128)(2,1)} %refs_1_.1) | copy-start | bytes 2359300
  83.2 11.7 %copy-start.6 = (s32[1,4]{1,0:T(1,128)S(1)}, s32[1,4]{1,0:T(1,128)}, u32[]{:S(2)}) copy-start(s32[1,4]{1,0:T(1,128)} %param.13) | copy-start | bytes 52
  94.9 1.1 copy-start.4
  291.3 0.9 copy-start.3
  292.2 0.6 copy-start.5
  292.8 1.0 copy-start.7
  293.8 58.8 %copy-start.17 = (f32[1536]{0:T(1024)S(1)}, f32[1536]{0:T(1024)}, u32[]{:S(2)}) copy-start(f32[1536]{0:T(1024)} %param.15) | copy-start | bytes 18436
  343.4 5.9 collective-permute-start.1
  349.3 3.9 copy-start.8
  349.3 31.1 %collective-permute-start.5 = (bf16[384,4096]{1,0:T(8,128)(2,1)}, bf16[384,4096]{1,0:T(8,128)(2,1)}, u32[]{:S(2)}, u32[]{:S(2)}) collective-permute-start(bf16[384,4096]{1,0:T(8,128)(2,1)} %get-tuple-element.101.refs_8_), channel_id=1, source_target_pairs={{0,4},{4,0},{8,12},{12,8},{16,20},{20,16},{24,28},{28,24},{1,5},{5... | collective-permute-start | bytes 9437192 | tf_op jit(solution)/shard_map/ppermute | solution.py:33
  349.5 40.7 %collective-permute-start.6 = (bf16[384,4096]{1,0:T(8,128)(2,1)}, bf16[384,4096]{1,0:T(8,128)(2,1)}, u32[]{:S(2)}, u32[]{:S(2)}) collective-permute-start(bf16[384,4096]{1,0:T(8,128)(2,1)} %get-tuple-element.104.refs_8_), channel_id=1, source_target_pairs={{0,4},{4,0},{8,12},{12,8},{16,20},{20,16},{24,28},{28,24},{1,5},{5... | collective-permute-start | bytes 9437192 | tf_op jit(solution)/shard_map/ppermute | solution.py:33
  349.8 18.3 %collective-permute-start.7 = (bf16[8,192,384]{2,1,0:T(8,128)(2,1)}, bf16[8,192,384]{2,1,0:T(8,128)(2,1)}, u32[]{:S(2)}, u32[]{:S(2)}) collective-permute-start(bf16[8,192,384]{2,1,0:T(8,128)(2,1)} %bitcast.52), channel_id=1, source_target_pairs={{0,4},{4,0},{8,12},{12,8},{16,20},{20,16},{24,28},{28,24},{1,5},{5... | collective-permute-start | bytes 3538952 | tf_op jit(solution)/shard_map/ppermute | solution.py:33
  350.0 19.7 %collective-permute-start.8 = (bf16[384,1536]{1,0:T(8,128)(2,1)}, bf16[384,1536]{1,0:T(8,128)(2,1)}, u32[]{:S(2)}, u32[]{:S(2)}) collective-permute-start(bf16[384,1536]{1,0:T(8,128)(2,1)} %get-tuple-element.108.refs_8_), channel_id=1, source_target_pairs={{0,4},{4,0},{8,12},{12,8},{16,20},{20,16},{24,28},{28,24},{1,5},{5... | collective-permute-start | bytes 3538952 | tf_op jit(solution)/shard_map/ppermute | solution.py:33
  351.0 29.4 %collective-permute-start.4 = (bf16[8,192,384]{2,1,0:T(8,128)(2,1)}, bf16[8,192,384]{2,1,0:T(8,128)(2,1)}, u32[]{:S(2)}, u32[]{:S(2)}) collective-permute-start(bf16[8,192,384]{2,1,0:T(8,128)(2,1)} %bitcast.84), channel_id=1, source_target_pairs={{0,4},{4,0},{8,12},{12,8},{16,20},{20,16},{24,28},{28,24},{1,5},{5... | collective-permute-start | bytes 3538952 | tf_op jit(solution)/shard_map/ppermute | solution.py:33
  360.5 9.7 %copy-start.10 = (bf16[384,1536]{1,0:T(8,128)(2,1)S(1)}, bf16[384,1536]{1,0:T(8,128)(2,1)}, u32[]{:S(2)}) copy-start(bf16[384,1536]{1,0:T(8,128)(2,1)} %refs_6_.1) | copy-start | bytes 3538948
  368.1 37.0 %collective-permute-start.2 = (bf16[2,4,128,768]{3,2,1,0:T(8,128)(2,1)}, bf16[2,4,128,768]{3,2,1,0:T(8,128)(2,1)}, u32[]{:S(2)}, u32[]{:S(2)}) collective-permute-start(bf16[2,4,128,768]{3,2,1,0:T(8,128)(2,1)} %bitcast.14), channel_id=1, source_target_pairs={{0,16},{4,20},{8,24},{12,28},{16,0},{20,4},{24,8},{28,12},{1,17},{... | collective-permute-start | bytes 4718600 | tf_op jit(solution)/shard_map/ppermute | solution.py:33
  369.7 36.7 %collective-permute-start.3 = (bf16[2,4,128,768]{3,2,1,0:T(8,128)(2,1)}, bf16[2,4,128,768]{3,2,1,0:T(8,128)(2,1)}, u32[]{:S(2)}, u32[]{:S(2)}) collective-permute-start(bf16[2,4,128,768]{3,2,1,0:T(8,128)(2,1)} %bitcast.83), channel_id=1, source_target_pairs={{0,8},{4,12},{8,0},{12,4},{16,24},{20,28},{24,16},{28,20},{1,9},{5... | collective-permute-start | bytes 4718600 | tf_op jit(solution)/shard_map/ppermute | solution.py:33
  370.5 1.0 copy-start.19
  371.5 8.9 %copy-start.12 = (bf16[1536,384]{1,0:T(8,128)(2,1)}, bf16[1536,384]{1,0:T(8,128)(2,1)S(1)}, u32[]{:S(2)}) copy-start(bf16[1536,384]{1,0:T(8,128)(2,1)S(1)} %copy.58) | copy-start | bytes 3538948
  380.4 205.7 %collective-permute-start.9 = (bf16[8,192,384]{2,1,0:T(8,128)(2,1)S(1)}, bf16[8,192,384]{2,1,0:T(8,128)(2,1)}, u32[]{:S(2)}, u32[]{:S(2)}) collective-permute-start(bf16[8,192,384]{2,1,0:T(8,128)(2,1)S(1)} %bitcast.63), channel_id=1, source_target_pairs={{0,4},{4,0},{8,12},{12,8},{16,20},{20,16},{24,28},{28,24},{1,5},{5... | collective-permute-start | bytes 3538952 | tf_op jit(solution)/shard_map/ppermute | solution.py:33
  684.7 7.7 %copy-start.14 = (f32[48,4608]{1,0:T(8,128)S(1)}, f32[48,4608]{1,0:T(8,128)}, u32[]{:S(2)}) copy-start(f32[48,4608]{1,0:T(8,128)} %get-tuple-element.191) | copy-start | bytes 2654212
  690.0 3.3 copy-start.16
  692.4 1.7 copy-start.13
  694.1 1.7 copy-start.15
